TPU v7x, 32 devices: a whole 2x2x4 slice. The times are simulated.
32 devices in a mesh: gx: 2 (over x), gy: 4 (over y, core), gz: 4 (over z).
Axes of the slice: x: 2, y: 2, z: 4, core: 2. Of those that a mesh axis runs over, the one named last changes fastest.
Arguments:
- volume: float32 [32, 32, 1024], P('gz', 'gx', 'gy'), may hold values from -10 to 10
Outputs:
- diffused: float32 [32, 32, 1024], P('gz', 'gx', 'gy')
All inputs are finite; a program needn't handle non-finite values.
Results may differ from a plain program's by a relative error of at most 0.0003.
Values sent between devices are 32-bit elements; how exact they have to be, the bound alone decides.
No kernel may reach another device: no remote copies, remote signals or barrier semaphores. Data moves between devices by JAX's collectives and lax.ppermute only.
A program may use at most 64 MiB of HBM per device.

v0:
```python
import jax
import jax.numpy as jnp
from jax import lax
from jax.sharding import PartitionSpec as P

kernel_taps = (0.41111229, 0.8007374, 1.0, 0.8007374, 0.41111229)
time_step = 3000.0
contrast = 0.1


def extended(shard, sides, width):
    for axis, dim in sides:
        peers, length = (lax.axis_size(axis), shard.shape[dim])
        up = [(i, (i + 1) % peers) for i in range(peers - 1)]
        down = [(j, i) for i, j in up]
        last = lax.slice_in_dim(shard, length - width, length, axis=dim)
        leading = lax.slice_in_dim(shard, 0, width, axis=dim)
        before = lax.ppermute(last, axis, up)
        after = lax.ppermute(leading, axis, down)
        shard = jnp.concatenate([before, shard, after], axis=dim)
    return shard


def blur_valid(values, first_dim):
    weight_sum = sum(kernel_taps)
    for axis_dim in range(first_dim, first_dim + 3):
        out_size = values.shape[axis_dim] - 4
        blurred = kernel_taps[0] / weight_sum * lax.slice_in_dim(values, 0, out_size, axis=axis_dim)
        for offset in range(1, 5):
            blurred = blurred + kernel_taps[offset] / weight_sum * lax.slice_in_dim(
                values, offset, offset + out_size, axis=axis_dim
            )
        values = blurred
    return values


def gradients(values, first_dim):
    result = []
    for axis_dim in range(first_dim, first_dim + 3):
        cropped = values
        for other_dim in range(first_dim, first_dim + 3):
            if other_dim != axis_dim:
                cropped = lax.slice_in_dim(cropped, 1, cropped.shape[other_dim] - 1, axis=other_dim)
        length = cropped.shape[axis_dim] - 2
        forward = lax.slice_in_dim(cropped, 2, length + 2, axis=axis_dim)
        behind = lax.slice_in_dim(cropped, 0, length, axis=axis_dim)
        result.append((forward - behind) * 0.5)
    return result


def shifted(values, stride, axis_dim, fill_value):
    length = values.shape[axis_dim]
    if abs(stride) >= length:
        return jnp.full(values.shape, fill_value, values.dtype)
    pad_shape = list(values.shape)
    pad_shape[axis_dim] = abs(stride)
    padding = jnp.full(tuple(pad_shape), fill_value, values.dtype)
    if stride > 0:
        return jnp.concatenate(
            [padding, lax.slice_in_dim(values, 0, length - stride, axis=axis_dim)], axis=axis_dim
        )
    return jnp.concatenate(
        [lax.slice_in_dim(values, -stride, length, axis=axis_dim), padding], axis=axis_dim
    )


def every_other(values, first_row, axis_dim):
    return lax.slice_in_dim(values, first_row, values.shape[axis_dim], stride=2, axis=axis_dim)


def reduce_solve(sub_diag, main_diag, super_diag, right_sides, axis_dim):
    length = main_diag.shape[axis_dim]
    if length == 1:
        return [right_side / main_diag for right_side in right_sides]
    even_sub = every_other(sub_diag, 0, axis_dim)
    odd_sub = every_other(sub_diag, 1, axis_dim)
    even_main = every_other(main_diag, 0, axis_dim)
    odd_main = every_other(main_diag, 1, axis_dim)
    even_super = every_other(super_diag, 0, axis_dim)
    odd_super = every_other(super_diag, 1, axis_dim)
    even_sides = [every_other(right_side, 0, axis_dim) for right_side in right_sides]
    odd_sides = [every_other(right_side, 1, axis_dim) for right_side in right_sides]
    lower_factor = -even_sub / shifted(odd_main, 1, axis_dim, 1.0)
    upper_factor = -even_super / odd_main
    reduced = reduce_solve(
        lower_factor * shifted(odd_sub, 1, axis_dim, 0.0),
        even_main + lower_factor * shifted(odd_super, 1, axis_dim, 0.0) + upper_factor * odd_sub,
        upper_factor * odd_super,
        [
            even_side + lower_factor * shifted(odd_side, 1, axis_dim, 0.0) + upper_factor * odd_side
            for even_side, odd_side in zip(even_sides, odd_sides)
        ],
        axis_dim,
    )
    result = []
    for even_part, odd_side in zip(reduced, odd_sides):
        odd_part = (
            odd_side - odd_sub * even_part - odd_super * shifted(even_part, -1, axis_dim, 0.0)
        ) / odd_main
        joined = jnp.stack([even_part, odd_part], axis=axis_dim + 1)
        joined_shape = list(even_part.shape)
        joined_shape[axis_dim] = 2 * joined_shape[axis_dim]
        result.append(joined.reshape(tuple(joined_shape)))
    return result


def inside_volume(squares, rim, positions, counts):
    full_shape = squares[0].shape
    inside_mask = None
    for axis_dim in range(3):
        length = full_shape[axis_dim] - 2 * rim
        global_index = (
            positions[axis_dim] * length
            + lax.broadcasted_iota(jnp.int32, full_shape, axis_dim)
            - rim
        )
        within = (global_index >= 0) & (global_index < length * counts[axis_dim])
        inside_mask = within if inside_mask is None else inside_mask & within
    return [jnp.where(inside_mask, square, 0.0) for square in squares]


def face_pairs(diffusivity, axis_dim, position, device_count):
    cropped = diffusivity
    for other_dim in range(3):
        if other_dim != axis_dim:
            cropped = lax.slice_in_dim(cropped, 1, cropped.shape[other_dim] - 1, axis=other_dim)
    length = cropped.shape[axis_dim] - 2
    centre = lax.slice_in_dim(cropped, 1, length + 1, axis=axis_dim)
    following = lax.slice_in_dim(cropped, 2, length + 2, axis=axis_dim)
    before = lax.slice_in_dim(cropped, 0, length, axis=axis_dim)
    face_up = (centre + following) * 0.5
    face_down = (before + centre) * 0.5
    global_index = position * length + lax.broadcasted_iota(jnp.int32, face_up.shape, axis_dim)
    face_up = jnp.where(global_index < length * device_count - 1, face_up, 0.0)
    face_down = jnp.where(global_index > 0, face_down, 0.0)
    return (face_up, face_down)


def line_solve(values, face_up, axis_dim, stiffness):
    face_down = shifted(face_up, 1, axis_dim, 0.0)
    return reduce_solve(
        -stiffness * face_down,
        1.0 + stiffness * (face_down + face_up),
        -stiffness * face_up,
        [values],
        axis_dim,
    )[0]


def body(volume):
    stiffness = 3.0 * time_step
    positions = (lax.axis_index("gz"), lax.axis_index("gx"), lax.axis_index("gy"))
    counts = (lax.axis_size("gz"), lax.axis_size("gx"), lax.axis_size("gy"))
    widened = extended(volume, (("gx", 1), ("gy", 2), ("gz", 0)), 6)
    blurred = blur_valid(widened, 0)
    squares = inside_volume(
        [slope * slope for slope in gradients(blurred, 0)], 3, positions, counts
    )
    tensor = blur_valid(jnp.stack(squares), 1)
    diffusivity = 1.0 / (1.0 + tensor / (contrast * contrast))
    up_z, down_z = face_pairs(diffusivity[0], 0, positions[0], counts[0])
    up_x, down_x = face_pairs(diffusivity[1], 1, positions[1], counts[1])
    up_y, down_y = face_pairs(diffusivity[2], 2, positions[2], counts[2])
    lines_x = (lambda pieces: line_solve(pieces[0], pieces[1], 1, stiffness))(
        (
            lax.all_to_all(volume, "gx", split_axis=0, concat_axis=1, tiled=True),
            lax.all_to_all(up_x, "gx", split_axis=0, concat_axis=1, tiled=True),
        )
    )
    solved_x = lax.all_to_all(lines_x, "gx", split_axis=1, concat_axis=0, tiled=True)
    lines_y = (lambda pieces: line_solve(pieces[0], pieces[1], 2, stiffness))(
        (
            lax.all_to_all(volume, "gy", split_axis=0, concat_axis=2, tiled=True),
            lax.all_to_all(up_y, "gy", split_axis=0, concat_axis=2, tiled=True),
        )
    )
    solved_y = lax.all_to_all(lines_y, "gy", split_axis=2, concat_axis=0, tiled=True)
    lines_z = (lambda pieces: line_solve(pieces[0], pieces[1], 0, stiffness))(
        (
            lax.all_to_all(volume, "gz", split_axis=1, concat_axis=0, tiled=True),
            lax.all_to_all(up_z, "gz", split_axis=1, concat_axis=0, tiled=True),
        )
    )
    solved_z = lax.all_to_all(lines_z, "gz", split_axis=0, concat_axis=1, tiled=True)
    summed = solved_x + solved_y + solved_z
    return summed / 3.0


def solution(mesh):
    return jax.shard_map(
        body,
        mesh=mesh,
        in_specs=(P("gz", "gx", "gy"),),
        out_specs=P("gz", "gx", "gy"),
        check_vma=False,
    )
```

profile of v0, /device:TPU:0, one launch (start us, length us, event | category | flops | bytes accessed | tf_op | source)
XLA Modules:
  0.0 231.3 jit_solution(13661686531999886231)
XLA Ops:
  0.0 4.2 %all-to-all-start = ((f32[8,16,256]{2,1,0:T(8,128)}), f32[8,16,256]{2,1,0:T(8,128)S(1)}, u32[]{:S(2)}, u32[]{:S(2)}) async-start(f32[8,16,256]{2,1,0:T(8,128)} %param.1), calls=%async_computation | async-start | bytes 262144 | tf_op jit(solution)/shard_map/all_to_all | solution.py:166
  5.1 4.1 %collective-permute-start = (f32[8,6,256]{2,1,0:T(8,128)S(1)}, f32[8,6,256]{2,1,0:T(8,128)S(1)}, u32[]{:S(2)}, u32[]{:S(2)}) collective-permute-start(f32[8,6,256]{2,1,0:T(8,128)S(1)} %get-tuple-element.65), channel_id=1, source_target_pairs={{0,16},{1,17},{2,18},{3,19},{4,20},{5,21},{6,22},{7,23},{8,24},{9,... | collective-permute-start | bytes 147464 | tf_op jit(solution)/shard_map/ppermute | solution.py:18
  11.1 4.3 %collective-permute-done.1 = f32[8,6,256]{2,1,0:T(8,128)S(1)} collective-permute-done((f32[8,6,256]{2,1,0:T(8,128)S(1)}, f32[8,6,256]{2,1,0:T(8,128)S(1)}, u32[]{:S(2)}, u32[]{:S(2)}) %collective-permute-start.1) | collective-permute-done | bytes 49184 | tf_op jit(solution)/shard_map/ppermute | solution.py:19
  19.0 1.6 copy.257
  20.6 2.5 %collective-permute-done.3 = f32[8,28,6]{2,1,0:T(8,128)S(1)} collective-permute-done((f32[8,28,6]{2,1,0:T(8,128)S(1)}, f32[8,28,6]{2,1,0:T(8,128)S(1)}, u32[]{:S(2)}, u32[]{:S(2)}) %collective-permute-start.3) | collective-permute-done | bytes 5408 | tf_op jit(solution)/shard_map/ppermute | solution.py:19
  24.3 4.8 %all-to-all-start.3 = ((f32[8,16,256]{2,1,0:T(8,128)}), f32[8,16,256]{2,1,0:T(8,128)S(1)}, u32[]{:S(2)}, u32[]{:S(2)}) async-start(f32[8,16,256]{2,1,0:T(8,128)} %param.1), calls=%async_computation.3 | async-start | bytes 262144 | tf_op jit(solution)/shard_map/all_to_all | solution.py:173
  29.2 3.5 %collective-permute-start.4 = (f32[6,28,268]{2,1,0:T(8,128)S(1)}, f32[6,28,268]{2,1,0:T(8,128)S(1)}, u32[]{:S(2)}, u32[]{:S(2)}) collective-permute-start(f32[6,28,268]{2,1,0:T(8,128)S(1)} %get-tuple-element.35), channel_id=1, source_target_pairs={{0,1},{1,2},{2,3},{4,5},{5,6},{6,7},{8,9},{9,10},{10,11},{12,13},{... | collective-permute-start | bytes 540296 | tf_op jit(solution)/shard_map/ppermute | solution.py:18
  34.0 5.9 %all-to-all-start.6 = ((f32[8,16,256]{2,0,1:T(8,128)}), f32[8,16,256]{2,0,1:T(8,128)S(1)}, u32[]{:S(2)}, u32[]{:S(2)}) async-start(f32[8,16,256]{2,0,1:T(8,128)} %copy.257), calls=%async_computation.6 | async-start | bytes 262144 | tf_op jit(solution)/shard_map/all_to_all | solution.py:180
  41.2 2.2 slice.1063
  43.4 3.1 %all-to-all-done.6 = f32[8,16,256]{2,0,1:T(8,128)S(1)} async-done(((f32[8,16,256]{2,0,1:T(8,128)}), f32[8,16,256]{2,0,1:T(8,128)S(1)}, u32[]{:S(2)}, u32[]{:S(2)}) %all-to-all-start.6) | async-done | bytes 131104 | tf_op jit(solution)/shard_map/all_to_all | solution.py:180
  54.1 3.4 %all-to-all-start.1 = ((f32[8,16,256]{2,1,0:T(8,128)}), f32[8,16,256]{2,1,0:T(8,128)S(1)}, u32[]{:S(2)}, u32[]{:S(2)}) async-start(f32[8,16,256]{2,1,0:T(8,128)} %fusion.44), calls=%async_computation.1 | async-start | bytes 262144 | tf_op jit(solution)/shard_map/all_to_all | solution.py:167
  59.1 3.1 %all-to-all-done.1 = f32[8,16,256]{2,1,0:T(8,128)S(1)} async-done(((f32[8,16,256]{2,1,0:T(8,128)}), f32[8,16,256]{2,1,0:T(8,128)S(1)}, u32[]{:S(2)}, u32[]{:S(2)}) %all-to-all-start.1) | async-done | bytes 131104 | tf_op jit(solution)/shard_map/all_to_all | solution.py:167
  62.3 3.3 %all-to-all-start.4 = ((f32[8,16,256]{2,1,0:T(8,128)}), f32[8,16,256]{2,1,0:T(8,128)S(1)}, u32[]{:S(2)}, u32[]{:S(2)}) async-start(f32[8,16,256]{2,1,0:T(8,128)} %fusion.42), calls=%async_computation.4 | async-start | bytes 262144 | tf_op jit(solution)/shard_map/all_to_all | solution.py:174
  68.1 2.0 all-to-all-done.4
  70.2 4.1 %all-to-all-start.7 = ((f32[8,16,256]{2,0,1:T(8,128)}), f32[8,16,256]{2,0,1:T(8,128)}, u32[]{:S(2)}, u32[]{:S(2)}) async-start(f32[8,16,256]{2,0,1:T(8,128)} %copy.259), calls=%async_computation.7 | async-start | bytes 262144 | tf_op jit(solution)/shard_map/all_to_all | solution.py:181
  74.7 1.6 pad_multiply_fusion
  76.3 3.1 %slice.1076 = f32[2,16,512]{1,2,0:T(8,128)S(1)} slice(f32[2,16,1024]{1,2,0:T(8,128)} %get-tuple-element.25), slice={[0:2:1], [0:16:1], [1:1024:2]} | slice | bytes 131072 | tf_op jit(solution)/shard_map/slice | solution.py:68
  79.4 2.2 slice.1069
  81.6 3.0 %slice.1070 = f32[2,16,512]{1,2,0:T(8,128)S(1)} slice(f32[2,16,1024]{1,2,0:T(8,128)} %get-tuple-element.26), slice={[0:2:1], [0:16:1], [1:1024:2]} | slice | bytes 131072 | tf_op jit(solution)/shard_map/slice | solution.py:68
  84.6 4.1 %slice.1079 = f32[2,16,512]{1,2,0:T(8,128)} slice(f32[2,16,1024]{1,2,0:T(8,128)} %get-tuple-element.26), slice={[0:2:1], [0:16:1], [0:1024:2]} | slice | bytes 131072 | tf_op jit(solution)/shard_map/slice | solution.py:68
  89.4 2.2 slice.1074
  91.6 3.0 %multiply_add_fusion.2 = (f32[2,16,512]{1,2,0:T(8,128)S(1)}, f32[2,16,512]{1,2,0:T(8,128)}, f32[2,16,512]{1,2,0:T(8,128)S(1)}, f32[2,16,512]{1,2,0:T(8,128)}) fusion(f32[2,16,512]{1,2,0:T(8,128)S(1)} %slice.1072, f32[2,16,512]{1,2,0:T(8,128)} %slice.1063, f32[2,16,511]{1,2,0:T(8,128)S(1)} %bitcast.238, f32[2,16,512]{1,2,0:T(8,128)S(1)} %slice.1070, ...), kind=kLoop, calls=%fused_computation.66 | loop fusion | flops 229376 | bytes 1048064 | tf_op jit(solution)/shard_map/add | solution.py:90
  96.6 1.7 slice.1091
  100.3 1.7 slice.1086
  102.1 2.2 multiply_add_fusion.4
  105.3 1.6 slice.1087
  107.9 1.6 slice.1103
  110.4 1.6 slice.1090
  112.0 1.6 slice.1104
  113.7 1.6 slice.1098
  115.3 2.1 multiply_add_fusion.7
  117.4 1.5 slice.1108
  118.9 1.5 slice.1099
  120.4 1.5 slice.1106
  122.0 1.5 slice.1115
  123.5 1.5 slice.1112
  125.0 1.5 slice.1102
  126.6 1.5 slice.1116
  128.1 1.5 slice.1110
  129.6 1.9 multiply_add_fusion.12
  131.6 1.4 slice.1120
  133.0 1.5 slice.1111
  134.5 1.5 slice.1118
  135.9 1.5 slice.1127
  137.4 1.5 slice.1124
  138.8 1.5 slice.1114
  140.3 1.4 slice.1128
  141.7 1.4 slice.1122
  143.2 1.7 multiply_add_fusion.18
  148.3 1.4 slice.1139
  149.7 1.4 slice.1136
  151.1 1.4 slice.1126
  152.4 1.4 slice.1140
  153.8 1.4 slice.1134
  155.1 1.5 multiply_add_fusion.24
  167.1 1.5 multiply_add_fusion.30
  179.0 1.4 multiply_add_fusion.34
  201.8 2.1 reshape.84
  203.9 3.5 %all-to-all-start.2 = ((f32[4,32,256]{2,0,1:T(4,128)}), f32[4,32,256]{2,0,1:T(4,128)S(1)}, u32[]{:S(2)}, u32[]{:S(2)}) async-start(f32[4,32,256]{2,0,1:T(4,128)} %bitcast.23), calls=%async_computation.2 | async-start | bytes 262144 | tf_op jit(solution)/shard_map/all_to_all | solution.py:170
  211.9 3.3 %all-to-all-start.5 = ((f32[4,1,8192]{2,1,0:T(1,128)}), f32[4,1,8192]{2,1,0:T(1,128)S(1)}, u32[]{:S(2)}, u32[]{:S(2)}) async-start(f32[4,1,8192]{2,1,0:T(1,128)} %reshape.84), calls=%async_computation.5 | async-start | bytes 262144 | tf_op jit(solution)/shard_map/all_to_all | solution.py:177
  215.9 3.8 %all-to-all-done.5 = f32[4,1,8192]{2,1,0:T(1,128)S(1)} async-done(((f32[4,1,8192]{2,1,0:T(1,128)}), f32[4,1,8192]{2,1,0:T(1,128)S(1)}, u32[]{:S(2)}, u32[]{:S(2)}) %all-to-all-start.5) | async-done | bytes 131104 | tf_op jit(solution)/shard_map/all_to_all | solution.py:177
  219.8 4.9 %all-to-all-start.8 = ((f32[32,4,256]{2,1,0:T(4,128)}), f32[32,4,256]{2,1,0:T(4,128)S(1)}, u32[]{:S(2)}, u32[]{:S(2)}) async-start(f32[32,4,256]{2,1,0:T(4,128)} %bitcast.89), calls=%async_computation.8 | async-start | bytes 262144 | tf_op jit(solution)/shard_map/all_to_all | solution.py:184
  226.2 1.4 reshape.85
  228.1 2.5 %all-to-all-done.8 = f32[32,4,256]{2,1,0:T(4,128)S(1)} async-done(((f32[32,4,256]{2,1,0:T(4,128)}), f32[32,4,256]{2,1,0:T(4,128)S(1)}, u32[]{:S(2)}, u32[]{:S(2)}) %all-to-all-start.8) | async-done | bytes 131104 | tf_op jit(solution)/shard_map/all_to_all | solution.py:184
  (292 shorter events, 82.4 us)
Async XLA Ops:
  0.0 24.3 %all-to-all-start = ((f32[8,16,256]{2,1,0:T(8,128)}), f32[8,16,256]{2,1,0:T(8,128)S(1)}, u32[]{:S(2)}, u32[]{:S(2)}) async-start(f32[8,16,256]{2,1,0:T(8,128)} %param.1), calls=%async_computation | async-start | bytes 262144 | tf_op jit(solution)/shard_map/all_to_all | solution.py:166
  5.1 5.9 %collective-permute-start = (f32[8,6,256]{2,1,0:T(8,128)S(1)}, f32[8,6,256]{2,1,0:T(8,128)S(1)}, u32[]{:S(2)}, u32[]{:S(2)}) collective-permute-start(f32[8,6,256]{2,1,0:T(8,128)S(1)} %get-tuple-element.65), channel_id=1, source_target_pairs={{0,16},{1,17},{2,18},{3,19},{4,20},{5,21},{6,22},{7,23},{8,24},{9,... | collective-permute-start | bytes 147464 | tf_op jit(solution)/shard_map/ppermute | solution.py:18
  9.2 6.2 %collective-permute-start.1 = (f32[8,6,256]{2,1,0:T(8,128)S(1)}, f32[8,6,256]{2,1,0:T(8,128)S(1)}, u32[]{:S(2)}, u32[]{:S(2)}) collective-permute-start(f32[8,6,256]{2,1,0:T(8,128)S(1)} %get-tuple-element.66), channel_id=1, source_target_pairs={{16,0},{17,1},{18,2},{19,3},{20,4},{21,5},{22,6},{23,7},{24,8},{25... | collective-permute-start | bytes 147464 | tf_op jit(solution)/shard_map/ppermute | solution.py:19
  16.4 4.3 %collective-permute-start.2 = (f32[8,28,6]{2,1,0:T(8,128)S(1)}, f32[8,28,6]{2,1,0:T(8,128)S(1)}, u32[]{:S(2)}, u32[]{:S(2)}) collective-permute-start(f32[8,28,6]{2,1,0:T(8,128)S(1)} %get-tuple-element.45), channel_id=1, source_target_pairs={{0,4},{4,8},{8,12},{1,5},{5,9},{9,13},{2,6},{6,10},{10,14},{3,7},{... | collective-permute-start | bytes 16136 | tf_op jit(solution)/shard_map/ppermute | solution.py:18
  17.7 5.5 %collective-permute-start.3 = (f32[8,28,6]{2,1,0:T(8,128)S(1)}, f32[8,28,6]{2,1,0:T(8,128)S(1)}, u32[]{:S(2)}, u32[]{:S(2)}) collective-permute-start(f32[8,28,6]{2,1,0:T(8,128)S(1)} %get-tuple-element.46), channel_id=1, source_target_pairs={{4,0},{8,4},{12,8},{5,1},{9,5},{13,9},{6,2},{10,6},{14,10},{7,3},{... | collective-permute-start | bytes 16136 | tf_op jit(solution)/shard_map/ppermute | solution.py:19
  24.3 9.7 %all-to-all-start.3 = ((f32[8,16,256]{2,1,0:T(8,128)}), f32[8,16,256]{2,1,0:T(8,128)S(1)}, u32[]{:S(2)}, u32[]{:S(2)}) async-start(f32[8,16,256]{2,1,0:T(8,128)} %param.1), calls=%async_computation.3 | async-start | bytes 262144 | tf_op jit(solution)/shard_map/all_to_all | solution.py:173
  29.2 18.5 %collective-permute-start.4 = (f32[6,28,268]{2,1,0:T(8,128)S(1)}, f32[6,28,268]{2,1,0:T(8,128)S(1)}, u32[]{:S(2)}, u32[]{:S(2)}) collective-permute-start(f32[6,28,268]{2,1,0:T(8,128)S(1)} %get-tuple-element.35), channel_id=1, source_target_pairs={{0,1},{1,2},{2,3},{4,5},{5,6},{6,7},{8,9},{9,10},{10,11},{12,13},{... | collective-permute-start | bytes 540296 | tf_op jit(solution)/shard_map/ppermute | solution.py:18
  32.7 15.0 %collective-permute-start.5 = (f32[6,28,268]{2,1,0:T(8,128)S(1)}, f32[6,28,268]{2,1,0:T(8,128)S(1)}, u32[]{:S(2)}, u32[]{:S(2)}) collective-permute-start(f32[6,28,268]{2,1,0:T(8,128)S(1)} %get-tuple-element.36), channel_id=1, source_target_pairs={{1,0},{2,1},{3,2},{5,4},{6,5},{7,6},{9,8},{10,9},{11,10},{13,12},{... | collective-permute-start | bytes 540296 | tf_op jit(solution)/shard_map/ppermute | solution.py:19
  34.0 12.4 %all-to-all-start.6 = ((f32[8,16,256]{2,0,1:T(8,128)}), f32[8,16,256]{2,0,1:T(8,128)S(1)}, u32[]{:S(2)}, u32[]{:S(2)}) async-start(f32[8,16,256]{2,0,1:T(8,128)} %copy.257), calls=%async_computation.6 | async-start | bytes 262144 | tf_op jit(solution)/shard_map/all_to_all | solution.py:180
  54.1 8.2 %all-to-all-start.1 = ((f32[8,16,256]{2,1,0:T(8,128)}), f32[8,16,256]{2,1,0:T(8,128)S(1)}, u32[]{:S(2)}, u32[]{:S(2)}) async-start(f32[8,16,256]{2,1,0:T(8,128)} %fusion.44), calls=%async_computation.1 | async-start | bytes 262144 | tf_op jit(solution)/shard_map/all_to_all | solution.py:167
  62.3 7.9 %all-to-all-start.4 = ((f32[8,16,256]{2,1,0:T(8,128)}), f32[8,16,256]{2,1,0:T(8,128)S(1)}, u32[]{:S(2)}, u32[]{:S(2)}) async-start(f32[8,16,256]{2,1,0:T(8,128)} %fusion.42), calls=%async_computation.4 | async-start | bytes 262144 | tf_op jit(solution)/shard_map/all_to_all | solution.py:174
  70.2 133.7 %all-to-all-start.7 = ((f32[8,16,256]{2,0,1:T(8,128)}), f32[8,16,256]{2,0,1:T(8,128)}, u32[]{:S(2)}, u32[]{:S(2)}) async-start(f32[8,16,256]{2,0,1:T(8,128)} %copy.259), calls=%async_computation.7 | async-start | bytes 262144 | tf_op jit(solution)/shard_map/all_to_all | solution.py:181
  76.3 3.1 %copy-start = (f32[2,16,1024]{1,2,0:T(8,128)S(1)}, f32[2,16,1024]{1,2,0:T(8,128)}, u32[]{:S(2)}) copy-start(f32[2,16,1024]{1,2,0:T(8,128)} %get-tuple-element.25) | copy-start | bytes 393220
  99.2 2.8 %copy-start.7 = (f32[2,16,256]{1,2,0:T(8,128)S(1)}, f32[2,16,256]{1,2,0:T(8,128)}, u32[]{:S(2)}) copy-start(f32[2,16,256]{1,2,0:T(8,128)} %slice.1075) | copy-start | bytes 98308
  190.4 8.3 %copy-start.3 = (f32[2,16,64]{1,2,0:T(8,128)S(1)}, f32[2,16,64]{1,2,0:T(8,128)}, u32[]{:S(2)}) copy-start(f32[2,16,64]{1,2,0:T(8,128)} %slice.1108) | copy-start | bytes 24580
  190.4 8.3 %copy-start.4 = (f32[2,16,64]{1,2,0:T(8,128)S(1)}, f32[2,16,64]{1,2,0:T(8,128)}, u32[]{:S(2)}) copy-start(f32[2,16,64]{1,2,0:T(8,128)} %slice.1106) | copy-start | bytes 24580
  190.4 8.3 %copy-start.5 = (f32[2,16,64]{1,2,0:T(8,128)S(1)}, f32[2,16,64]{1,2,0:T(8,128)}, u32[]{:S(2)}) copy-start(f32[2,16,64]{1,2,0:T(8,128)} %slice.1112) | copy-start | bytes 24580
  190.5 8.3 %copy-start.6 = (f32[2,16,64]{1,2,0:T(8,128)S(1)}, f32[2,16,64]{1,2,0:T(8,128)}, u32[]{:S(2)}) copy-start(f32[2,16,64]{1,2,0:T(8,128)} %slice.1116) | copy-start | bytes 24580
  196.9 2.1 copy-start.1
  203.9 5.6 %copy-start.2 = (f32[16,4,256]{2,0,1:T(8,128)S(1)}, f32[16,4,256]{2,0,1:T(8,128)}, u32[]{:S(2)}) copy-start(f32[16,4,256]{2,0,1:T(8,128)} %slice.1201) | copy-start | bytes 196612
  203.9 5.6 %copy-start.8 = (f32[16,4,256]{2,0,1:T(8,128)S(1)}, f32[16,4,256]{2,0,1:T(8,128)}, u32[]{:S(2)}) copy-start(f32[16,4,256]{2,0,1:T(8,128)} %slice.1193) | copy-start | bytes 196612
  203.9 8.0 %all-to-all-start.2 = ((f32[4,32,256]{2,0,1:T(4,128)}), f32[4,32,256]{2,0,1:T(4,128)S(1)}, u32[]{:S(2)}, u32[]{:S(2)}) async-start(f32[4,32,256]{2,0,1:T(4,128)} %bitcast.23), calls=%async_computation.2 | async-start | bytes 262144 | tf_op jit(solution)/shard_map/all_to_all | solution.py:170
  211.9 7.9 %all-to-all-start.5 = ((f32[4,1,8192]{2,1,0:T(1,128)}), f32[4,1,8192]{2,1,0:T(1,128)S(1)}, u32[]{:S(2)}, u32[]{:S(2)}) async-start(f32[4,1,8192]{2,1,0:T(1,128)} %reshape.84), calls=%async_computation.5 | async-start | bytes 262144 | tf_op jit(solution)/shard_map/all_to_all | solution.py:177
  219.8 10.8 %all-to-all-start.8 = ((f32[32,4,256]{2,1,0:T(4,128)}), f32[32,4,256]{2,1,0:T(4,128)S(1)}, u32[]{:S(2)}, u32[]{:S(2)}) async-start(f32[32,4,256]{2,1,0:T(4,128)} %bitcast.89), calls=%async_computation.8 | async-start | bytes 262144 | tf_op jit(solution)/shard_map/all_to_all | solution.py:184
where the time goes:
time: 236 us; the launch traced here: 231 us
  local copies, waits for them, and re-layouts  121 us (51%)
  starting transfers between devices  50.3 us (21%)
  other arithmetic  35.5 us (15%)
  waiting for transfers between devices  22.7 us (10%)
    slice x136, local copies, waits for them, and re-layouts, every_other(): lax.slice_in_dim(values, first_row, values.shape[axis_dim], stride=2, axi...  104 us
    add x17, other arithmetic, reduce_solve(): even_side + lower_factor * shifted(odd_side, 1, axis_dim, 0.0)  16.4 us
    ppermute x3, starting transfers between devices, extended(): before = lax.ppermute(last, axis, up)  8.85 us
    ppermute x3, waiting for transfers between devices, extended(): after = lax.ppermute(leading, axis, down)  6.8 us
    all_to_all x1, starting transfers between devices, body(): lax.all_to_all(volume, 'gz', split_axis=1, concat_axis=0, tiled=True)  5.95 us
    unnamed x27, local copies, waits for them, and re-layouts  5.24 us
    all_to_all x1, starting transfers between devices, body(): lax.all_to_all(lines_z, 'gz', split_axis=0, concat_axis=1, tiled=True)  4.87 us
    all_to_all x1, starting transfers between devices, body(): lax.all_to_all(volume, 'gy', split_axis=0, concat_axis=2, tiled=True)  4.82 us
  transfers between devices with their start and end apart: 15, of which 9 were waited for; matrix products, arithmetic and copies ran while one was open for 65% of the time, Pallas kernels for 0%

commit v1 on v0

v1 whole, which is shorter than its diff:
```python
import functools

import jax
import jax.numpy as jnp
from jax import lax
from jax.experimental import pallas as pl
from jax.experimental.pallas import tpu as pltpu
from jax.sharding import PartitionSpec as P

kernel_taps = (0.41111229, 0.8007374, 1.0, 0.8007374, 0.41111229)
time_step = 3000.0
contrast = 0.1
stiffness = 3.0 * time_step
halo = 6
lanes = 128
edge = 8
VMEM = pl.BlockSpec(memory_space=pltpu.VMEM)


def taps(scale=1.0):
    total = sum(kernel_taps)
    return tuple(scale * tap / total for tap in kernel_taps[:3])


def five(k, a, b, c, d, e):
    return k[0] * (a + e) + k[1] * (b + d) + k[2] * c


def lane_shift(tiles, k, wanted):
    count = len(tiles)
    rolled = [pltpu.roll(t, (-k) % lanes, axis=1) for t in tiles]
    lane = lax.broadcasted_iota(jnp.int32, tiles[0].shape, 1)
    out = []
    for t in wanted:
        if k > 0:
            out.append(jnp.where(lane < lanes - k, rolled[t], rolled[(t + 1) % count]))
        else:
            out.append(jnp.where(lane >= -k, rolled[t], rolled[(t - 1) % count]))
    return out


def lane_blur(k, tiles, wanted):
    s = {o: lane_shift(tiles, o, wanted) for o in (-2, -1, 1, 2)}
    return [five(k, s[-2][i], s[-1][i], tiles[t], s[1][i], s[2][i]) for i, t in enumerate(wanted)]


def merge(low, high):
    a0, an, g00, g0n, gnn, c = low
    b0, bn, h00, h0n, hnn, e = high
    w = c / (1.0 + c * (gnn + h00))
    flux = w * (b0 - an)
    by_left = w * g0n
    by_right = w * h0n
    joined = (a0 + g0n * flux, bn - h0n * flux, g00 - g0n * by_left, by_left * h0n, hnn - h0n * by_right, e)
    return joined, (flux, by_left, by_right)


def pick(upper, own, other):
    low = tuple(jnp.where(upper, o, m) for m, o in zip(own, other))
    high = tuple(jnp.where(upper, m, o) for m, o in zip(own, other))
    return low, high


def last_message(upper, seg):
    a0, an, g00, g0n, gnn, c = seg
    return (jnp.where(upper, a0, an), jnp.where(upper, g00, c / (1.0 + c * gnn)))


def bit_of(position, level):
    return (position // (2**level)) % 2 == 1


def climb(position, own, received):
    coefs = []
    for level, other in enumerate(received):
        low, high = pick(bit_of(position, level), own, other)
        own, coef = merge(low, high)
        coefs.append(coef)
    return own, coefs


def end_fluxes(position, own, received, final):
    seg, coefs = climb(position, own, received)
    top = len(received)
    upper = bit_of(position, top)
    mine = last_message(upper, seg)
    (low_a, low_y), (high_a, high_g) = pick(upper, mine, final)
    flux = low_y * (high_a - low_a) / (1.0 + low_y * high_g)
    left = jnp.where(upper, -flux, 0.0)
    right = jnp.where(upper, 0.0, flux)
    for level in reversed(range(top)):
        const, by_left, by_right = coefs[level]
        flux = const + by_right * right - by_left * left
        upper = bit_of(position, level)
        left, right = jnp.where(upper, -flux, left), jnp.where(upper, right, flux)
    return left, right


def eliminate(v, c, count, keep):
    a0 = an = v(0)
    g00 = g0n = gnn = jnp.ones_like(an)
    for i in range(count - 1):
        face = c(i)
        w = face / (1.0 + face * (gnn + 1.0))
        following = v(i + 1)
        d = following - an
        keep(i, w, d, g0n)
        flux = w * d
        a0 = a0 + g0n * flux
        an = following - flux
        hw = g0n * w
        g00 = g00 - g0n * hw
        g0n = hw
        gnn = 1.0 - w
    return a0, an, g00, g0n, gnn, c(count - 1)


def substitute(factors, count, left, right, emit):
    above = right
    for i in reversed(range(count - 1)):
        w, d, h = factors(i)
        flux = w * (d + above - h * left)
        emit(i + 1, above - flux)
        above = flux
    emit(0, above + left)


def strip_kernel(dims, swap, *refs):
    nz, nx, ny = dims
    if swap:
        zlo, v, zhi, xr, first, last = refs
        at_x = lax.axis_index("gx")
        keep_lo = jnp.where(at_x == 1, 1.0, 0.0)
        keep_hi = jnp.where(at_x == 0, 1.0, 0.0)
    else:
        zlo, v, zhi, xlo, xhi, first, last = refs
    width = nx + 2 * edge
    per = lanes // width

    def row(z, t):
        cols = slice(t * lanes, (t + 1) * lanes)
        if z < halo:
            mid = zlo[nz - halo + z, :, cols]
        elif z < halo + nz:
            mid = v[z - halo, :, cols]
        else:
            mid = zhi[z - halo - nz, :, cols]
        if swap:
            side = xr[z, :, cols]
            return [side * keep_lo, mid, side * keep_hi]
        return [xlo[z, :, cols], mid, xhi[z, :, cols]]

    for t, out, begin in ((0, first, 0), (ny // lanes - 1, last, lanes - edge)):
        for chunk in range((nz + 2 * halo) // per):
            rows = []
            for z in range(per):
                rows += row(chunk * per + z, t)
            turned = jnp.concatenate(rows, axis=0).T
            out[:, chunk * lanes:(chunk + 1) * lanes] = turned[begin:begin + edge, :]


def main_kernel(dims, counts, swap, *refs):
    nz, nx, ny = dims
    nt = ny // lanes
    own = tuple(range(nt))
    every = tuple(range(nt + 1))
    lines = nz * nx
    if swap:
        zlo, v, zhi, xr, yl, yr = refs[:6]
        refs = refs[6:]
    else:
        zlo, v, zhi, xlo, xhi, yl, yr = refs[:7]
        refs = refs[7:]
    (fz, fx, fy, cy_out, send_z, send_x, send_y,
     wh, zp, bb, t1, dxs, vs, cz, cxs, cys, ct, vt) = refs
    at_z, at_x, at_y = lax.axis_index("gz"), lax.axis_index("gx"), lax.axis_index("gy")
    width = nx + 2 * edge
    rows_b = nx + 8
    per = lanes // width
    k = taps()
    kt = taps(0.25 / (contrast * contrast))
    if swap:
        keep_lo = jnp.where(at_x == 1, 1.0, 0.0)
        keep_hi = jnp.where(at_x == 0, 1.0, 0.0)

    gap = jnp.zeros((lanes - 2 * edge, lanes), jnp.float32)
    for chunk in range((nz + 2 * halo) // per):
        cols = slice(chunk * lanes, (chunk + 1) * lanes)
        turned = jnp.concatenate([yr[:, cols], gap, yl[:, cols]], axis=0).T
        for z in range(per):
            wh[chunk * per + z] = turned[z * width:(z + 1) * width, :]

    def centre(z, t):
        cols = slice(t * lanes, (t + 1) * lanes)
        if z < halo:
            return zlo[nz - halo + z, :, cols]
        if z < halo + nz:
            return v[z - halo, :, cols]
        return zhi[z - halo - nz, :, cols]

    def z_blur(load, store, count, weights):
        window = [load(i) for i in range(4)]
        for i in range(count):
            window.append(load(i + 4))
            store(i, five(weights, *window))
            window.pop(0)

    nb = nz + 8
    for t in own:
        cols = slice(t * lanes, (t + 1) * lanes)

        def put(rows, scale=None, t=t):
            def store(i, value):
                zp[t, i, rows, :] = value if scale is None else value * scale
            return store

        z_blur(lambda z: centre(z, t), put(slice(edge, edge + nx)), nb, k)
        if swap:
            def both(i, value):
                zp[t, i, 0:edge, :] = value * keep_lo
                zp[t, i, edge + nx:width, :] = value * keep_hi
            z_blur(lambda z: xr[z, :, cols], both, nb, k)
        else:
            z_blur(lambda z: xlo[z, :, cols], put(slice(0, edge)), nb, k)
            z_blur(lambda z: xhi[z, :, cols], put(slice(edge + nx, width)), nb, k)

    def put_h(i, value):
        zp[nt, i] = value
    z_blur(lambda z: wh[z], put_h, nb, k)

    blank = jnp.zeros((edge, lanes), jnp.float32)
    for z in range(nb):
        along_x = [five(k, *[zp[t, z, 2 + o:2 + o + rows_b, :] for o in range(5)]) for t in every]
        done = lane_blur(k, along_x, every)
        for t in every:
            bb[t, z, 0:edge, :] = blank
            bb[t, z, edge:edge + rows_b, :] = done[t]
            bb[t, z, edge + rows_b:, :] = blank

    xi = at_x * nx + lax.broadcasted_iota(jnp.int32, (rows_b, lanes), 0) - 4
    x_in = (xi >= 0) & (xi < nx * counts[1])
    lane = lax.broadcasted_iota(jnp.int32, (rows_b, lanes), 1)
    not_first = (at_y > 0).astype(jnp.float32)
    not_last = (at_y < counts[2] - 1).astype(jnp.float32)
    y_in = jnp.where(lane < lanes // 2, not_last, not_first)
    x_mask = jnp.where(x_in, 1.0, 0.0)
    masks = [x_mask] * nt + [x_mask * y_in]

    def z_mask(z, value):
        if 0 <= z < nz:
            return value
        inside = (at_z > 0) if z < 0 else (at_z < counts[0] - 1)
        return value * inside.astype(jnp.float32)

    def tensor(square, count):
        for t in every:
            window = [square(t, z) for z in range(-2, 2)]
            for i in range(count):
                window.append(square(t, i + 2))
                t1[t, i, 0:rows_b, :] = five(kt, *window)
                window.pop(0)

    def finish(z, first_row, rows, wanted):
        along_x = [five(k, *[t1[t, z, first_row + o:first_row + o + rows, :] for o in range(5)]) for t in every]
        return [1.0 / (1.0 + value) for value in lane_blur(k, along_x, wanted)]

    for t in every:
        for z in range(nz + 1):
            t1[t, z, rows_b:, :] = blank

    def square_z(t, z):
        slope = bb[t, z + 5, edge:edge + rows_b, :] - bb[t, z + 3, edge:edge + rows_b, :]
        return z_mask(z, slope * slope * masks[t])

    tensor(square_z, nz + 1)
    before = None
    for z in range(nz + 1):
        here = finish(z, 2, nx, own)
        if before is not None:
            scale = 0.5 * stiffness
            if z == nz:
                scale = jnp.where(at_z < counts[0] - 1, scale, 0.0)
            for t in own:
                cz[z - 1, :, t * lanes:(t + 1) * lanes] = (before[t] + here[t]) * scale
        before = here

    def keep_z(i, w, d, h):
        fz[0, i], fz[1, i], fz[2, i] = w, d, h

    seg = eliminate(lambda i: v[i], lambda i: cz[i], nz, keep_z)
    for i, value in enumerate(seg if counts[0] > 2 else last_message(bit_of(at_z, 0), seg)):
        send_z[i] = value

    def square_x(t, z):
        slope = bb[t, z + 4, edge + 1:edge + 1 + rows_b, :] - bb[t, z + 4, edge - 1:edge - 1 + rows_b, :]
        return z_mask(z, slope * slope * masks[t])

    tensor(square_x, nz)
    for z in range(nz):
        here = finish(z, 2, rows_b, own)
        for t in own:
            dxs[t, z * rows_b:(z + 1) * rows_b, :] = here[t]
            vs[t, z * nx:(z + 1) * nx, :] = v[z, :, t * lanes:(t + 1) * lanes]
    for t in own:
        cols = slice(t * lanes, (t + 1) * lanes)
        here = dxs[t, pl.ds(0, nz, stride=rows_b), :]
        for x in range(nx):
            following = dxs[t, pl.ds(x + 1, nz, stride=rows_b), :]
            scale = 0.5 * stiffness
            if x == nx - 1:
                scale = jnp.where(at_x < counts[1] - 1, scale, 0.0)
            cxs[0, x, :, cols] = (here + following) * scale
            cxs[1, x, :, cols] = vs[t, pl.ds(x, nz, stride=nx), :]
            here = following

    def keep_x(i, w, d, h):
        fx[0, i], fx[1, i], fx[2, i] = w, d, h

    seg = eliminate(lambda i: cxs[1, i], lambda i: cxs[0, i], nx, keep_x)
    for i, value in enumerate(seg if counts[1] > 2 else last_message(bit_of(at_x, 0), seg)):
        send_x[i] = value

    def square_y_layer(z):
        tiles = [bb[t, z + 4, edge:edge + rows_b, :] for t in every]
        up, down = lane_shift(tiles, 1, every), lane_shift(tiles, -1, every)
        out = []
        for t in every:
            slope = up[t] - down[t]
            out.append(z_mask(z, slope * slope * masks[t]))
        return out

    window = [square_y_layer(z) for z in range(-2, 2)]
    for z in range(nz):
        window.append(square_y_layer(z + 2))
        for t in every:
            t1[t, z, 0:rows_b, :] = five(kt, *[layer[t] for layer in window])
        window.pop(0)
    for z in range(nz):
        here = finish(z, 2, nx, every)
        following = lane_shift(here, 1, own)
        for t in own:
            cys[t, z * nx:(z + 1) * nx, :] = (here[t] + following[t]) * (0.5 * stiffness)
    for t in own:
        ct[t * lanes:(t + 1) * lanes, :] = cys[t].T
        vt[t * lanes:(t + 1) * lanes, :] = vs[t].T
    closing = jnp.where(at_y < counts[2] - 1, 1.0, 0.0)
    ct[ny - 1:ny, :] = ct[ny - 1:ny, :] * closing

    steps = ny // 16
    segs = []
    for half in range(2):
        def at(ref, i, half=half):
            return ref[pl.ds(half * steps + i, 8, stride=2 * steps), :]

        def keep_y(i, w, d, h, half=half):
            fy[0, i, half], fy[1, i, half], fy[2, i, half] = w, d, h

        segs.append(eliminate(functools.partial(at, vt), functools.partial(at, ct), steps, keep_y))
    seg, coef = merge(segs[0], segs[1])
    for i in range(3):
        cy_out[0, i] = coef[i]
    for level in range(3):
        other = tuple(pltpu.roll(value, 8 - 2**level, axis=0) for value in seg)
        seg, coef = merge(seg, other)
        for i in range(3):
            cy_out[level + 1, i] = coef[i]
    seg = seg if counts[2] > 2 else last_message(bit_of(at_y, 0), seg)
    for i, value in enumerate(seg):
        send_y[i:i + 1, :] = value[0:1, :]


def summary(ref, axis, count):
    if axis == 2:
        return tuple(ref[i:i + 1, :] for i in range(count))
    return tuple(ref[i] for i in range(count))


def merge_kernel(level, counts, depths, axes, *refs):
    refs = list(refs)
    groups = [[refs.pop(0) for _ in range(level + 2)] for _ in axes]
    for axis, group, out in zip(axes, groups, refs):
        position = lax.axis_index(("gz", "gx", "gy")[axis])
        own, *received = [summary(ref, axis, 6) for ref in group]
        seg, _ = climb(position, own, received)
        if depths[axis] == level + 2:
            seg = last_message(bit_of(position, level + 1), seg)
        for i, value in enumerate(seg):
            if axis == 2:
                out[i:i + 1, :] = value
            else:
                out[i] = value


def last_kernel(dims, depths, *refs):
    nz, nx, ny = dims
    nt = ny // lanes
    refs = list(refs)
    v, fz, fx, fy, cy = [refs.pop(0) for _ in range(5)]
    groups = [[refs.pop(0) for _ in range(depths[axis] + 1)] for axis in range(3)]
    out, acc, st, sx = refs
    fluxes = []
    for axis, group in enumerate(groups):
        position = lax.axis_index(("gz", "gx", "gy")[axis])
        if depths[axis] == 1:
            upper = bit_of(position, 0)
            mine, final = [summary(ref, axis, 2) for ref in group]
            (low_a, low_y), (high_a, high_g) = pick(upper, mine, final)
            flux = low_y * (high_a - low_a) / (1.0 + low_y * high_g)
            fluxes.append((jnp.where(upper, -flux, 0.0), jnp.where(upper, 0.0, flux)))
        else:
            own, *received = [summary(ref, axis, 6) for ref in group[:-1]]
            fluxes.append(end_fluxes(position, own, received, summary(group[-1], axis, 2)))

    left, right = fluxes[2]
    left = jnp.broadcast_to(left, (8, lanes))
    right = jnp.broadcast_to(right, (8, lanes))
    sub = lax.broadcasted_iota(jnp.int32, (8, lanes), 0)
    for level in (2, 1, 0):
        stride = 2**level
        const, by_left, by_right = [cy[level + 1, i] for i in range(3)]
        flux = const + by_right * right - by_left * left
        lower = sub % (2 * stride) == 0
        left, right = (jnp.where(lower, left, -pltpu.roll(flux, stride, axis=0)),
                       jnp.where(lower, flux, pltpu.roll(right, stride, axis=0)))
    flux = cy[0, 0] + cy[0, 2] * right - cy[0, 1] * left
    steps = ny // 16
    for half, (a, b) in enumerate(((left, flux), (-flux, right))):
        def factors(i, half=half):
            return fy[0, i, half], fy[1, i, half], fy[2, i, half]

        def emit(i, value, half=half):
            st[pl.ds(half * steps + i, 8, stride=2 * steps), :] = value

        substitute(factors, steps, a, b, emit)

    def emit_x(i, value):
        for t in range(nt):
            sx[t, pl.ds(i, nz, stride=nx), :] = value[:, t * lanes:(t + 1) * lanes]

    substitute(lambda i: (fx[0, i], fx[1, i], fx[2, i]), nx, *fluxes[1], emit_x)

    def emit_z(i, value):
        acc[i] = value

    substitute(lambda i: (fz[0, i], fz[1, i], fz[2, i]), nz, *fluxes[0], emit_z)
    for t in range(nt):
        cols = slice(t * lanes, (t + 1) * lanes)
        turned = st[cols, :].T
        for z in range(nz):
            rows = slice(z * nx, (z + 1) * nx)
            total = acc[z, :, cols] + sx[t, rows, :] + turned[rows, :]
            out[z, :, cols] = v[z, :, cols] + total * (1.0 / 3.0)


def shift(value, axis, step):
    n = lax.axis_size(axis)
    return lax.ppermute(value, axis, [(i, i + step) for i in range(n) if 0 <= i + step < n])


def swap_bit(value, axis, level):
    n = lax.axis_size(axis)
    return lax.ppermute(value, axis, [(i, i ^ (2**level)) for i in range(n)])


def body(volume):
    dims = volume.shape
    nz, nx, ny = dims
    nt = ny // lanes
    names = ("gz", "gx", "gy")
    counts = tuple(lax.axis_size(name) for name in names)
    depths = tuple(count.bit_length() - 1 for count in counts)
    assert all(2**d == n and d >= 1 for d, n in zip(depths, counts))
    assert nz == 8 and nz * nx == lanes and nx >= 8
    swap = counts[1] == 2
    f32 = lambda *shape: jax.ShapeDtypeStruct(shape, jnp.float32)
    scratch = lambda *shape: pltpu.VMEM(shape, jnp.float32)
    call = functools.partial(pl.pallas_call)

    zlo = shift(volume, "gz", 1)
    zhi = shift(volume, "gz", -1)
    tall = jnp.concatenate([zlo[nz - halo:], volume, zhi[:halo]], axis=0)
    low_rows, high_rows = tall[:, :edge], tall[:, nx - edge:]
    if swap:
        sides = [swap_bit(jnp.where(lax.axis_index("gx") == 0, high_rows, low_rows), "gx", 0)]
    else:
        sides = [shift(high_rows, "gx", 1), shift(low_rows, "gx", -1)]
    high = nz + 2 * halo
    width = nx + 2 * edge
    flat = high * width
    first, last = call(
        functools.partial(strip_kernel, dims, swap),
        out_shape=[f32(edge, flat)] * 2,
        in_specs=[VMEM] * (3 + len(sides)), out_specs=[VMEM] * 2,
    )(zlo, volume, zhi, *sides)
    yl = shift(last, "gy", 1)
    yr = shift(first, "gy", -1)

    steps = ny // 16
    send_shape = lambda d: 6 if d > 1 else 2
    rows_b = nx + 8
    fz, fx, fy, cy, send_z, send_x, send_y = call(
        functools.partial(main_kernel, dims, counts, swap),
        out_shape=[f32(3, nz - 1, nx, ny), f32(3, nx - 1, nz, ny), f32(3, steps - 1, 2, 8, lanes), f32(4, 3, 8, lanes),
                   f32(send_shape(depths[0]), nx, ny), f32(send_shape(depths[1]), nz, ny), f32(8, lanes)],
        in_specs=[VMEM] * (5 + len(sides)), out_specs=[VMEM] * 7,
        scratch_shapes=[scratch(high, width, lanes), scratch(nt + 1, nz + 8, width, lanes),
                        scratch(nt + 1, nz + 8, rows_b + 2 * edge, lanes), scratch(nt + 1, nz + 1, rows_b + 8, lanes),
                        scratch(nt, nz * rows_b, lanes), scratch(nt, lanes, lanes), scratch(nz, nx, ny),
                        scratch(2, nx, nz, ny), scratch(nt, lanes, lanes), scratch(ny, lanes), scratch(ny, lanes)],
    )(zlo, volume, zhi, *sides, yl, yr)

    groups = [[send_z], [send_x], [send_y]]
    message = [send_z, send_x, send_y]
    for level in range(max(depths)):
        for axis in range(3):
            if level < depths[axis]:
                groups[axis].append(swap_bit(message[axis], names[axis], level))
        axes = [axis for axis in range(3) if depths[axis] > level + 1]
        if axes:
            shapes = []
            for axis in axes:
                count = 2 if depths[axis] == level + 2 else 6
                shapes.append(f32(8, lanes) if axis == 2 else f32(count, *((nx, ny) if axis == 0 else (nz, ny))))
            sent = call(
                functools.partial(merge_kernel, level, counts, depths, axes),
                out_shape=shapes,
                in_specs=[VMEM] * (len(axes) * (level + 2)), out_specs=[VMEM] * len(axes),
            )(*[ref for axis in axes for ref in groups[axis]])
            for axis, value in zip(axes, sent):
                message[axis] = value
    return call(
        functools.partial(last_kernel, dims, depths),
        out_shape=f32(*dims),
        in_specs=[VMEM] * (5 + sum(len(g) for g in groups)), out_specs=VMEM,
        scratch_shapes=[scratch(*dims), scratch(ny, lanes), scratch(nt, lanes, lanes)],
    )(volume, fz, fx, fy, cy, *groups[0], *groups[1], *groups[2])


def solution(mesh):
    return jax.shard_map(
        body,
        mesh=mesh,
        in_specs=(P("gz", "gx", "gy"),),
        out_specs=P("gz", "gx", "gy"),
        check_vma=False,
    )
```

time: 236 us -> 49.8 us (0.21); the launches traced: 231 us -> 49.5 us
  local copies, waits for them, and re-layouts: 121 us -> 3.69 us
  other arithmetic: 35.5 us -> 0.04 us
  starting transfers between devices: 50.3 us -> 21.7 us
  Pallas kernels: 0 us -> 10.6 us
  waiting for transfers between devices: 22.7 us -> 13.4 us
    slice x168 -> x2, local copies, waits for them, and re-layouts: 108 us -> 0.01 us  [body(): tall = jnp.concatenate([zlo[nz - halo:], volume, zhi[:halo]], axis=0)]
    all_to_all x9 -> x0, starting transfers between devices: 37.5 us -> none  [the longest x1 5.95 us: body(): lax.all_to_all(volume, 'gz', split_axis=1, concat_axis=0, tiled=True)]
    add x25 -> x0, other arithmetic: 19.3 us -> none  [the longest x17 16.4 us: reduce_solve(): even_side + lower_factor * shifted(odd_side, 1, axis_dim, 0.0)]
    all_to_all x9 -> x0, waiting for transfers between devices: 15.4 us -> none  [the longest x1 3.81 us: body(): lax.all_to_all(lines_y, 'gy', split_axis=2, concat_axis=0, tiled=True)]
    pallas_call x0 -> x4, Pallas kernels: none -> 10.6 us  [the longest x1 4.75 us: body(): call(functools.partial(main_kernel, dims, counts, swap), out_shape=[f32(3...]
    ppermute x6 -> x10, starting transfers between devices: 12.7 us -> 21.7 us  [the longest x6 12.2 us: swap_bit(): return lax.ppermute(value, axis, [(i, i ^ 2 ** level) for i in range(n)])]
    ppermute x6 -> x10, waiting for transfers between devices: 7.34 us -> 13.4 us  [the longest x4 6.95 us: shift(): lax.ppermute(value, axis, [(i, i + step) for i in range(n) if 0 <= i + st...]
    another operation x40 -> x0, other arithmetic: 5.58 us -> none  [the longest x38 4.69 us: reduce_solve(): joined = jnp.stack([even_part, odd_part], axis=axis_dim + 1)]
  transfers between devices with their start and end apart: 15 -> 10, of which waited for: 9 -> 7; matrix products, arithmetic and copies ran while one was open for 65% -> 0% of each run, Pallas kernels for 0% -> 0%
where the time goes in v1:
time: 49.8 us; the launch traced here: 49.5 us
  starting transfers between devices  21.7 us (44%)
  waiting for transfers between devices  13.4 us (27%)
  Pallas kernels  10.6 us (21%)
  local copies, waits for them, and re-layouts  3.69 us (7%)
    ppermute x6, starting transfers between devices, swap_bit(): return lax.ppermute(value, axis, [(i, i ^ 2 ** level) for i in range(n)])  12.2 us
    ppermute x4, starting transfers between devices, shift(): lax.ppermute(value, axis, [(i, i + step) for i in range(n) if 0 <= i + st...  9.45 us
    ppermute x4, waiting for transfers between devices, shift(): lax.ppermute(value, axis, [(i, i + step) for i in range(n) if 0 <= i + st...  6.95 us
    ppermute x6, waiting for transfers between devices, swap_bit(): return lax.ppermute(value, axis, [(i, i ^ 2 ** level) for i in range(n)])  6.45 us
    pallas_call x1, Pallas kernels, body(): call(functools.partial(main_kernel, dims, counts, swap), out_shape=[f32(3...  4.75 us
    unnamed x26, local copies, waits for them, and re-layouts  3.68 us
    pallas_call x1, Pallas kernels, body(): call(functools.partial(last_kernel, dims, depths), out_shape=f32(*dims),...  2.28 us
    pallas_call x1, Pallas kernels, body(): call(functools.partial(strip_kernel, dims, swap), out_shape=[f32(edge, fl...  1.95 us
  transfers between devices with their start and end apart: 10, of which 7 were waited for; matrix products, arithmetic and copies ran while one was open for 0% of the time, Pallas kernels for 0%

profile of v1, /device:TPU:0, one launch (start us, length us, event | category | flops | bytes accessed | tf_op | source)
XLA Modules:
  0.0 49.5 jit_solution(10363735295789021417)
XLA Ops:
  0.0 1.3 %collective-permute-start.1 = (f32[8,16,256]{2,1,0:T(8,128)}, f32[8,16,256]{2,1,0:T(8,128)S(1)}, u32[]{:S(2)}, u32[]{:S(2)}) collective-permute-start(f32[8,16,256]{2,1,0:T(8,128)} %refs_0_.1), channel_id=1, source_target_pairs={{1,0},{2,1},{3,2},{5,4},{6,5},{7,6},{9,8},{10,9},{11,10},{13,12},{... | collective-permute-start | bytes 393224 | tf_op jit(solution)/shard_map/ppermute | solution.py:457
  1.3 5.6 %collective-permute-start = (f32[8,16,256]{2,1,0:T(8,128)}, f32[8,16,256]{2,1,0:T(8,128)S(1)}, u32[]{:S(2)}, u32[]{:S(2)}) collective-permute-start(f32[8,16,256]{2,1,0:T(8,128)} %refs_0_.1), channel_id=1, source_target_pairs={{0,1},{1,2},{2,3},{4,5},{5,6},{6,7},{8,9},{9,10},{10,11},{12,13},{... | collective-permute-start | bytes 393224 | tf_op jit(solution)/shard_map/ppermute | solution.py:457
  6.9 1.8 %collective-permute-done.1.refs_2_ = f32[8,16,256]{2,1,0:T(8,128)S(1)} collective-permute-done((f32[8,16,256]{2,1,0:T(8,128)}, f32[8,16,256]{2,1,0:T(8,128)S(1)}, u32[]{:S(2)}, u32[]{:S(2)}) %collective-permute-start.1) | collective-permute-done | bytes 131104 | tf_op jit(solution)/shard_map/ppermute | solution.py:457
  8.7 0.0 copy-start.1
  8.7 0.0 copy-start
  8.7 1.3 %collective-permute-done.refs_0_ = f32[8,16,256]{2,1,0:T(8,128)S(1)} collective-permute-done((f32[8,16,256]{2,1,0:T(8,128)}, f32[8,16,256]{2,1,0:T(8,128)S(1)}, u32[]{:S(2)}, u32[]{:S(2)}) %collective-permute-start) | collective-permute-done | bytes 131104 | tf_op jit(solution)/shard_map/ppermute | solution.py:457
  9.9 0.0 copy-start.2
  10.0 0.0 copy-done.1
  10.0 0.0 copy-done
  10.0 0.6 %copy-done.2 = f32[8,16,256]{2,1,0:T(8,128)} copy-done((f32[8,16,256]{2,1,0:T(8,128)}, f32[8,16,256]{2,1,0:T(8,128)S(1)}, u32[]{:S(2)}) %copy-start.2) | copy-done | bytes 131096
  10.6 1.8 %collective-permute-start.2 = (f32[20,8,256]{2,1,0:T(8,128)S(1)}, f32[20,8,256]{2,1,0:T(8,128)S(1)}, u32[]{:S(2)}, u32[]{:S(2)}) collective-permute-start(f32[20,8,256]{2,1,0:T(8,128)S(1)} %slice_select_fusion), channel_id=1, source_target_pairs={{0,16},{16,0},{1,17},{17,1},{2,18},{18,2},{3,19},{19,3},{4,20},{20... | collective-permute-start | bytes 491528 | tf_op jit(solution)/shard_map/ppermute | solution.py:462
  12.4 3.6 %collective-permute-done.2.refs_3_ = f32[20,8,256]{2,1,0:T(8,128)S(1)} collective-permute-done((f32[20,8,256]{2,1,0:T(8,128)S(1)}, f32[20,8,256]{2,1,0:T(8,128)S(1)}, u32[]{:S(2)}, u32[]{:S(2)}) %collective-permute-start.2) | collective-permute-done | bytes 163872 | tf_op jit(solution)/shard_map/ppermute | solution.py:462
  16.0 0.0 copy-start.3
  16.0 0.7 %copy-done.3 = f32[20,8,256]{2,1,0:T(8,128)} copy-done((f32[20,8,256]{2,1,0:T(8,128)}, f32[20,8,256]{2,1,0:T(8,128)S(1)}, u32[]{:S(2)}) %copy-start.3) | copy-done | bytes 163864
  16.7 2.0 %shard_map.17 = (f32[8,640]{1,0:T(8,128)}, f32[8,640]{1,0:T(8,128)}) custom-call(f32[8,16,256]{2,1,0:T(8,128)} %copy-done.2, f32[8,16,256]{2,1,0:T(8,128)} %refs_0_.1, f32[8,16,256]{2,1,0:T(8,128)} %copy-done.1, f32[20,8,256]{2,1,0:T(8,128)} %copy-done.3), custom_call_target="tpu_custom_call" | custom-call | tf_op jit(solution)/shard_map/pallas_call | solution.py:490
  18.6 1.3 %collective-permute-start.3 = (f32[8,640]{1,0:T(8,128)}, f32[8,640]{1,0:T(8,128)S(1)}, u32[]{:S(2)}, u32[]{:S(2)}) collective-permute-start(f32[8,640]{1,0:T(8,128)} %get-tuple-element.16), channel_id=1, source_target_pairs={{0,4},{4,8},{8,12},{1,5},{5,9},{9,13},{2,6},{6,10},{10,14},{3,7},{... | collective-permute-start | bytes 61448 | tf_op jit(solution)/shard_map/ppermute | solution.py:457
  19.9 1.3 %collective-permute-start.4 = (f32[8,640]{1,0:T(8,128)}, f32[8,640]{1,0:T(8,128)S(1)}, u32[]{:S(2)}, u32[]{:S(2)}) collective-permute-start(f32[8,640]{1,0:T(8,128)} %get-tuple-element.17), channel_id=1, source_target_pairs={{4,0},{8,4},{12,8},{5,1},{9,5},{13,9},{6,2},{10,6},{14,10},{7,3},{... | collective-permute-start | bytes 61448 | tf_op jit(solution)/shard_map/ppermute | solution.py:457
  21.2 0.0 collective-permute-done.3.refs_4_
  21.2 0.0 copy-start.6
  21.2 3.9 %collective-permute-done.4.refs_5_ = f32[8,640]{1,0:T(8,128)S(1)} collective-permute-done((f32[8,640]{1,0:T(8,128)}, f32[8,640]{1,0:T(8,128)S(1)}, u32[]{:S(2)}, u32[]{:S(2)}) %collective-permute-start.4) | collective-permute-done | bytes 20512 | tf_op jit(solution)/shard_map/ppermute | solution.py:457
  25.2 0.0 copy-done.6
  25.2 0.0 copy-start.7
  25.2 0.6 %copy-done.7 = f32[8,640]{1,0:T(8,128)} copy-done((f32[8,640]{1,0:T(8,128)}, f32[8,640]{1,0:T(8,128)S(1)}, u32[]{:S(2)}) %copy-start.7) | copy-done | bytes 20504
  25.8 4.7 %shard_map.18 = (f32[3,7,16,256]{3,2,1,0:T(8,128)}, f32[3,15,8,256]{3,2,1,0:T(8,128)}, f32[3,15,2,8,128]{4,3,2,1,0:T(8,128)}, f32[4,3,8,128]{3,2,1,0:T(8,128)}, ...) custom-call(f32[8,16,256]{2,1,0:T(8,128)} %copy-done.2, f32[8,16,256]{2,1,0:T(8,128)} %refs_0_.1, ...), custom_call_target="tpu_custom_call" | custom-call | tf_op jit(solution)/shard_map/pallas_call | solution.py:501
  30.5 2.3 %collective-permute-start.5 = (f32[6,16,256]{2,1,0:T(8,128)}, f32[6,16,256]{2,1,0:T(8,128)S(1)}, u32[]{:S(2)}, u32[]{:S(2)}) collective-permute-start(f32[6,16,256]{2,1,0:T(8,128)} %get-tuple-element.22.refs_0_.refs_5_), channel_id=1, source_target_pairs={{0,1},{1,0},{2,3},{3,2},{4,5},{5,4},{6,7},{7,6},{8,9},{9,8},{10,11... | collective-permute-start | bytes 294920 | tf_op jit(solution)/shard_map/ppermute | solution.py:462
  32.8 0.0 copy-start.8
  32.8 2.2 %collective-permute-start.6 = (f32[8,128]{1,0:T(8,128)}, f32[8,128]{1,0:T(8,128)S(1)}, u32[]{:S(2)}, u32[]{:S(2)}) collective-permute-start(f32[8,128]{1,0:T(8,128)} %get-tuple-element.23.refs_2_.refs_10_), channel_id=1, source_target_pairs={{0,4},{4,0},{8,12},{12,8},{1,5},{5,1},{9,13},{13,9},{2,6},{6,2},{1... | collective-permute-start | bytes 12296 | tf_op jit(solution)/shard_map/ppermute | solution.py:462
  35.1 1.0 %collective-permute-done.6.refs_3_.refs_11_ = f32[8,128]{1,0:T(8,128)S(1)} collective-permute-done((f32[8,128]{1,0:T(8,128)}, f32[8,128]{1,0:T(8,128)S(1)}, u32[]{:S(2)}, u32[]{:S(2)}) %collective-permute-start.6) | collective-permute-done | bytes 4128 | tf_op jit(solution)/shard_map/ppermute | solution.py:462
  36.1 0.0 copy-start.10
  36.1 0.0 collective-permute-done.5.refs_1_.refs_6_
  36.1 0.6 %copy-done.10 = f32[8,128]{1,0:T(8,128)} copy-done((f32[8,128]{1,0:T(8,128)}, f32[8,128]{1,0:T(8,128)S(1)}, u32[]{:S(2)}) %copy-start.10) | copy-done | bytes 4120
  36.7 0.0 copy-start.4
  36.7 0.6 %copy-done.4 = f32[6,16,256]{2,1,0:T(8,128)} copy-done((f32[6,16,256]{2,1,0:T(8,128)}, f32[6,16,256]{2,1,0:T(8,128)S(1)}, u32[]{:S(2)}) %copy-start.4) | copy-done | bytes 98328
  37.3 1.6 %shard_map.19 = (f32[2,16,256]{2,1,0:T(8,128)}, f32[8,128]{1,0:T(8,128)}) custom-call(f32[6,16,256]{2,1,0:T(8,128)} %get-tuple-element.22.refs_0_.refs_5_, f32[6,16,256]{2,1,0:T(8,128)} %copy-done.4, f32[8,128]{1,0:T(8,128)} %get-tuple-element.23.refs_2_.refs_10_, f32[8,128]{1,0:T(8,128)} %copy-done.10), custom_call_target="tpu_custom_call" | custom-call | tf_op jit(solution)/shard_map/pallas_call | solution.py:524
  38.9 0.0 copy-start.12
  38.9 2.6 %collective-permute-start.7 = (f32[2,16,256]{2,1,0:T(8,128)}, f32[2,16,256]{2,1,0:T(8,128)S(1)}, u32[]{:S(2)}, u32[]{:S(2)}) collective-permute-start(f32[2,16,256]{2,1,0:T(8,128)} %get-tuple-element.24), channel_id=1, source_target_pairs={{0,2},{1,3},{2,0},{3,1},{4,6},{5,7},{6,4},{7,5},{8,10},{9,11},{10,... | collective-permute-start | bytes 98312 | tf_op jit(solution)/shard_map/ppermute | solution.py:462
  41.5 0.0 copy-done.8
  41.5 1.5 %collective-permute-start.8 = (f32[2,8,256]{2,1,0:T(8,128)S(1)}, f32[2,8,256]{2,1,0:T(8,128)S(1)}, u32[]{:S(2)}, u32[]{:S(2)}) collective-permute-start(f32[2,8,256]{2,1,0:T(8,128)S(1)} %copy-done.8), channel_id=1, source_target_pairs={{0,16},{16,0},{1,17},{17,1},{2,18},{18,2},{3,19},{19,3},{4,20},{20... | collective-permute-start | bytes 49160 | tf_op jit(solution)/shard_map/ppermute | solution.py:462
  43.0 0.0 copy-done.12
  43.0 1.8 %collective-permute-start.9 = (f32[8,128]{1,0:T(8,128)S(1)}, f32[8,128]{1,0:T(8,128)S(1)}, u32[]{:S(2)}, u32[]{:S(2)}) collective-permute-start(f32[8,128]{1,0:T(8,128)S(1)} %copy-done.12), channel_id=1, source_target_pairs={{0,8},{4,12},{8,0},{12,4},{1,9},{5,13},{9,1},{13,5},{2,10},{6,14},... | collective-permute-start | bytes 12296 | tf_op jit(solution)/shard_map/ppermute | solution.py:462
  44.8 0.4 collective-permute-done.8.refs_9_
  45.3 0.0 copy-start.9
  45.3 1.4 %collective-permute-done.9.refs_12_ = f32[8,128]{1,0:T(8,128)S(1)} collective-permute-done((f32[8,128]{1,0:T(8,128)S(1)}, f32[8,128]{1,0:T(8,128)S(1)}, u32[]{:S(2)}, u32[]{:S(2)}) %collective-permute-start.9) | collective-permute-done | bytes 4128 | tf_op jit(solution)/shard_map/ppermute | solution.py:462
  46.6 0.0 copy-start.11
  46.6 0.0 collective-permute-done.7.refs_7_
  46.6 0.0 copy-start.5
  46.6 0.0 copy-done.9
  46.6 0.6 %copy-done.11 = f32[8,128]{1,0:T(8,128)} copy-done((f32[8,128]{1,0:T(8,128)}, f32[8,128]{1,0:T(8,128)S(1)}, u32[]{:S(2)}) %copy-start.11) | copy-done | bytes 4120
  47.2 0.0 copy-done.5
  47.2 2.3 %shard_map.20 = f32[8,16,256]{2,1,0:T(8,128)} custom-call(f32[8,16,256]{2,1,0:T(8,128)} %refs_0_.1, f32[3,7,16,256]{3,2,1,0:T(8,128)} %get-tuple-element.18.refs_1_, f32[3,15,8,256]{3,2,1,0:T(8,128)} %get-tuple-element.19.refs_2_, f32[3,15,2,8,128]{4,3,2,1,0:T(8,128)} %get-tuple-element.20.refs_3_, f32[4,3,8,128]{3,2,1,0:T(8,128)} %get-tuple-element.21.refs_4_, ...), custom_call_target="tpu_custom_call" | custom-call | tf_op jit(solution)/shard_map/pallas_call | solution.py:531
  (4 shorter events, 0.1 us)
Async XLA Ops:
  0.0 8.6 %collective-permute-start.1 = (f32[8,16,256]{2,1,0:T(8,128)}, f32[8,16,256]{2,1,0:T(8,128)S(1)}, u32[]{:S(2)}, u32[]{:S(2)}) collective-permute-start(f32[8,16,256]{2,1,0:T(8,128)} %refs_0_.1), channel_id=1, source_target_pairs={{1,0},{2,1},{3,2},{5,4},{6,5},{7,6},{9,8},{10,9},{11,10},{13,12},{... | collective-permute-start | bytes 393224 | tf_op jit(solution)/shard_map/ppermute | solution.py:457
  1.3 8.7 %collective-permute-start = (f32[8,16,256]{2,1,0:T(8,128)}, f32[8,16,256]{2,1,0:T(8,128)S(1)}, u32[]{:S(2)}, u32[]{:S(2)}) collective-permute-start(f32[8,16,256]{2,1,0:T(8,128)} %refs_0_.1), channel_id=1, source_target_pairs={{0,1},{1,2},{2,3},{4,5},{5,6},{6,7},{8,9},{9,10},{10,11},{12,13},{... | collective-permute-start | bytes 393224 | tf_op jit(solution)/shard_map/ppermute | solution.py:457
  8.7 1.3 %copy-start.1 = (f32[8,16,256]{2,1,0:T(8,128)}, f32[8,16,256]{2,1,0:T(8,128)S(1)}, u32[]{:S(2)}) copy-start(f32[8,16,256]{2,1,0:T(8,128)S(1)} %collective-permute-done.1.refs_2_) | copy-start | bytes 393220
  8.7 1.3 %copy-start = (f32[8,16,256]{2,1,0:T(8,128)S(1)}, f32[8,16,256]{2,1,0:T(8,128)}, u32[]{:S(2)}) copy-start(f32[8,16,256]{2,1,0:T(8,128)} %refs_0_.1) | copy-start | bytes 393220
  9.9 0.7 %copy-start.2 = (f32[8,16,256]{2,1,0:T(8,128)}, f32[8,16,256]{2,1,0:T(8,128)S(1)}, u32[]{:S(2)}) copy-start(f32[8,16,256]{2,1,0:T(8,128)S(1)} %collective-permute-done.refs_0_) | copy-start | bytes 393220
  10.6 5.4 %collective-permute-start.2 = (f32[20,8,256]{2,1,0:T(8,128)S(1)}, f32[20,8,256]{2,1,0:T(8,128)S(1)}, u32[]{:S(2)}, u32[]{:S(2)}) collective-permute-start(f32[20,8,256]{2,1,0:T(8,128)S(1)} %slice_select_fusion), channel_id=1, source_target_pairs={{0,16},{16,0},{1,17},{17,1},{2,18},{18,2},{3,19},{19,3},{4,20},{20... | collective-permute-start | bytes 491528 | tf_op jit(solution)/shard_map/ppermute | solution.py:462
  16.0 0.7 %copy-start.3 = (f32[20,8,256]{2,1,0:T(8,128)}, f32[20,8,256]{2,1,0:T(8,128)S(1)}, u32[]{:S(2)}) copy-start(f32[20,8,256]{2,1,0:T(8,128)S(1)} %collective-permute-done.2.refs_3_) | copy-start | bytes 491524
  18.6 2.6 %collective-permute-start.3 = (f32[8,640]{1,0:T(8,128)}, f32[8,640]{1,0:T(8,128)S(1)}, u32[]{:S(2)}, u32[]{:S(2)}) collective-permute-start(f32[8,640]{1,0:T(8,128)} %get-tuple-element.16), channel_id=1, source_target_pairs={{0,4},{4,8},{8,12},{1,5},{5,9},{9,13},{2,6},{6,10},{10,14},{3,7},{... | collective-permute-start | bytes 61448 | tf_op jit(solution)/shard_map/ppermute | solution.py:457
  19.9 5.3 %collective-permute-start.4 = (f32[8,640]{1,0:T(8,128)}, f32[8,640]{1,0:T(8,128)S(1)}, u32[]{:S(2)}, u32[]{:S(2)}) collective-permute-start(f32[8,640]{1,0:T(8,128)} %get-tuple-element.17), channel_id=1, source_target_pairs={{4,0},{8,4},{12,8},{5,1},{9,5},{13,9},{6,2},{10,6},{14,10},{7,3},{... | collective-permute-start | bytes 61448 | tf_op jit(solution)/shard_map/ppermute | solution.py:457
  21.2 3.9 %copy-start.6 = (f32[8,640]{1,0:T(8,128)}, f32[8,640]{1,0:T(8,128)S(1)}, u32[]{:S(2)}) copy-start(f32[8,640]{1,0:T(8,128)S(1)} %collective-permute-done.3.refs_4_) | copy-start | bytes 61444
  25.2 0.6 %copy-start.7 = (f32[8,640]{1,0:T(8,128)}, f32[8,640]{1,0:T(8,128)S(1)}, u32[]{:S(2)}) copy-start(f32[8,640]{1,0:T(8,128)S(1)} %collective-permute-done.4.refs_5_) | copy-start | bytes 61444
  30.5 5.6 %collective-permute-start.5 = (f32[6,16,256]{2,1,0:T(8,128)}, f32[6,16,256]{2,1,0:T(8,128)S(1)}, u32[]{:S(2)}, u32[]{:S(2)}) collective-permute-start(f32[6,16,256]{2,1,0:T(8,128)} %get-tuple-element.22.refs_0_.refs_5_), channel_id=1, source_target_pairs={{0,1},{1,0},{2,3},{3,2},{4,5},{5,4},{6,7},{7,6},{8,9},{9,8},{10,11... | collective-permute-start | bytes 294920 | tf_op jit(solution)/shard_map/ppermute | solution.py:462
  32.8 8.7 %copy-start.8 = (f32[2,8,256]{2,1,0:T(8,128)S(1)}, f32[2,8,256]{2,1,0:T(8,128)}, u32[]{:S(2)}) copy-start(f32[2,8,256]{2,1,0:T(8,128)} %get-tuple-element.25.refs_8_) | copy-start | bytes 49156
  32.8 3.3 %collective-permute-start.6 = (f32[8,128]{1,0:T(8,128)}, f32[8,128]{1,0:T(8,128)S(1)}, u32[]{:S(2)}, u32[]{:S(2)}) collective-permute-start(f32[8,128]{1,0:T(8,128)} %get-tuple-element.23.refs_2_.refs_10_), channel_id=1, source_target_pairs={{0,4},{4,0},{8,12},{12,8},{1,5},{5,1},{9,13},{13,9},{2,6},{6,2},{1... | collective-permute-start | bytes 12296 | tf_op jit(solution)/shard_map/ppermute | solution.py:462
  36.1 0.6 %copy-start.10 = (f32[8,128]{1,0:T(8,128)}, f32[8,128]{1,0:T(8,128)S(1)}, u32[]{:S(2)}) copy-start(f32[8,128]{1,0:T(8,128)S(1)} %collective-permute-done.6.refs_3_.refs_11_) | copy-start | bytes 12292
  36.7 0.6 %copy-start.4 = (f32[6,16,256]{2,1,0:T(8,128)}, f32[6,16,256]{2,1,0:T(8,128)S(1)}, u32[]{:S(2)}) copy-start(f32[6,16,256]{2,1,0:T(8,128)S(1)} %collective-permute-done.5.refs_1_.refs_6_) | copy-start | bytes 294916
  38.9 4.1 %copy-start.12 = (f32[8,128]{1,0:T(8,128)S(1)}, f32[8,128]{1,0:T(8,128)}, u32[]{:S(2)}) copy-start(f32[8,128]{1,0:T(8,128)} %get-tuple-element.26) | copy-start | bytes 12292
  38.9 7.7 %collective-permute-start.7 = (f32[2,16,256]{2,1,0:T(8,128)}, f32[2,16,256]{2,1,0:T(8,128)S(1)}, u32[]{:S(2)}, u32[]{:S(2)}) collective-permute-start(f32[2,16,256]{2,1,0:T(8,128)} %get-tuple-element.24), channel_id=1, source_target_pairs={{0,2},{1,3},{2,0},{3,1},{4,6},{5,7},{6,4},{7,5},{8,10},{9,11},{10,... | collective-permute-start | bytes 98312 | tf_op jit(solution)/shard_map/ppermute | solution.py:462
  41.5 3.7 %collective-permute-start.8 = (f32[2,8,256]{2,1,0:T(8,128)S(1)}, f32[2,8,256]{2,1,0:T(8,128)S(1)}, u32[]{:S(2)}, u32[]{:S(2)}) collective-permute-start(f32[2,8,256]{2,1,0:T(8,128)S(1)} %copy-done.8), channel_id=1, source_target_pairs={{0,16},{16,0},{1,17},{17,1},{2,18},{18,2},{3,19},{19,3},{4,20},{20... | collective-permute-start | bytes 49160 | tf_op jit(solution)/shard_map/ppermute | solution.py:462
  43.0 3.6 %collective-permute-start.9 = (f32[8,128]{1,0:T(8,128)S(1)}, f32[8,128]{1,0:T(8,128)S(1)}, u32[]{:S(2)}, u32[]{:S(2)}) collective-permute-start(f32[8,128]{1,0:T(8,128)S(1)} %copy-done.12), channel_id=1, source_target_pairs={{0,8},{4,12},{8,0},{12,4},{1,9},{5,13},{9,1},{13,5},{2,10},{6,14},... | collective-permute-start | bytes 12296 | tf_op jit(solution)/shard_map/ppermute | solution.py:462
  45.3 1.4 %copy-start.9 = (f32[2,8,256]{2,1,0:T(8,128)}, f32[2,8,256]{2,1,0:T(8,128)S(1)}, u32[]{:S(2)}) copy-start(f32[2,8,256]{2,1,0:T(8,128)S(1)} %collective-permute-done.8.refs_9_) | copy-start | bytes 49156
  46.6 0.6 %copy-start.11 = (f32[8,128]{1,0:T(8,128)}, f32[8,128]{1,0:T(8,128)S(1)}, u32[]{:S(2)}) copy-start(f32[8,128]{1,0:T(8,128)S(1)} %collective-permute-done.9.refs_12_) | copy-start | bytes 12292
  46.6 0.6 %copy-start.5 = (f32[2,16,256]{2,1,0:T(8,128)}, f32[2,16,256]{2,1,0:T(8,128)S(1)}, u32[]{:S(2)}) copy-start(f32[2,16,256]{2,1,0:T(8,128)S(1)} %collective-permute-done.7.refs_7_) | copy-start | bytes 98308

commit v2 on v1

--- a/solution.py
+++ b/solution.py
@@ -474,7 +474,7 @@
     swap = counts[1] == 2
     f32 = lambda *shape: jax.ShapeDtypeStruct(shape, jnp.float32)
     scratch = lambda *shape: pltpu.VMEM(shape, jnp.float32)
-    call = functools.partial(pl.pallas_call)
+    call = functools.partial(pl.pallas_call, compiler_params=pltpu.CompilerParams(vmem_limit_bytes=16 * 2**20))
 
     zlo = shift(volume, "gz", 1)
     zhi = shift(volume, "gz", -1)

time: 49.8 us -> 39.8 us (0.80)
  Pallas kernels: 10.6 us -> 3.95 us
  local copies, waits for them, and re-layouts: 3.69 us -> 0.02 us
  starting transfers between devices: 21.7 us -> 22.7 us
  waiting for transfers between devices: 13.4 us -> 12.8 us
    unnamed x26 -> x2, local copies, waits for them, and re-layouts: 3.68 us -> 0.01 us
    pallas_call x1, Pallas kernels: 4.75 us -> 2.73 us  [body(): call(functools.partial(main_kernel, dims, counts, swap), out_shape=[f32(3...]
    pallas_call x1, Pallas kernels: 1.95 us -> 0.22 us  [body(): call(functools.partial(strip_kernel, dims, swap), out_shape=[f32(edge, fl...]
    pallas_call x1, Pallas kernels: 1.6 us -> 0.05 us  [body(): call(functools.partial(merge_kernel, level, counts, depths, axes), out_sh...]
    pallas_call x1, Pallas kernels: 2.28 us -> 0.96 us  [body(): call(functools.partial(last_kernel, dims, depths), out_shape=f32(*dims),...]
    ppermute x6, starting transfers between devices: 12.2 us -> 13.2 us  [swap_bit(): return lax.ppermute(value, axis, [(i, i ^ 2 ** level) for i in range(n)])]
  transfers between devices with their start and end apart: 10 -> 10, of which waited for: 7 -> 6; matrix products, arithmetic and copies ran while one was open for 0% -> 0% of each run, Pallas kernels for 0% -> 0%
where the time goes in v2:
time: 39.8 us; the launch traced here: 39.6 us
  starting transfers between devices  22.7 us (57%)
  waiting for transfers between devices  12.8 us (32%)
  Pallas kernels  3.95 us (10%)
    ppermute x6, starting transfers between devices, swap_bit(): return lax.ppermute(value, axis, [(i, i ^ 2 ** level) for i in range(n)])  13.2 us
    ppermute x4, starting transfers between devices, shift(): lax.ppermute(value, axis, [(i, i + step) for i in range(n) if 0 <= i + st...  9.47 us
    ppermute x4, waiting for transfers between devices, shift(): lax.ppermute(value, axis, [(i, i + step) for i in range(n) if 0 <= i + st...  6.75 us
    ppermute x6, waiting for transfers between devices, swap_bit(): return lax.ppermute(value, axis, [(i, i ^ 2 ** level) for i in range(n)])  6.04 us
    pallas_call x1, Pallas kernels, body(): call(functools.partial(main_kernel, dims, counts, swap), out_shape=[f32(3...  2.73 us
    pallas_call x1, Pallas kernels, body(): call(functools.partial(last_kernel, dims, depths), out_shape=f32(*dims),...  0.96 us
  transfers between devices with their start and end apart: 10, of which 6 were waited for; matrix products, arithmetic and copies ran while one was open for 0% of the time, Pallas kernels for 0%

profile of v2, /device:TPU:0, one launch (start us, length us, event | category | flops | bytes accessed | tf_op | source)
XLA Modules:
  0.0 39.6 jit_solution(9521354386659699641)
XLA Ops:
  0.0 1.3 %collective-permute-start.1 = (f32[8,16,256]{2,1,0:T(8,128)}, f32[8,16,256]{2,1,0:T(8,128)S(1)}, u32[]{:S(2)}, u32[]{:S(2)}) collective-permute-start(f32[8,16,256]{2,1,0:T(8,128)} %refs_0_.1), channel_id=1, source_target_pairs={{1,0},{2,1},{3,2},{5,4},{6,5},{7,6},{9,8},{10,9},{11,10},{13,12},{... | collective-permute-start | bytes 393224 | tf_op jit(solution)/shard_map/ppermute | solution.py:457
  1.3 5.6 %collective-permute-start = (f32[8,16,256]{2,1,0:T(8,128)}, f32[8,16,256]{2,1,0:T(8,128)S(1)}, u32[]{:S(2)}, u32[]{:S(2)}) collective-permute-start(f32[8,16,256]{2,1,0:T(8,128)} %refs_0_.1), channel_id=1, source_target_pairs={{0,1},{1,2},{2,3},{4,5},{5,6},{6,7},{8,9},{9,10},{10,11},{12,13},{... | collective-permute-start | bytes 393224 | tf_op jit(solution)/shard_map/ppermute | solution.py:457
  6.9 1.8 %collective-permute-done.1.refs_2_ = f32[8,16,256]{2,1,0:T(8,128)S(1)} collective-permute-done((f32[8,16,256]{2,1,0:T(8,128)}, f32[8,16,256]{2,1,0:T(8,128)S(1)}, u32[]{:S(2)}, u32[]{:S(2)}) %collective-permute-start.1) | collective-permute-done | bytes 131104 | tf_op jit(solution)/shard_map/ppermute | solution.py:457
  8.7 0.0 copy-start
  8.7 1.3 %collective-permute-done.refs_0_ = f32[8,16,256]{2,1,0:T(8,128)S(1)} collective-permute-done((f32[8,16,256]{2,1,0:T(8,128)}, f32[8,16,256]{2,1,0:T(8,128)S(1)}, u32[]{:S(2)}, u32[]{:S(2)}) %collective-permute-start) | collective-permute-done | bytes 131104 | tf_op jit(solution)/shard_map/ppermute | solution.py:457
  9.9 0.0 copy-done
  10.0 1.8 %collective-permute-start.2 = (f32[20,8,256]{2,1,0:T(8,128)S(1)}, f32[20,8,256]{2,1,0:T(8,128)S(1)}, u32[]{:S(2)}, u32[]{:S(2)}) collective-permute-start(f32[20,8,256]{2,1,0:T(8,128)S(1)} %slice_select_fusion), channel_id=1, source_target_pairs={{0,16},{16,0},{1,17},{17,1},{2,18},{18,2},{3,19},{19,3},{4,20},{20... | collective-permute-start | bytes 491528 | tf_op jit(solution)/shard_map/ppermute | solution.py:462
  11.8 3.6 %collective-permute-done.2.refs_3_ = f32[20,8,256]{2,1,0:T(8,128)S(1)} collective-permute-done((f32[20,8,256]{2,1,0:T(8,128)S(1)}, f32[20,8,256]{2,1,0:T(8,128)S(1)}, u32[]{:S(2)}, u32[]{:S(2)}) %collective-permute-start.2) | collective-permute-done | bytes 163872 | tf_op jit(solution)/shard_map/ppermute | solution.py:462
  15.4 0.2 shard_map.17
  15.6 1.3 %collective-permute-start.3 = (f32[8,640]{1,0:T(8,128)S(1)}, f32[8,640]{1,0:T(8,128)S(1)}, u32[]{:S(2)}, u32[]{:S(2)}) collective-permute-start(f32[8,640]{1,0:T(8,128)S(1)} %get-tuple-element.16), channel_id=1, source_target_pairs={{0,4},{4,8},{8,12},{1,5},{5,9},{9,13},{2,6},{6,10},{10,14},{3,7},{... | collective-permute-start | bytes 61448 | tf_op jit(solution)/shard_map/ppermute | solution.py:457
  16.9 1.3 %collective-permute-start.4 = (f32[8,640]{1,0:T(8,128)S(1)}, f32[8,640]{1,0:T(8,128)S(1)}, u32[]{:S(2)}, u32[]{:S(2)}) collective-permute-start(f32[8,640]{1,0:T(8,128)S(1)} %get-tuple-element.17), channel_id=1, source_target_pairs={{4,0},{8,4},{12,8},{5,1},{9,5},{13,9},{6,2},{10,6},{14,10},{7,3},{... | collective-permute-start | bytes 61448 | tf_op jit(solution)/shard_map/ppermute | solution.py:457
  18.2 0.0 collective-permute-done.3.refs_4_
  18.2 3.7 %collective-permute-done.4.refs_5_ = f32[8,640]{1,0:T(8,128)S(1)} collective-permute-done((f32[8,640]{1,0:T(8,128)S(1)}, f32[8,640]{1,0:T(8,128)S(1)}, u32[]{:S(2)}, u32[]{:S(2)}) %collective-permute-start.4) | collective-permute-done | bytes 20512 | tf_op jit(solution)/shard_map/ppermute | solution.py:457
  22.0 2.7 %shard_map.18 = (f32[3,7,16,256]{3,2,1,0:T(8,128)S(1)}, f32[3,15,8,256]{3,2,1,0:T(8,128)S(1)}, f32[3,15,2,8,128]{4,3,2,1,0:T(8,128)S(1)}, f32[4,3,8,128]{3,2,1,0...) custom-call(f32[8,16,256]{2,1,0:T(8,128)S(1)} %collective-permute-done.refs_0_, ...), custom_call_target="tpu_custom_call" | custom-call | tf_op jit(solution)/shard_map/pallas_call | solution.py:501
  24.7 2.4 %collective-permute-start.5 = (f32[6,16,256]{2,1,0:T(8,128)S(1)}, f32[6,16,256]{2,1,0:T(8,128)S(1)}, u32[]{:S(2)}, u32[]{:S(2)}) collective-permute-start(f32[6,16,256]{2,1,0:T(8,128)S(1)} %get-tuple-element.22.refs_0_.refs_5_), channel_id=1, source_target_pairs={{0,1},{1,0},{2,3},{3,2},{4,5},{5,4},{6,7},{7,6},{8,9},{9,8},{10,11... | collective-permute-start | bytes 294920 | tf_op jit(solution)/shard_map/ppermute | solution.py:462
  27.1 2.2 %collective-permute-start.6 = (f32[8,128]{1,0:T(8,128)S(1)}, f32[8,128]{1,0:T(8,128)S(1)}, u32[]{:S(2)}, u32[]{:S(2)}) collective-permute-start(f32[8,128]{1,0:T(8,128)S(1)} %get-tuple-element.23.refs_2_.refs_10_), channel_id=1, source_target_pairs={{0,4},{4,0},{8,12},{12,8},{1,5},{5,1},{9,13},{13,9},{2,6},{6,2},{1... | collective-permute-start | bytes 12296 | tf_op jit(solution)/shard_map/ppermute | solution.py:462
  29.4 0.8 %collective-permute-done.6.refs_3_.refs_11_ = f32[8,128]{1,0:T(8,128)S(1)} collective-permute-done((f32[8,128]{1,0:T(8,128)S(1)}, f32[8,128]{1,0:T(8,128)S(1)}, u32[]{:S(2)}, u32[]{:S(2)}) %collective-permute-start.6) | collective-permute-done | bytes 4128 | tf_op jit(solution)/shard_map/ppermute | solution.py:462
  30.2 0.0 collective-permute-done.5.refs_1_.refs_6_
  30.2 2.7 %collective-permute-start.7 = (f32[2,16,256]{2,1,0:T(8,128)S(1)}, f32[2,16,256]{2,1,0:T(8,128)S(1)}, u32[]{:S(2)}, u32[]{:S(2)}) collective-permute-start(f32[2,16,256]{2,1,0:T(8,128)S(1)} %get-tuple-element.24), channel_id=1, source_target_pairs={{0,2},{1,3},{2,0},{3,1},{4,6},{5,7},{6,4},{7,5},{8,10},{9,11},{10,... | collective-permute-start | bytes 98312 | tf_op jit(solution)/shard_map/ppermute | solution.py:462
  32.9 1.5 %collective-permute-start.8 = (f32[2,8,256]{2,1,0:T(8,128)S(1)}, f32[2,8,256]{2,1,0:T(8,128)S(1)}, u32[]{:S(2)}, u32[]{:S(2)}) collective-permute-start(f32[2,8,256]{2,1,0:T(8,128)S(1)} %get-tuple-element.25.refs_8_), channel_id=1, source_target_pairs={{0,16},{16,0},{1,17},{17,1},{2,18},{18,2},{3,19},{19,3},{4,20},{20... | collective-permute-start | bytes 49160 | tf_op jit(solution)/shard_map/ppermute | solution.py:462
  34.4 2.7 %collective-permute-start.9 = (f32[8,128]{1,0:T(8,128)S(1)}, f32[8,128]{1,0:T(8,128)S(1)}, u32[]{:S(2)}, u32[]{:S(2)}) collective-permute-start(f32[8,128]{1,0:T(8,128)S(1)} %get-tuple-element.26), channel_id=1, source_target_pairs={{0,8},{4,12},{8,0},{12,4},{1,9},{5,13},{9,1},{13,5},{2,10},{6,14},... | collective-permute-start | bytes 12296 | tf_op jit(solution)/shard_map/ppermute | solution.py:462
  37.1 0.0 collective-permute-done.8.refs_9_
  37.1 1.6 %collective-permute-done.9.refs_12_ = f32[8,128]{1,0:T(8,128)S(1)} collective-permute-done((f32[8,128]{1,0:T(8,128)S(1)}, f32[8,128]{1,0:T(8,128)S(1)}, u32[]{:S(2)}, u32[]{:S(2)}) %collective-permute-start.9) | collective-permute-done | bytes 4128 | tf_op jit(solution)/shard_map/ppermute | solution.py:462
  38.6 0.0 collective-permute-done.7.refs_7_
  38.6 1.0 %shard_map.20 = f32[8,16,256]{2,1,0:T(8,128)} custom-call(f32[8,16,256]{2,1,0:T(8,128)S(1)} %copy-done, f32[3,7,16,256]{3,2,1,0:T(8,128)S(1)} %get-tuple-element.18.refs_1_, f32[3,15,8,256]{3,2,1,0:T(8,128)S(1)} %get-tuple-element.19.refs_2_, f32[3,15,2,8,128]{4,3,2,1,0:T(8,128)S(1)} %get-tuple-element.20.refs_3_, ...), custom_call_target="tpu_custom_call" | custom-call | tf_op jit(solution)/shard_map/pallas_call | solution.py:531
  (5 shorter events, 0.1 us)
Async XLA Ops:
  0.0 8.6 %collective-permute-start.1 = (f32[8,16,256]{2,1,0:T(8,128)}, f32[8,16,256]{2,1,0:T(8,128)S(1)}, u32[]{:S(2)}, u32[]{:S(2)}) collective-permute-start(f32[8,16,256]{2,1,0:T(8,128)} %refs_0_.1), channel_id=1, source_target_pairs={{1,0},{2,1},{3,2},{5,4},{6,5},{7,6},{9,8},{10,9},{11,10},{13,12},{... | collective-permute-start | bytes 393224 | tf_op jit(solution)/shard_map/ppermute | solution.py:457
  1.3 8.7 %collective-permute-start = (f32[8,16,256]{2,1,0:T(8,128)}, f32[8,16,256]{2,1,0:T(8,128)S(1)}, u32[]{:S(2)}, u32[]{:S(2)}) collective-permute-start(f32[8,16,256]{2,1,0:T(8,128)} %refs_0_.1), channel_id=1, source_target_pairs={{0,1},{1,2},{2,3},{4,5},{5,6},{6,7},{8,9},{9,10},{10,11},{12,13},{... | collective-permute-start | bytes 393224 | tf_op jit(solution)/shard_map/ppermute | solution.py:457
  8.7 1.3 %copy-start = (f32[8,16,256]{2,1,0:T(8,128)S(1)}, f32[8,16,256]{2,1,0:T(8,128)}, u32[]{:S(2)}) copy-start(f32[8,16,256]{2,1,0:T(8,128)} %refs_0_.1) | copy-start | bytes 393220
  10.0 5.4 %collective-permute-start.2 = (f32[20,8,256]{2,1,0:T(8,128)S(1)}, f32[20,8,256]{2,1,0:T(8,128)S(1)}, u32[]{:S(2)}, u32[]{:S(2)}) collective-permute-start(f32[20,8,256]{2,1,0:T(8,128)S(1)} %slice_select_fusion), channel_id=1, source_target_pairs={{0,16},{16,0},{1,17},{17,1},{2,18},{18,2},{3,19},{19,3},{4,20},{20... | collective-permute-start | bytes 491528 | tf_op jit(solution)/shard_map/ppermute | solution.py:462
  15.6 2.6 %collective-permute-start.3 = (f32[8,640]{1,0:T(8,128)S(1)}, f32[8,640]{1,0:T(8,128)S(1)}, u32[]{:S(2)}, u32[]{:S(2)}) collective-permute-start(f32[8,640]{1,0:T(8,128)S(1)} %get-tuple-element.16), channel_id=1, source_target_pairs={{0,4},{4,8},{8,12},{1,5},{5,9},{9,13},{2,6},{6,10},{10,14},{3,7},{... | collective-permute-start | bytes 61448 | tf_op jit(solution)/shard_map/ppermute | solution.py:457
  16.9 5.0 %collective-permute-start.4 = (f32[8,640]{1,0:T(8,128)S(1)}, f32[8,640]{1,0:T(8,128)S(1)}, u32[]{:S(2)}, u32[]{:S(2)}) collective-permute-start(f32[8,640]{1,0:T(8,128)S(1)} %get-tuple-element.17), channel_id=1, source_target_pairs={{4,0},{8,4},{12,8},{5,1},{9,5},{13,9},{6,2},{10,6},{14,10},{7,3},{... | collective-permute-start | bytes 61448 | tf_op jit(solution)/shard_map/ppermute | solution.py:457
  24.7 5.5 %collective-permute-start.5 = (f32[6,16,256]{2,1,0:T(8,128)S(1)}, f32[6,16,256]{2,1,0:T(8,128)S(1)}, u32[]{:S(2)}, u32[]{:S(2)}) collective-permute-start(f32[6,16,256]{2,1,0:T(8,128)S(1)} %get-tuple-element.22.refs_0_.refs_5_), channel_id=1, source_target_pairs={{0,1},{1,0},{2,3},{3,2},{4,5},{5,4},{6,7},{7,6},{8,9},{9,8},{10,11... | collective-permute-start | bytes 294920 | tf_op jit(solution)/shard_map/ppermute | solution.py:462
  27.1 3.1 %collective-permute-start.6 = (f32[8,128]{1,0:T(8,128)S(1)}, f32[8,128]{1,0:T(8,128)S(1)}, u32[]{:S(2)}, u32[]{:S(2)}) collective-permute-start(f32[8,128]{1,0:T(8,128)S(1)} %get-tuple-element.23.refs_2_.refs_10_), channel_id=1, source_target_pairs={{0,4},{4,0},{8,12},{12,8},{1,5},{5,1},{9,13},{13,9},{2,6},{6,2},{1... | collective-permute-start | bytes 12296 | tf_op jit(solution)/shard_map/ppermute | solution.py:462
  30.2 8.4 %collective-permute-start.7 = (f32[2,16,256]{2,1,0:T(8,128)S(1)}, f32[2,16,256]{2,1,0:T(8,128)S(1)}, u32[]{:S(2)}, u32[]{:S(2)}) collective-permute-start(f32[2,16,256]{2,1,0:T(8,128)S(1)} %get-tuple-element.24), channel_id=1, source_target_pairs={{0,2},{1,3},{2,0},{3,1},{4,6},{5,7},{6,4},{7,5},{8,10},{9,11},{10,... | collective-permute-start | bytes 98312 | tf_op jit(solution)/shard_map/ppermute | solution.py:462
  32.9 4.2 %collective-permute-start.8 = (f32[2,8,256]{2,1,0:T(8,128)S(1)}, f32[2,8,256]{2,1,0:T(8,128)S(1)}, u32[]{:S(2)}, u32[]{:S(2)}) collective-permute-start(f32[2,8,256]{2,1,0:T(8,128)S(1)} %get-tuple-element.25.refs_8_), channel_id=1, source_target_pairs={{0,16},{16,0},{1,17},{17,1},{2,18},{18,2},{3,19},{19,3},{4,20},{20... | collective-permute-start | bytes 49160 | tf_op jit(solution)/shard_map/ppermute | solution.py:462
  34.4 4.3 %collective-permute-start.9 = (f32[8,128]{1,0:T(8,128)S(1)}, f32[8,128]{1,0:T(8,128)S(1)}, u32[]{:S(2)}, u32[]{:S(2)}) collective-permute-start(f32[8,128]{1,0:T(8,128)S(1)} %get-tuple-element.26), channel_id=1, source_target_pairs={{0,8},{4,12},{8,0},{12,4},{1,9},{5,13},{9,1},{13,5},{2,10},{6,14},... | collective-permute-start | bytes 12296 | tf_op jit(solution)/shard_map/ppermute | solution.py:462

commit v3 on v2

--- a/solution.py
+++ b/solution.py
@@ -125,126 +125,98 @@
     emit(0, above + left)
 
 
-def strip_kernel(dims, swap, *refs):
-    nz, nx, ny = dims
-    if swap:
-        zlo, v, zhi, xr, first, last = refs
-        at_x = lax.axis_index("gx")
-        keep_lo = jnp.where(at_x == 1, 1.0, 0.0)
-        keep_hi = jnp.where(at_x == 0, 1.0, 0.0)
-    else:
-        zlo, v, zhi, xlo, xhi, first, last = refs
-    width = nx + 2 * edge
-    per = lanes // width
-
-    def row(z, t):
-        cols = slice(t * lanes, (t + 1) * lanes)
-        if z < halo:
-            mid = zlo[nz - halo + z, :, cols]
-        elif z < halo + nz:
-            mid = v[z - halo, :, cols]
-        else:
-            mid = zhi[z - halo - nz, :, cols]
-        if swap:
-            side = xr[z, :, cols]
-            return [side * keep_lo, mid, side * keep_hi]
-        return [xlo[z, :, cols], mid, xhi[z, :, cols]]
-
-    for t, out, begin in ((0, first, 0), (ny // lanes - 1, last, lanes - edge)):
-        for chunk in range((nz + 2 * halo) // per):
-            rows = []
-            for z in range(per):
-                rows += row(chunk * per + z, t)
-            turned = jnp.concatenate(rows, axis=0).T
-            out[:, chunk * lanes:(chunk + 1) * lanes] = turned[begin:begin + edge, :]
-
-
-def main_kernel(dims, counts, swap, *refs):
+def cut(t):
+    return slice(t * lanes, (t + 1) * lanes)
+
+
+def z_blur(load, store, count, weights):
+    window = [load(i) for i in range(4)]
+    for i in range(count):
+        window.append(load(i + 4))
+        store(i, five(weights, *window))
+        window.pop(0)
+
+
+def neighbours(position, refs, load):
+    odd = position % 2 == 1
+    first = load(refs[0])
+    second = load(refs[1]) if len(refs) > 1 else jnp.zeros_like(first)
+    return jnp.where(odd, first, second), jnp.where(odd, second, first)
+
+
+def z_kernel(dims, pairs, *refs):
+    nz, nx, ny = dims
+    v, zr = refs[0], refs[1:1 + pairs[0]]
+    out, *sends = refs[1 + pairs[0]:]
+    at_z, at_x = lax.axis_index("gz"), lax.axis_index("gx")
+    odd_x = at_x % 2 == 1
+    for t in range(ny // lanes):
+        cols = cut(t)
+        below, above = {}, {}
+        for z in range(halo):
+            odd = at_z % 2 == 1
+            first_top, first_low = zr[0][nz - halo + z, :, cols], zr[0][z, :, cols]
+            if len(zr) > 1:
+                second_top, second_low = zr[1][nz - halo + z, :, cols], zr[1][z, :, cols]
+            else:
+                second_top = second_low = jnp.zeros_like(first_low)
+            below[z] = jnp.where(odd, first_top, second_top)
+            above[z] = jnp.where(odd, second_low, first_low)
+
+        def load(z):
+            if z < halo:
+                return below[z]
+            return v[z - halo, :, cols] if z < halo + nz else above[z - halo - nz]
+
+        def store(i, value):
+            out[t, i] = value
+            low, high = value[:halo], value[nx - halo:]
+            rows = slice(i * halo, (i + 1) * halo)
+            sends[0][rows, cols] = jnp.where(odd_x, low, high)
+            if len(sends) > 1:
+                sends[1][rows, cols] = jnp.where(odd_x, high, low)
+
+        z_blur(load, store, nz + 8, taps())
+
+
+def x_kernel(dims, pairs, *refs):
+    nz, nx, ny = dims
+    zb, xr = refs[0], refs[1:1 + pairs[1]]
+    out, *rest = refs[1 + pairs[1]:]
+    sends, wide = rest[:-1], rest[-1]
+    at_x, at_y = lax.axis_index("gx"), lax.axis_index("gy")
+    nt, nb, rows_b = ny // lanes, nz + 8, nx + 8
+    k = taps()
+    for t in range(nt):
+        for i in range(nb):
+            rows = slice(i * halo, (i + 1) * halo)
+            low, high = neighbours(at_x, xr, lambda ref: ref[rows, cut(t)])
+            wide[i, edge - halo:edge, :] = low
+            wide[i, edge:edge + nx, :] = zb[t, i]
+            wide[i, edge + nx:edge + nx + halo, :] = high
+        for i in range(nb):
+            out[t, i] = five(k, *[wide[i, 2 + o:2 + o + rows_b, :] for o in range(5)])
+    odd_y = at_y % 2 == 1
+    flat = lambda t, chunk: out.at[t].reshape(nb * rows_b, lanes)[chunk * lanes:(chunk + 1) * lanes, :]
+    for chunk in range(nb * rows_b // lanes):
+        first = flat(0, chunk).T[:edge, :]
+        last = flat(nt - 1, chunk).T[lanes - edge:, :]
+        sends[0][:, cut(chunk)] = jnp.where(odd_y, first, last)
+        if len(sends) > 1:
+            sends[1][:, cut(chunk)] = jnp.where(odd_y, last, first)
+
+
+def grid_masks(dims, counts):
     nz, nx, ny = dims
     nt = ny // lanes
-    own = tuple(range(nt))
-    every = tuple(range(nt + 1))
-    lines = nz * nx
-    if swap:
-        zlo, v, zhi, xr, yl, yr = refs[:6]
-        refs = refs[6:]
-    else:
-        zlo, v, zhi, xlo, xhi, yl, yr = refs[:7]
-        refs = refs[7:]
-    (fz, fx, fy, cy_out, send_z, send_x, send_y,
-     wh, zp, bb, t1, dxs, vs, cz, cxs, cys, ct, vt) = refs
     at_z, at_x, at_y = lax.axis_index("gz"), lax.axis_index("gx"), lax.axis_index("gy")
-    width = nx + 2 * edge
     rows_b = nx + 8
-    per = lanes // width
-    k = taps()
-    kt = taps(0.25 / (contrast * contrast))
-    if swap:
-        keep_lo = jnp.where(at_x == 1, 1.0, 0.0)
-        keep_hi = jnp.where(at_x == 0, 1.0, 0.0)
-
-    gap = jnp.zeros((lanes - 2 * edge, lanes), jnp.float32)
-    for chunk in range((nz + 2 * halo) // per):
-        cols = slice(chunk * lanes, (chunk + 1) * lanes)
-        turned = jnp.concatenate([yr[:, cols], gap, yl[:, cols]], axis=0).T
-        for z in range(per):
-            wh[chunk * per + z] = turned[z * width:(z + 1) * width, :]
-
-    def centre(z, t):
-        cols = slice(t * lanes, (t + 1) * lanes)
-        if z < halo:
-            return zlo[nz - halo + z, :, cols]
-        if z < halo + nz:
-            return v[z - halo, :, cols]
-        return zhi[z - halo - nz, :, cols]
-
-    def z_blur(load, store, count, weights):
-        window = [load(i) for i in range(4)]
-        for i in range(count):
-            window.append(load(i + 4))
-            store(i, five(weights, *window))
-            window.pop(0)
-
-    nb = nz + 8
-    for t in own:
-        cols = slice(t * lanes, (t + 1) * lanes)
-
-        def put(rows, scale=None, t=t):
-            def store(i, value):
-                zp[t, i, rows, :] = value if scale is None else value * scale
-            return store
-
-        z_blur(lambda z: centre(z, t), put(slice(edge, edge + nx)), nb, k)
-        if swap:
-            def both(i, value):
-                zp[t, i, 0:edge, :] = value * keep_lo
-                zp[t, i, edge + nx:width, :] = value * keep_hi
-            z_blur(lambda z: xr[z, :, cols], both, nb, k)
-        else:
-            z_blur(lambda z: xlo[z, :, cols], put(slice(0, edge)), nb, k)
-            z_blur(lambda z: xhi[z, :, cols], put(slice(edge + nx, width)), nb, k)
-
-    def put_h(i, value):
-        zp[nt, i] = value
-    z_blur(lambda z: wh[z], put_h, nb, k)
-
-    blank = jnp.zeros((edge, lanes), jnp.float32)
-    for z in range(nb):
-        along_x = [five(k, *[zp[t, z, 2 + o:2 + o + rows_b, :] for o in range(5)]) for t in every]
-        done = lane_blur(k, along_x, every)
-        for t in every:
-            bb[t, z, 0:edge, :] = blank
-            bb[t, z, edge:edge + rows_b, :] = done[t]
-            bb[t, z, edge + rows_b:, :] = blank
-
     xi = at_x * nx + lax.broadcasted_iota(jnp.int32, (rows_b, lanes), 0) - 4
-    x_in = (xi >= 0) & (xi < nx * counts[1])
+    x_mask = jnp.where((xi >= 0) & (xi < nx * counts[1]), 1.0, 0.0)
     lane = lax.broadcasted_iota(jnp.int32, (rows_b, lanes), 1)
     not_first = (at_y > 0).astype(jnp.float32)
     not_last = (at_y < counts[2] - 1).astype(jnp.float32)
-    y_in = jnp.where(lane < lanes // 2, not_last, not_first)
-    x_mask = jnp.where(x_in, 1.0, 0.0)
-    masks = [x_mask] * nt + [x_mask * y_in]
+    masks = [x_mask] * nt + [x_mask * jnp.where(lane < lanes // 2, not_last, not_first)]
 
     def z_mask(z, value):
         if 0 <= z < nz:
@@ -252,36 +224,65 @@
         inside = (at_z > 0) if z < 0 else (at_z < counts[0] - 1)
         return value * inside.astype(jnp.float32)
 
-    def tensor(square, count):
+    return masks, z_mask
+
+
+def tensor(t1, every, rows_b, square, count):
+    kt = taps(0.25 / (contrast * contrast))
+    for t in every:
+        window = [square(t, z) for z in range(-2, 2)]
+        for i in range(count):
+            window.append(square(t, i + 2))
+            t1[t, i, 0:rows_b, :] = five(kt, *window)
+            window.pop(0)
+
+
+def finish(t1, every, z, rows, wanted):
+    k = taps()
+    along_x = [five(k, *[t1[t, z, 2 + o:2 + o + rows, :] for o in range(5)]) for t in every]
+    return [1.0 / (1.0 + value) for value in lane_blur(k, along_x, wanted)]
+
+
+def main_kernel(dims, counts, pairs, *refs):
+    nz, nx, ny = dims
+    nt = ny // lanes
+    own, every = tuple(range(nt)), tuple(range(nt + 1))
+    v, xb, yr = refs[0], refs[1], refs[2:2 + pairs[2]]
+    bb, fz, send_z, wh, t1, cz = refs[2 + pairs[2]:]
+    at_z, at_y = lax.axis_index("gz"), lax.axis_index("gy")
+    nb, rows_b = nz + 8, nx + 8
+    k = taps()
+
+    gap = jnp.zeros((lanes - 2 * edge, lanes), jnp.float32)
+    for chunk in range(nb * rows_b // lanes):
+        low, high = neighbours(at_y, yr, lambda ref: ref[:, cut(chunk)])
+        wh[chunk * lanes:(chunk + 1) * lanes, :] = jnp.concatenate([high, gap, low], axis=0).T
+
+    blank = jnp.zeros((edge, lanes), jnp.float32)
+    for z in range(nb):
+        tiles = [xb[t, z] for t in own] + [wh[z * rows_b:(z + 1) * rows_b, :]]
+        done = lane_blur(k, tiles, every)
         for t in every:
-            window = [square(t, z) for z in range(-2, 2)]
-            for i in range(count):
-                window.append(square(t, i + 2))
-                t1[t, i, 0:rows_b, :] = five(kt, *window)
-                window.pop(0)
-
-    def finish(z, first_row, rows, wanted):
-        along_x = [five(k, *[t1[t, z, first_row + o:first_row + o + rows, :] for o in range(5)]) for t in every]
-        return [1.0 / (1.0 + value) for value in lane_blur(k, along_x, wanted)]
-
-    for t in every:
-        for z in range(nz + 1):
-            t1[t, z, rows_b:, :] = blank
+            bb[t, z, 0:edge, :] = blank
+            bb[t, z, edge:edge + rows_b, :] = done[t]
+            bb[t, z, edge + rows_b:, :] = blank
+
+    masks, z_mask = grid_masks(dims, counts)
 
     def square_z(t, z):
         slope = bb[t, z + 5, edge:edge + rows_b, :] - bb[t, z + 3, edge:edge + rows_b, :]
         return z_mask(z, slope * slope * masks[t])
 
-    tensor(square_z, nz + 1)
+    tensor(t1, every, rows_b, square_z, nz + 1)
     before = None
     for z in range(nz + 1):
-        here = finish(z, 2, nx, own)
+        here = finish(t1, every, z, nx, own)
         if before is not None:
             scale = 0.5 * stiffness
             if z == nz:
                 scale = jnp.where(at_z < counts[0] - 1, scale, 0.0)
             for t in own:
-                cz[z - 1, :, t * lanes:(t + 1) * lanes] = (before[t] + here[t]) * scale
+                cz[z - 1, :, cut(t)] = (before[t] + here[t]) * scale
         before = here
 
     def keep_z(i, w, d, h):
@@ -291,26 +292,40 @@
     for i, value in enumerate(seg if counts[0] > 2 else last_message(bit_of(at_z, 0), seg)):
         send_z[i] = value
 
+
+def side_kernel(dims, counts, *refs):
+    nz, nx, ny = dims
+    nt = ny // lanes
+    own, every = tuple(range(nt)), tuple(range(nt + 1))
+    v, bb, fx, fy, cy_out, send_x, send_y, t1, dxs, vs, cxs, cys, ct, vt = refs
+    at_x, at_y = lax.axis_index("gx"), lax.axis_index("gy")
+    rows_b = nx + 8
+    masks, z_mask = grid_masks(dims, counts)
+    kt = taps(0.25 / (contrast * contrast))
+    blank = jnp.zeros((edge, lanes), jnp.float32)
+    for t in every:
+        for z in range(nz):
+            t1[t, z, rows_b:, :] = blank
+
     def square_x(t, z):
         slope = bb[t, z + 4, edge + 1:edge + 1 + rows_b, :] - bb[t, z + 4, edge - 1:edge - 1 + rows_b, :]
         return z_mask(z, slope * slope * masks[t])
 
-    tensor(square_x, nz)
+    tensor(t1, every, rows_b, square_x, nz)
     for z in range(nz):
-        here = finish(z, 2, rows_b, own)
+        here = finish(t1, every, z, rows_b, own)
         for t in own:
             dxs[t, z * rows_b:(z + 1) * rows_b, :] = here[t]
-            vs[t, z * nx:(z + 1) * nx, :] = v[z, :, t * lanes:(t + 1) * lanes]
+            vs[t, z * nx:(z + 1) * nx, :] = v[z, :, cut(t)]
     for t in own:
-        cols = slice(t * lanes, (t + 1) * lanes)
         here = dxs[t, pl.ds(0, nz, stride=rows_b), :]
         for x in range(nx):
             following = dxs[t, pl.ds(x + 1, nz, stride=rows_b), :]
             scale = 0.5 * stiffness
             if x == nx - 1:
                 scale = jnp.where(at_x < counts[1] - 1, scale, 0.0)
-            cxs[0, x, :, cols] = (here + following) * scale
-            cxs[1, x, :, cols] = vs[t, pl.ds(x, nz, stride=nx), :]
+            cxs[0, x, :, cut(t)] = (here + following) * scale
+            cxs[1, x, :, cut(t)] = vs[t, pl.ds(x, nz, stride=nx), :]
             here = following
 
     def keep_x(i, w, d, h):
@@ -336,7 +351,7 @@
             t1[t, z, 0:rows_b, :] = five(kt, *[layer[t] for layer in window])
         window.pop(0)
     for z in range(nz):
-        here = finish(z, 2, nx, every)
+        here = finish(t1, every, z, nx, every)
         following = lane_shift(here, 1, own)
         for t in own:
             cys[t, z * nx:(z + 1) * nx, :] = (here[t] + following[t]) * (0.5 * stiffness)
@@ -452,14 +467,18 @@
             out[z, :, cols] = v[z, :, cols] + total * (1.0 / 3.0)
 
 
-def shift(value, axis, step):
-    n = lax.axis_size(axis)
-    return lax.ppermute(value, axis, [(i, i + step) for i in range(n) if 0 <= i + step < n])
-
-
 def swap_bit(value, axis, level):
     n = lax.axis_size(axis)
     return lax.ppermute(value, axis, [(i, i ^ (2**level)) for i in range(n)])
+
+
+def swap_pairs(values, axis):
+    n = lax.axis_size(axis)
+    out = []
+    for start, value in enumerate(values):
+        lows = range(start, n - 1, 2)
+        out.append(lax.ppermute(value, axis, [(i, i + 1) for i in lows] + [(i + 1, i) for i in lows]))
+    return out
 
 
 def body(volume):
@@ -469,45 +488,45 @@
     names = ("gz", "gx", "gy")
     counts = tuple(lax.axis_size(name) for name in names)
     depths = tuple(count.bit_length() - 1 for count in counts)
+    pairs = tuple(1 if count == 2 else 2 for count in counts)
+    nb, rows_b = nz + 8, nx + 8
     assert all(2**d == n and d >= 1 for d, n in zip(depths, counts))
-    assert nz == 8 and nz * nx == lanes and nx >= 8
-    swap = counts[1] == 2
+    assert nz == 8 and nz * nx == lanes and nx >= 8 and nb * rows_b % lanes == 0
     f32 = lambda *shape: jax.ShapeDtypeStruct(shape, jnp.float32)
     scratch = lambda *shape: pltpu.VMEM(shape, jnp.float32)
-    call = functools.partial(pl.pallas_call, compiler_params=pltpu.CompilerParams(vmem_limit_bytes=16 * 2**20))
-
-    zlo = shift(volume, "gz", 1)
-    zhi = shift(volume, "gz", -1)
-    tall = jnp.concatenate([zlo[nz - halo:], volume, zhi[:halo]], axis=0)
-    low_rows, high_rows = tall[:, :edge], tall[:, nx - edge:]
-    if swap:
-        sides = [swap_bit(jnp.where(lax.axis_index("gx") == 0, high_rows, low_rows), "gx", 0)]
-    else:
-        sides = [shift(high_rows, "gx", 1), shift(low_rows, "gx", -1)]
-    high = nz + 2 * halo
-    width = nx + 2 * edge
-    flat = high * width
-    first, last = call(
-        functools.partial(strip_kernel, dims, swap),
-        out_shape=[f32(edge, flat)] * 2,
-        in_specs=[VMEM] * (3 + len(sides)), out_specs=[VMEM] * 2,
-    )(zlo, volume, zhi, *sides)
-    yl = shift(last, "gy", 1)
-    yr = shift(first, "gy", -1)
+
+    def call(kernel, out_shape, scratch_shapes, *args):
+        return pl.pallas_call(
+            kernel, out_shape=out_shape, in_specs=[VMEM] * len(args), out_specs=[VMEM] * len(out_shape),
+            scratch_shapes=scratch_shapes,
+            compiler_params=pltpu.CompilerParams(vmem_limit_bytes=16 * 2**20),
+        )(*args)
+
+    z_received = swap_pairs([volume] * pairs[0], "gz")
+    blurred_z, *x_sends = call(
+        functools.partial(z_kernel, dims, pairs),
+        [f32(nt, nb, nx, lanes)] + [f32(nb * halo, ny)] * pairs[1], [], volume, *z_received)
+    x_received = swap_pairs(x_sends, "gx")
+    blurred_x, *y_sends = call(
+        functools.partial(x_kernel, dims, pairs),
+        [f32(nt, nb, rows_b, lanes)] + [f32(edge, nb * rows_b)] * pairs[2],
+        [scratch(nb, nx + 2 * edge, lanes)], blurred_z, *x_received)
+    y_received = swap_pairs(y_sends, "gy")
 
     steps = ny // 16
     send_shape = lambda d: 6 if d > 1 else 2
-    rows_b = nx + 8
-    fz, fx, fy, cy, send_z, send_x, send_y = call(
-        functools.partial(main_kernel, dims, counts, swap),
-        out_shape=[f32(3, nz - 1, nx, ny), f32(3, nx - 1, nz, ny), f32(3, steps - 1, 2, 8, lanes), f32(4, 3, 8, lanes),
-                   f32(send_shape(depths[0]), nx, ny), f32(send_shape(depths[1]), nz, ny), f32(8, lanes)],
-        in_specs=[VMEM] * (5 + len(sides)), out_specs=[VMEM] * 7,
-        scratch_shapes=[scratch(high, width, lanes), scratch(nt + 1, nz + 8, width, lanes),
-                        scratch(nt + 1, nz + 8, rows_b + 2 * edge, lanes), scratch(nt + 1, nz + 1, rows_b + 8, lanes),
-                        scratch(nt, nz * rows_b, lanes), scratch(nt, lanes, lanes), scratch(nz, nx, ny),
-                        scratch(2, nx, nz, ny), scratch(nt, lanes, lanes), scratch(ny, lanes), scratch(ny, lanes)],
-    )(zlo, volume, zhi, *sides, yl, yr)
+    bb, fz, send_z = call(
+        functools.partial(main_kernel, dims, counts, pairs),
+        [f32(nt + 1, nb, rows_b + 2 * edge, lanes), f32(3, nz - 1, nx, ny), f32(send_shape(depths[0]), nx, ny)],
+        [scratch(nb * rows_b, lanes), scratch(nt + 1, nz + 1, rows_b + 8, lanes), scratch(nz, nx, ny)],
+        volume, blurred_x, *y_received)
+    fx, fy, cy, send_x, send_y = call(
+        functools.partial(side_kernel, dims, counts),
+        [f32(3, nx - 1, nz, ny), f32(3, steps - 1, 2, 8, lanes), f32(4, 3, 8, lanes),
+         f32(send_shape(depths[1]), nz, ny), f32(8, lanes)],
+        [scratch(nt + 1, nz, rows_b + 8, lanes), scratch(nt, nz * rows_b, lanes), scratch(nt, lanes, lanes),
+         scratch(2, nx, nz, ny), scratch(nt, lanes, lanes), scratch(ny, lanes), scratch(ny, lanes)],
+        volume, bb)
 
     groups = [[send_z], [send_x], [send_y]]
     message = [send_z, send_x, send_y]
@@ -521,19 +540,14 @@
             for axis in axes:
                 count = 2 if depths[axis] == level + 2 else 6
                 shapes.append(f32(8, lanes) if axis == 2 else f32(count, *((nx, ny) if axis == 0 else (nz, ny))))
-            sent = call(
-                functools.partial(merge_kernel, level, counts, depths, axes),
-                out_shape=shapes,
-                in_specs=[VMEM] * (len(axes) * (level + 2)), out_specs=[VMEM] * len(axes),
-            )(*[ref for axis in axes for ref in groups[axis]])
+            sent = call(functools.partial(merge_kernel, level, counts, depths, axes), shapes, [],
+                        *[ref for axis in axes for ref in groups[axis]])
             for axis, value in zip(axes, sent):
                 message[axis] = value
     return call(
-        functools.partial(last_kernel, dims, depths),
-        out_shape=f32(*dims),
-        in_specs=[VMEM] * (5 + sum(len(g) for g in groups)), out_specs=VMEM,
-        scratch_shapes=[scratch(*dims), scratch(ny, lanes), scratch(nt, lanes, lanes)],
-    )(volume, fz, fx, fy, cy, *groups[0], *groups[1], *groups[2])
+        functools.partial(last_kernel, dims, depths), [f32(*dims)],
+        [scratch(*dims), scratch(ny, lanes), scratch(nt, lanes, lanes)],
+        volume, fz, fx, fy, cy, *groups[0], *groups[1], *groups[2])[0]
 
 
 def solution(mesh):

time: 39.8 us -> 35.3 us (0.89)
  waiting for transfers between devices: 12.8 us -> 8.91 us
  starting transfers between devices: 22.7 us -> 21.5 us
  local copies, waits for them, and re-layouts: 0.02 us -> 0.91 us
    ppermute x6 -> x5, waiting for transfers between devices: 6.04 us -> 2.41 us  [swap_bit(): return lax.ppermute(value, axis, [(i, i ^ 2 ** level) for i in range(n)])]
    ppermute x4 -> x5, starting transfers between devices: 9.47 us -> 6.17 us  [swap_pairs(): lax.ppermute(value, axis, [(i, i + 1) for i in lows] + [(i + 1, i) for i...]
    ppermute x6 -> x5, starting transfers between devices: 13.2 us -> 15.3 us  [swap_bit(): return lax.ppermute(value, axis, [(i, i ^ 2 ** level) for i in range(n)])]
    unnamed x2 -> x4, local copies, waits for them, and re-layouts: 0.01 us -> 0.91 us
    ppermute x4 -> x5, waiting for transfers between devices: 6.75 us -> 6.5 us  [swap_pairs(): lax.ppermute(value, axis, [(i, i + 1) for i in lows] + [(i + 1, i) for i...]
    pallas_call x4 -> x6, Pallas kernels: 3.95 us -> 3.77 us  [call(): pl.pallas_call(kernel, out_shape=out_shape, in_specs=[VMEM] * len(args),...]
  transfers between devices with their start and end apart: 10 -> 10, of which waited for: 6 -> 5; matrix products, arithmetic and copies ran while one was open for 0% -> 0% of each run, Pallas kernels for 0% -> 4%
where the time goes in v3:
time: 35.3 us; the launch traced here: 35.1 us
  starting transfers between devices  21.5 us (61%)
  waiting for transfers between devices  8.91 us (25%)
  Pallas kernels  3.77 us (11%)
  local copies, waits for them, and re-layouts  0.91 us (3%)
    ppermute x5, starting transfers between devices, swap_bit(): return lax.ppermute(value, axis, [(i, i ^ 2 ** level) for i in range(n)])  15.3 us
    ppermute x5, waiting for transfers between devices, swap_pairs(): lax.ppermute(value, axis, [(i, i + 1) for i in lows] + [(i + 1, i) for i...  6.5 us
    ppermute x5, starting transfers between devices, swap_pairs(): lax.ppermute(value, axis, [(i, i + 1) for i in lows] + [(i + 1, i) for i...  6.17 us
    pallas_call x6, Pallas kernels, call(): pl.pallas_call(kernel, out_shape=out_shape, in_specs=[VMEM] * len(args),...  3.77 us
    ppermute x5, waiting for transfers between devices, swap_bit(): return lax.ppermute(value, axis, [(i, i ^ 2 ** level) for i in range(n)])  2.41 us
    unnamed x4, local copies, waits for them, and re-layouts  0.91 us
  transfers between devices with their start and end apart: 10, of which 5 were waited for; matrix products, arithmetic and copies ran while one was open for 0% of the time, Pallas kernels for 4%

profile of v3, /device:TPU:0, one launch (start us, length us, event | category | flops | bytes accessed | tf_op | source)
XLA Modules:
  0.0 35.1 jit_solution(16537774881713375166)
XLA Ops:
  0.0 3.1 %collective-permute-start = (f32[8,16,256]{2,1,0:T(8,128)}, f32[8,16,256]{2,1,0:T(8,128)S(1)}, u32[]{:S(2)}, u32[]{:S(2)}) collective-permute-start(f32[8,16,256]{2,1,0:T(8,128)} %refs_0_.7), channel_id=1, source_target_pairs={{0,1},{2,3},{1,0},{3,2},{4,5},{6,7},{5,4},{7,6},{8,9},{10,11},{9,8... | collective-permute-start | bytes 393224 | tf_op jit(solution)/shard_map/ppermute | solution.py:480
  3.1 0.7 %collective-permute-start.1 = (f32[8,16,256]{2,1,0:T(8,128)}, f32[8,16,256]{2,1,0:T(8,128)S(1)}, u32[]{:S(2)}, u32[]{:S(2)}) collective-permute-start(f32[8,16,256]{2,1,0:T(8,128)} %refs_0_.7), channel_id=1, source_target_pairs={{1,2},{2,1},{5,6},{6,5},{9,10},{10,9},{13,14},{14,13},{17,18},{18,... | collective-permute-start | bytes 393224 | tf_op jit(solution)/shard_map/ppermute | solution.py:480
  3.7 3.0 %collective-permute-done.refs_1_ = f32[8,16,256]{2,1,0:T(8,128)S(1)} collective-permute-done((f32[8,16,256]{2,1,0:T(8,128)}, f32[8,16,256]{2,1,0:T(8,128)S(1)}, u32[]{:S(2)}, u32[]{:S(2)}) %collective-permute-start) | collective-permute-done | bytes 131104 | tf_op jit(solution)/shard_map/ppermute | solution.py:480
  6.8 0.0 collective-permute-done.1.refs_2_
  6.8 0.0 copy-start
  6.8 0.9 %copy-done = f32[8,16,256]{2,1,0:T(8,128)S(1)} copy-done((f32[8,16,256]{2,1,0:T(8,128)S(1)}, f32[8,16,256]{2,1,0:T(8,128)}, u32[]{:S(2)}) %copy-start) | copy-done | bytes 131096
  7.7 0.1 shard_map.17
  7.8 1.7 %collective-permute-start.2 = (f32[96,256]{1,0:T(8,128)S(1)}, f32[96,256]{1,0:T(8,128)S(1)}, u32[]{:S(2)}, u32[]{:S(2)}) collective-permute-start(f32[96,256]{1,0:T(8,128)S(1)} %get-tuple-element.21), channel_id=1, source_target_pairs={{0,16},{16,0},{1,17},{17,1},{2,18},{18,2},{3,19},{19,3},{4,20},{20... | collective-permute-start | bytes 294920 | tf_op jit(solution)/shard_map/ppermute | solution.py:480
  9.5 3.0 %collective-permute-done.2.refs_1_ = f32[96,256]{1,0:T(8,128)S(1)} collective-permute-done((f32[96,256]{1,0:T(8,128)S(1)}, f32[96,256]{1,0:T(8,128)S(1)}, u32[]{:S(2)}, u32[]{:S(2)}) %collective-permute-start.2) | collective-permute-done | bytes 98336 | tf_op jit(solution)/shard_map/ppermute | solution.py:480
  12.4 0.0 copy-start.1
  12.4 0.2 shard_map.18
  12.7 0.1 collective-permute-start.3
  12.8 0.7 %collective-permute-start.4 = (f32[8,384]{1,0:T(8,128)S(1)}, f32[8,384]{1,0:T(8,128)S(1)}, u32[]{:S(2)}, u32[]{:S(2)}) collective-permute-start(f32[8,384]{1,0:T(8,128)S(1)} %get-tuple-element.24), channel_id=1, source_target_pairs={{4,8},{8,4},{5,9},{9,5},{6,10},{10,6},{7,11},{11,7},{20,24},{24,20... | collective-permute-start | bytes 36872 | tf_op jit(solution)/shard_map/ppermute | solution.py:480
  13.4 0.5 %collective-permute-done.3.refs_2_ = f32[8,384]{1,0:T(8,128)S(1)} collective-permute-done((f32[8,384]{1,0:T(8,128)S(1)}, f32[8,384]{1,0:T(8,128)S(1)}, u32[]{:S(2)}, u32[]{:S(2)}) %collective-permute-start.3) | collective-permute-done | bytes 12320 | tf_op jit(solution)/shard_map/ppermute | solution.py:480
  13.9 0.0 collective-permute-done.4.refs_3_
  13.9 0.0 copy-done.1
  13.9 1.0 %shard_map.19 = (f32[3,16,40,128]{3,2,1,0:T(8,128)S(1)}, f32[3,7,16,256]{3,2,1,0:T(8,128)S(1)}, f32[6,16,256]{2,1,0:T(8,128)S(1)}) custom-call(f32[8,16,256]{2,1,0:T(8,128)S(1)} %copy-done.1, f32[2,16,24,128]{3,2,1,0:T(8,128)S(1)} %get-tuple-element.22.refs_1_, f32[8,384]{1,0:T(8,128)S(1)} %collective-permute-done.3.refs_2_, ...), custom_call_target="tpu_custom_call" | custom-call | tf_op jit(solution)/shard_map/pallas_call | solution.py:499
  15.0 4.8 %collective-permute-start.5 = (f32[6,16,256]{2,1,0:T(8,128)S(1)}, f32[6,16,256]{2,1,0:T(8,128)S(1)}, u32[]{:S(2)}, u32[]{:S(2)}) collective-permute-start(f32[6,16,256]{2,1,0:T(8,128)S(1)} %get-tuple-element.30.refs_0_.refs_5_), channel_id=1, source_target_pairs={{0,1},{1,0},{2,3},{3,2},{4,5},{5,4},{6,7},{7,6},{8,9},{9,8},{10,11... | collective-permute-start | bytes 294920 | tf_op jit(solution)/shard_map/ppermute | solution.py:472
  19.8 1.4 %shard_map.20 = (f32[3,15,8,256]{3,2,1,0:T(8,128)S(1)}, f32[3,15,2,8,128]{4,3,2,1,0:T(8,128)S(1)}, f32[4,3,8,128]{3,2,1,0:T(8,128)S(1)}, f32[2,8,256]{2,1,0:T(8,128)S(1)}, f32[8,128]{1,0:T(8,128)S(1)}) custom-call(f32[8,16,256]{2,1,0:T(8,128)S(1)} %copy-done.1, f32[3,16,40,128]{3,2,1,0:T(8,128)S(1)} %get-tuple-element.26.refs_1_), custom_call_target="tpu_custom_call" | custom-call | tf_op jit(solution)/shard_map/pallas_call | solution.py:499
  21.2 4.1 %collective-permute-start.6 = (f32[8,128]{1,0:T(8,128)S(1)}, f32[8,128]{1,0:T(8,128)S(1)}, u32[]{:S(2)}, u32[]{:S(2)}) collective-permute-start(f32[8,128]{1,0:T(8,128)S(1)} %get-tuple-element.31.refs_2_.refs_10_), channel_id=1, source_target_pairs={{0,4},{4,0},{8,12},{12,8},{1,5},{5,1},{9,13},{13,9},{2,6},{6,2},{1... | collective-permute-start | bytes 12296 | tf_op jit(solution)/shard_map/ppermute | solution.py:472
  25.3 0.8 %collective-permute-done.6.refs_3_.refs_11_ = f32[8,128]{1,0:T(8,128)S(1)} collective-permute-done((f32[8,128]{1,0:T(8,128)S(1)}, f32[8,128]{1,0:T(8,128)S(1)}, u32[]{:S(2)}, u32[]{:S(2)}) %collective-permute-start.6) | collective-permute-done | bytes 4128 | tf_op jit(solution)/shard_map/ppermute | solution.py:472
  26.2 0.0 collective-permute-done.5.refs_1_.refs_6_
  26.2 1.5 %collective-permute-start.7 = (f32[2,16,256]{2,1,0:T(8,128)S(1)}, f32[2,16,256]{2,1,0:T(8,128)S(1)}, u32[]{:S(2)}, u32[]{:S(2)}) collective-permute-start(f32[2,16,256]{2,1,0:T(8,128)S(1)} %get-tuple-element.32), channel_id=1, source_target_pairs={{0,2},{1,3},{2,0},{3,1},{4,6},{5,7},{6,4},{7,5},{8,10},{9,11},{10,... | collective-permute-start | bytes 98312 | tf_op jit(solution)/shard_map/ppermute | solution.py:472
  27.7 1.5 %collective-permute-start.8 = (f32[2,8,256]{2,1,0:T(8,128)S(1)}, f32[2,8,256]{2,1,0:T(8,128)S(1)}, u32[]{:S(2)}, u32[]{:S(2)}) collective-permute-start(f32[2,8,256]{2,1,0:T(8,128)S(1)} %get-tuple-element.33.refs_8_), channel_id=1, source_target_pairs={{0,16},{16,0},{1,17},{17,1},{2,18},{18,2},{3,19},{19,3},{4,20},{20... | collective-permute-start | bytes 49160 | tf_op jit(solution)/shard_map/ppermute | solution.py:472
  29.2 3.3 %collective-permute-start.9 = (f32[8,128]{1,0:T(8,128)S(1)}, f32[8,128]{1,0:T(8,128)S(1)}, u32[]{:S(2)}, u32[]{:S(2)}) collective-permute-start(f32[8,128]{1,0:T(8,128)S(1)} %get-tuple-element.34), channel_id=1, source_target_pairs={{0,8},{4,12},{8,0},{12,4},{1,9},{5,13},{9,1},{13,5},{2,10},{6,14},... | collective-permute-start | bytes 12296 | tf_op jit(solution)/shard_map/ppermute | solution.py:472
  32.6 0.0 collective-permute-done.8.refs_9_
  32.6 1.6 %collective-permute-done.9.refs_12_ = f32[8,128]{1,0:T(8,128)S(1)} collective-permute-done((f32[8,128]{1,0:T(8,128)S(1)}, f32[8,128]{1,0:T(8,128)S(1)}, u32[]{:S(2)}, u32[]{:S(2)}) %collective-permute-start.9) | collective-permute-done | bytes 4128 | tf_op jit(solution)/shard_map/ppermute | solution.py:472
  34.2 0.0 collective-permute-done.7.refs_7_
  34.2 1.0 %shard_map.22 = f32[8,16,256]{2,1,0:T(8,128)} custom-call(f32[8,16,256]{2,1,0:T(8,128)S(1)} %copy-done.1, f32[3,7,16,256]{3,2,1,0:T(8,128)S(1)} %get-tuple-element.25.refs_1_, f32[3,15,8,256]{3,2,1,0:T(8,128)S(1)} %get-tuple-element.27.refs_2_, f32[3,15,2,8,128]{4,3,2,1,0:T(8,128)S(1)} %get-tuple-element.28.refs_3_, ...), custom_call_target="tpu_custom_call" | custom-call | tf_op jit(solution)/shard_map/pallas_call | solution.py:499
  (1 shorter events, 0.0 us)
Async XLA Ops:
  0.0 6.8 %collective-permute-start = (f32[8,16,256]{2,1,0:T(8,128)}, f32[8,16,256]{2,1,0:T(8,128)S(1)}, u32[]{:S(2)}, u32[]{:S(2)}) collective-permute-start(f32[8,16,256]{2,1,0:T(8,128)} %refs_0_.7), channel_id=1, source_target_pairs={{0,1},{2,3},{1,0},{3,2},{4,5},{6,7},{5,4},{7,6},{8,9},{10,11},{9,8... | collective-permute-start | bytes 393224 | tf_op jit(solution)/shard_map/ppermute | solution.py:480
  3.1 3.7 %collective-permute-start.1 = (f32[8,16,256]{2,1,0:T(8,128)}, f32[8,16,256]{2,1,0:T(8,128)S(1)}, u32[]{:S(2)}, u32[]{:S(2)}) collective-permute-start(f32[8,16,256]{2,1,0:T(8,128)} %refs_0_.7), channel_id=1, source_target_pairs={{1,2},{2,1},{5,6},{6,5},{9,10},{10,9},{13,14},{14,13},{17,18},{18,... | collective-permute-start | bytes 393224 | tf_op jit(solution)/shard_map/ppermute | solution.py:480
  6.8 0.9 %copy-start = (f32[8,16,256]{2,1,0:T(8,128)S(1)}, f32[8,16,256]{2,1,0:T(8,128)}, u32[]{:S(2)}) copy-start(f32[8,16,256]{2,1,0:T(8,128)} %refs_0_.7) | copy-start | bytes 393220
  7.8 4.7 %collective-permute-start.2 = (f32[96,256]{1,0:T(8,128)S(1)}, f32[96,256]{1,0:T(8,128)S(1)}, u32[]{:S(2)}, u32[]{:S(2)}) collective-permute-start(f32[96,256]{1,0:T(8,128)S(1)} %get-tuple-element.21), channel_id=1, source_target_pairs={{0,16},{16,0},{1,17},{17,1},{2,18},{18,2},{3,19},{19,3},{4,20},{20... | collective-permute-start | bytes 294920 | tf_op jit(solution)/shard_map/ppermute | solution.py:480
  12.4 1.5 %copy-start.1 = (f32[8,16,256]{2,1,0:T(8,128)S(1)}, f32[8,16,256]{2,1,0:T(8,128)}, u32[]{:S(2)}) copy-start(f32[8,16,256]{2,1,0:T(8,128)} %refs_0_.7) | copy-start | bytes 393220
  12.7 1.2 %collective-permute-start.3 = (f32[8,384]{1,0:T(8,128)S(1)}, f32[8,384]{1,0:T(8,128)S(1)}, u32[]{:S(2)}, u32[]{:S(2)}) collective-permute-start(f32[8,384]{1,0:T(8,128)S(1)} %get-tuple-element.23), channel_id=1, source_target_pairs={{0,4},{8,12},{4,0},{12,8},{1,5},{9,13},{5,1},{13,9},{2,6},{10,14},... | collective-permute-start | bytes 36872 | tf_op jit(solution)/shard_map/ppermute | solution.py:480
  12.8 1.2 %collective-permute-start.4 = (f32[8,384]{1,0:T(8,128)S(1)}, f32[8,384]{1,0:T(8,128)S(1)}, u32[]{:S(2)}, u32[]{:S(2)}) collective-permute-start(f32[8,384]{1,0:T(8,128)S(1)} %get-tuple-element.24), channel_id=1, source_target_pairs={{4,8},{8,4},{5,9},{9,5},{6,10},{10,6},{7,11},{11,7},{20,24},{24,20... | collective-permute-start | bytes 36872 | tf_op jit(solution)/shard_map/ppermute | solution.py:480
  15.0 11.2 %collective-permute-start.5 = (f32[6,16,256]{2,1,0:T(8,128)S(1)}, f32[6,16,256]{2,1,0:T(8,128)S(1)}, u32[]{:S(2)}, u32[]{:S(2)}) collective-permute-start(f32[6,16,256]{2,1,0:T(8,128)S(1)} %get-tuple-element.30.refs_0_.refs_5_), channel_id=1, source_target_pairs={{0,1},{1,0},{2,3},{3,2},{4,5},{5,4},{6,7},{7,6},{8,9},{9,8},{10,11... | collective-permute-start | bytes 294920 | tf_op jit(solution)/shard_map/ppermute | solution.py:472
  21.2 4.9 %collective-permute-start.6 = (f32[8,128]{1,0:T(8,128)S(1)}, f32[8,128]{1,0:T(8,128)S(1)}, u32[]{:S(2)}, u32[]{:S(2)}) collective-permute-start(f32[8,128]{1,0:T(8,128)S(1)} %get-tuple-element.31.refs_2_.refs_10_), channel_id=1, source_target_pairs={{0,4},{4,0},{8,12},{12,8},{1,5},{5,1},{9,13},{13,9},{2,6},{6,2},{1... | collective-permute-start | bytes 12296 | tf_op jit(solution)/shard_map/ppermute | solution.py:472
  26.2 8.0 %collective-permute-start.7 = (f32[2,16,256]{2,1,0:T(8,128)S(1)}, f32[2,16,256]{2,1,0:T(8,128)S(1)}, u32[]{:S(2)}, u32[]{:S(2)}) collective-permute-start(f32[2,16,256]{2,1,0:T(8,128)S(1)} %get-tuple-element.32), channel_id=1, source_target_pairs={{0,2},{1,3},{2,0},{3,1},{4,6},{5,7},{6,4},{7,5},{8,10},{9,11},{10,... | collective-permute-start | bytes 98312 | tf_op jit(solution)/shard_map/ppermute | solution.py:472
  27.7 4.8 %collective-permute-start.8 = (f32[2,8,256]{2,1,0:T(8,128)S(1)}, f32[2,8,256]{2,1,0:T(8,128)S(1)}, u32[]{:S(2)}, u32[]{:S(2)}) collective-permute-start(f32[2,8,256]{2,1,0:T(8,128)S(1)} %get-tuple-element.33.refs_8_), channel_id=1, source_target_pairs={{0,16},{16,0},{1,17},{17,1},{2,18},{18,2},{3,19},{19,3},{4,20},{20... | collective-permute-start | bytes 49160 | tf_op jit(solution)/shard_map/ppermute | solution.py:472
  29.2 4.9 %collective-permute-start.9 = (f32[8,128]{1,0:T(8,128)S(1)}, f32[8,128]{1,0:T(8,128)S(1)}, u32[]{:S(2)}, u32[]{:S(2)}) collective-permute-start(f32[8,128]{1,0:T(8,128)S(1)} %get-tuple-element.34), channel_id=1, source_target_pairs={{0,8},{4,12},{8,0},{12,4},{1,9},{5,13},{9,1},{13,5},{2,10},{6,14},... | collective-permute-start | bytes 12296 | tf_op jit(solution)/shard_map/ppermute | solution.py:472

commit v4 on v3

--- a/solution.py
+++ b/solution.py
@@ -146,22 +146,25 @@
 
 def z_kernel(dims, pairs, *refs):
     nz, nx, ny = dims
+    nt, nb = ny // lanes, nz + 8
     v, zr = refs[0], refs[1:1 + pairs[0]]
     out, *sends = refs[1 + pairs[0]:]
-    at_z, at_x = lax.axis_index("gz"), lax.axis_index("gx")
-    odd_x = at_x % 2 == 1
-    for t in range(ny // lanes):
+    x_sends, y_sends = sends[:pairs[1]], sends[pairs[1]:pairs[1] + pairs[2]]
+    corner_sends = sends[pairs[1] + pairs[2]:]
+    odd_z = lax.axis_index("gz") % 2 == 1
+    odd_x = lax.axis_index("gx") % 2 == 1
+    odd_y = lax.axis_index("gy") % 2 == 1
+    for t in range(nt):
         cols = cut(t)
         below, above = {}, {}
         for z in range(halo):
-            odd = at_z % 2 == 1
             first_top, first_low = zr[0][nz - halo + z, :, cols], zr[0][z, :, cols]
             if len(zr) > 1:
                 second_top, second_low = zr[1][nz - halo + z, :, cols], zr[1][z, :, cols]
             else:
                 second_top = second_low = jnp.zeros_like(first_low)
-            below[z] = jnp.where(odd, first_top, second_top)
-            above[z] = jnp.where(odd, second_low, first_low)
+            below[z] = jnp.where(odd_z, first_top, second_top)
+            above[z] = jnp.where(odd_z, second_low, first_low)
 
         def load(z):
             if z < halo:
@@ -172,38 +175,27 @@
             out[t, i] = value
             low, high = value[:halo], value[nx - halo:]
             rows = slice(i * halo, (i + 1) * halo)
-            sends[0][rows, cols] = jnp.where(odd_x, low, high)
-            if len(sends) > 1:
-                sends[1][rows, cols] = jnp.where(odd_x, high, low)
-
-        z_blur(load, store, nz + 8, taps())
-
-
-def x_kernel(dims, pairs, *refs):
-    nz, nx, ny = dims
-    zb, xr = refs[0], refs[1:1 + pairs[1]]
-    out, *rest = refs[1 + pairs[1]:]
-    sends, wide = rest[:-1], rest[-1]
-    at_x, at_y = lax.axis_index("gx"), lax.axis_index("gy")
-    nt, nb, rows_b = ny // lanes, nz + 8, nx + 8
-    k = taps()
-    for t in range(nt):
-        for i in range(nb):
-            rows = slice(i * halo, (i + 1) * halo)
-            low, high = neighbours(at_x, xr, lambda ref: ref[rows, cut(t)])
-            wide[i, edge - halo:edge, :] = low
-            wide[i, edge:edge + nx, :] = zb[t, i]
-            wide[i, edge + nx:edge + nx + halo, :] = high
-        for i in range(nb):
-            out[t, i] = five(k, *[wide[i, 2 + o:2 + o + rows_b, :] for o in range(5)])
-    odd_y = at_y % 2 == 1
-    flat = lambda t, chunk: out.at[t].reshape(nb * rows_b, lanes)[chunk * lanes:(chunk + 1) * lanes, :]
-    for chunk in range(nb * rows_b // lanes):
-        first = flat(0, chunk).T[:edge, :]
-        last = flat(nt - 1, chunk).T[lanes - edge:, :]
-        sends[0][:, cut(chunk)] = jnp.where(odd_y, first, last)
-        if len(sends) > 1:
-            sends[1][:, cut(chunk)] = jnp.where(odd_y, last, first)
+            x_sends[0][rows, cols] = jnp.where(odd_x, low, high)
+            if len(x_sends) > 1:
+                x_sends[1][rows, cols] = jnp.where(odd_x, high, low)
+
+        z_blur(load, store, nb, taps())
+
+    def strips(first_tile, last_tile, targets):
+        first = first_tile.T[:edge, :]
+        last = last_tile.T[lanes - edge:, :]
+        for f, target in enumerate(targets):
+            ref, cols = target
+            ref[:, cols] = jnp.where(odd_y, last, first) if f else jnp.where(odd_y, first, last)
+
+    per = lanes // nx
+    for chunk in range(nb // per):
+        tiles = [out[t, chunk * per:(chunk + 1) * per].reshape(lanes, lanes) for t in (0, nt - 1)]
+        strips(*tiles, [(ref, cut(chunk)) for ref in y_sends])
+    pad = jnp.zeros((lanes - nb * halo, lanes), jnp.float32)
+    for e, ref in enumerate(x_sends):
+        tiles = [jnp.concatenate([ref[:, cut(t)], pad], axis=0) for t in (0, nt - 1)]
+        strips(*tiles, [(corner, slice(None)) for corner in corner_sends[e * pairs[2]:(e + 1) * pairs[2]]])
 
 
 def grid_masks(dims, counts):
@@ -247,21 +239,44 @@
     nz, nx, ny = dims
     nt = ny // lanes
     own, every = tuple(range(nt)), tuple(range(nt + 1))
-    v, xb, yr = refs[0], refs[1], refs[2:2 + pairs[2]]
-    bb, fz, send_z, wh, t1, cz = refs[2 + pairs[2]:]
-    at_z, at_y = lax.axis_index("gz"), lax.axis_index("gy")
+    refs = list(refs)
+    v, zb = refs.pop(0), refs.pop(0)
+    xr = [refs.pop(0) for _ in range(pairs[1])]
+    yr = [refs.pop(0) for _ in range(pairs[2])]
+    corners = [[refs.pop(0) for _ in range(pairs[2])] for _ in range(pairs[1])]
+    bb, fz, send_z, wide, t1, cz = refs
+    at_z, at_x, at_y = lax.axis_index("gz"), lax.axis_index("gx"), lax.axis_index("gy")
     nb, rows_b = nz + 8, nx + 8
     k = taps()
 
     gap = jnp.zeros((lanes - 2 * edge, lanes), jnp.float32)
-    for chunk in range(nb * rows_b // lanes):
-        low, high = neighbours(at_y, yr, lambda ref: ref[:, cut(chunk)])
-        wh[chunk * lanes:(chunk + 1) * lanes, :] = jnp.concatenate([high, gap, low], axis=0).T
+
+    def halo_tile(received, cols):
+        low, high = neighbours(at_y, received, lambda ref: ref[:, cols])
+        return jnp.concatenate([high, gap, low], axis=0).T
+
+    def sides(t, load, sources):
+        for i in range(nb):
+            rows = slice(i * halo, (i + 1) * halo)
+            low, high = neighbours(at_x, sources, lambda source: load(source, rows))
+            wide[t, i, edge - halo:edge, :] = low
+            wide[t, i, edge + nx:edge + nx + halo, :] = high
+
+    for t in own:
+        sides(t, lambda ref, rows: ref[rows, cut(t)], xr)
+        for i in range(nb):
+            wide[t, i, edge:edge + nx, :] = zb[t, i]
+    sides(nt, lambda tile, rows: tile[rows, :], [halo_tile(group, slice(None)) for group in corners])
+    per = lanes // nx
+    for chunk in range(nb // per):
+        turned = halo_tile(yr, cut(chunk))
+        for i in range(per):
+            wide[nt, chunk * per + i, edge:edge + nx, :] = turned[i * nx:(i + 1) * nx, :]
 
     blank = jnp.zeros((edge, lanes), jnp.float32)
     for z in range(nb):
-        tiles = [xb[t, z] for t in own] + [wh[z * rows_b:(z + 1) * rows_b, :]]
-        done = lane_blur(k, tiles, every)
+        along_x = [five(k, *[wide[t, z, 2 + o:2 + o + rows_b, :] for o in range(5)]) for t in every]
+        done = lane_blur(k, along_x, every)
         for t in every:
             bb[t, z, 0:edge, :] = blank
             bb[t, z, edge:edge + rows_b, :] = done[t]
@@ -472,13 +487,19 @@
     return lax.ppermute(value, axis, [(i, i ^ (2**level)) for i in range(n)])
 
 
-def swap_pairs(values, axis):
-    n = lax.axis_size(axis)
-    out = []
-    for start, value in enumerate(values):
-        lows = range(start, n - 1, 2)
-        out.append(lax.ppermute(value, axis, [(i, i + 1) for i in lows] + [(i + 1, i) for i in lows]))
-    return out
+def pairs_of(n, start):
+    lows = range(start, n - 1, 2)
+    return [(i, i + 1) for i in lows] + [(i + 1, i) for i in lows]
+
+
+def swap_pair(value, axis, start):
+    return lax.ppermute(value, axis, pairs_of(lax.axis_size(axis), start))
+
+
+def swap_corner(value, x_start, y_start):
+    nx, ny = lax.axis_size("gx"), lax.axis_size("gy")
+    moves = [(a * ny + c, b * ny + d) for a, b in pairs_of(nx, x_start) for c, d in pairs_of(ny, y_start)]
+    return lax.ppermute(value, ("gx", "gy"), moves)
 
 
 def body(volume):
@@ -491,7 +512,7 @@
     pairs = tuple(1 if count == 2 else 2 for count in counts)
     nb, rows_b = nz + 8, nx + 8
     assert all(2**d == n and d >= 1 for d, n in zip(depths, counts))
-    assert nz == 8 and nz * nx == lanes and nx >= 8 and nb * rows_b % lanes == 0
+    assert nz == 8 and nz * nx == lanes and nx >= 8 and nb * nx % lanes == 0 and nb * halo <= lanes
     f32 = lambda *shape: jax.ShapeDtypeStruct(shape, jnp.float32)
     scratch = lambda *shape: pltpu.VMEM(shape, jnp.float32)
 
@@ -502,24 +523,23 @@
             compiler_params=pltpu.CompilerParams(vmem_limit_bytes=16 * 2**20),
         )(*args)
 
-    z_received = swap_pairs([volume] * pairs[0], "gz")
-    blurred_z, *x_sends = call(
+    z_received = [swap_pair(volume, "gz", e) for e in range(pairs[0])]
+    ex, ey = range(pairs[1]), range(pairs[2])
+    blurred_z, *sends = call(
         functools.partial(z_kernel, dims, pairs),
-        [f32(nt, nb, nx, lanes)] + [f32(nb * halo, ny)] * pairs[1], [], volume, *z_received)
-    x_received = swap_pairs(x_sends, "gx")
-    blurred_x, *y_sends = call(
-        functools.partial(x_kernel, dims, pairs),
-        [f32(nt, nb, rows_b, lanes)] + [f32(edge, nb * rows_b)] * pairs[2],
-        [scratch(nb, nx + 2 * edge, lanes)], blurred_z, *x_received)
-    y_received = swap_pairs(y_sends, "gy")
+        [f32(nt, nb, nx, lanes)] + [f32(nb * halo, ny) for e in ex] + [f32(edge, nb * nx) for f in ey]
+        + [f32(edge, lanes) for e in ex for f in ey], [], volume, *z_received)
+    x_received = [swap_pair(sends[e], "gx", e) for e in ex]
+    y_received = [swap_pair(sends[pairs[1] + f], "gy", f) for f in reversed(ey)][::-1]
+    corners = [swap_corner(sends[pairs[1] + pairs[2] + e * pairs[2] + f], e, f) for e in ex for f in ey]
 
     steps = ny // 16
     send_shape = lambda d: 6 if d > 1 else 2
     bb, fz, send_z = call(
         functools.partial(main_kernel, dims, counts, pairs),
         [f32(nt + 1, nb, rows_b + 2 * edge, lanes), f32(3, nz - 1, nx, ny), f32(send_shape(depths[0]), nx, ny)],
-        [scratch(nb * rows_b, lanes), scratch(nt + 1, nz + 1, rows_b + 8, lanes), scratch(nz, nx, ny)],
-        volume, blurred_x, *y_received)
+        [scratch(nt + 1, nb, nx + 2 * edge, lanes), scratch(nt + 1, nz + 1, rows_b + 8, lanes), scratch(nz, nx, ny)],
+        volume, blurred_z, *x_received, *y_received, *corners)
     fx, fy, cy, send_x, send_y = call(
         functools.partial(side_kernel, dims, counts),
         [f32(3, nx - 1, nz, ny), f32(3, steps - 1, 2, 8, lanes), f32(4, 3, 8, lanes),

time: 35.3 us -> 34.4 us (0.975)
  waiting for transfers between devices: 8.91 us -> 6.13 us
  starting transfers between devices: 21.5 us -> 23.5 us
    ppermute x5 -> x7, starting transfers between devices: 6.17 us -> 9.82 us  [the longest x5 6.09 us: swap_pair(): return lax.ppermute(value, axis, pairs_of(lax.axis_size(axis), start))]
    ppermute x5 -> x7, waiting for transfers between devices: 6.5 us -> 3.72 us  [the longest x5 3.05 us: swap_pair(): return lax.ppermute(value, axis, pairs_of(lax.axis_size(axis), start))]
    ppermute x5, starting transfers between devices: 15.3 us -> 13.7 us  [swap_bit(): return lax.ppermute(value, axis, [(i, i ^ 2 ** level) for i in range(n)])]
    pallas_call x6 -> x5, Pallas kernels: 3.77 us -> 3.62 us  [call(): pl.pallas_call(kernel, out_shape=out_shape, in_specs=[VMEM] * len(args),...]
  transfers between devices with their start and end apart: 10 -> 12, of which waited for: 5 -> 5; matrix products, arithmetic and copies ran while one was open for 0% -> 0% of each run, Pallas kernels for 4% -> 4%
where the time goes in v4:
time: 34.4 us; the launch traced here: 34.2 us
  starting transfers between devices  23.5 us (68%)
  waiting for transfers between devices  6.13 us (18%)
  Pallas kernels  3.62 us (11%)
  local copies, waits for them, and re-layouts  0.91 us (3%)
    ppermute x5, starting transfers between devices, swap_bit(): return lax.ppermute(value, axis, [(i, i ^ 2 ** level) for i in range(n)])  13.7 us
    ppermute x5, starting transfers between devices, swap_pair(): return lax.ppermute(value, axis, pairs_of(lax.axis_size(axis), start))  6.09 us
    ppermute x2, starting transfers between devices, swap_corner(): return lax.ppermute(value, ('gx', 'gy'), moves)  3.74 us
    pallas_call x5, Pallas kernels, call(): pl.pallas_call(kernel, out_shape=out_shape, in_specs=[VMEM] * len(args),...  3.62 us
    ppermute x5, waiting for transfers between devices, swap_pair(): return lax.ppermute(value, axis, pairs_of(lax.axis_size(axis), start))  3.05 us
    ppermute x5, waiting for transfers between devices, swap_bit(): return lax.ppermute(value, axis, [(i, i ^ 2 ** level) for i in range(n)])  2.41 us
    unnamed x4, local copies, waits for them, and re-layouts  0.91 us
  transfers between devices with their start and end apart: 12, of which 5 were waited for; matrix products, arithmetic and copies ran while one was open for 0% of the time, Pallas kernels for 4%

profile of v4, /device:TPU:0, one launch (start us, length us, event | category | flops | bytes accessed | tf_op | source)
XLA Modules:
  0.0 34.2 jit_solution(13193876252718694803)
XLA Ops:
  0.0 3.1 %collective-permute-start = (f32[8,16,256]{2,1,0:T(8,128)}, f32[8,16,256]{2,1,0:T(8,128)S(1)}, u32[]{:S(2)}, u32[]{:S(2)}) collective-permute-start(f32[8,16,256]{2,1,0:T(8,128)} %refs_0_.7), channel_id=1, source_target_pairs={{0,1},{2,3},{1,0},{3,2},{4,5},{6,7},{5,4},{7,6},{8,9},{10,11},{9,8... | collective-permute-start | bytes 393224 | tf_op jit(solution)/shard_map/ppermute | solution.py:496
  3.1 0.7 %collective-permute-start.1 = (f32[8,16,256]{2,1,0:T(8,128)}, f32[8,16,256]{2,1,0:T(8,128)S(1)}, u32[]{:S(2)}, u32[]{:S(2)}) collective-permute-start(f32[8,16,256]{2,1,0:T(8,128)} %refs_0_.7), channel_id=1, source_target_pairs={{1,2},{2,1},{5,6},{6,5},{9,10},{10,9},{13,14},{14,13},{17,18},{18,... | collective-permute-start | bytes 393224 | tf_op jit(solution)/shard_map/ppermute | solution.py:496
  3.7 3.0 %collective-permute-done.refs_1_ = f32[8,16,256]{2,1,0:T(8,128)S(1)} collective-permute-done((f32[8,16,256]{2,1,0:T(8,128)}, f32[8,16,256]{2,1,0:T(8,128)S(1)}, u32[]{:S(2)}, u32[]{:S(2)}) %collective-permute-start) | collective-permute-done | bytes 131104 | tf_op jit(solution)/shard_map/ppermute | solution.py:496
  6.8 0.0 collective-permute-done.1.refs_2_
  6.8 0.0 copy-start
  6.8 0.9 %copy-done = f32[8,16,256]{2,1,0:T(8,128)S(1)} copy-done((f32[8,16,256]{2,1,0:T(8,128)S(1)}, f32[8,16,256]{2,1,0:T(8,128)}, u32[]{:S(2)}) %copy-start) | copy-done | bytes 131096
  7.7 0.0 copy-start.1
  7.7 0.2 shard_map.17
  7.8 1.7 %collective-permute-start.2 = (f32[96,256]{1,0:T(8,128)S(1)}, f32[96,256]{1,0:T(8,128)S(1)}, u32[]{:S(2)}, u32[]{:S(2)}) collective-permute-start(f32[96,256]{1,0:T(8,128)S(1)} %get-tuple-element.22), channel_id=1, source_target_pairs={{0,16},{16,0},{1,17},{17,1},{2,18},{18,2},{3,19},{19,3},{4,20},{20... | collective-permute-start | bytes 294920 | tf_op jit(solution)/shard_map/ppermute | solution.py:496
  9.6 0.0 collective-permute-start.3
  9.6 0.7 %collective-permute-start.4 = (f32[8,256]{1,0:T(8,128)S(1)}, f32[8,256]{1,0:T(8,128)S(1)}, u32[]{:S(2)}, u32[]{:S(2)}) collective-permute-start(f32[8,256]{1,0:T(8,128)S(1)} %get-tuple-element.24), channel_id=1, source_target_pairs={{4,8},{8,4},{5,9},{9,5},{6,10},{10,6},{7,11},{11,7},{20,24},{24,20... | collective-permute-start | bytes 24584 | tf_op jit(solution)/shard_map/ppermute | solution.py:496
  10.2 3.1 %collective-permute-start.5 = (f32[8,128]{1,0:T(8,128)S(1)}, f32[8,128]{1,0:T(8,128)S(1)}, u32[]{:S(2)}, u32[]{:S(2)}) collective-permute-start(f32[8,128]{1,0:T(8,128)S(1)} %get-tuple-element.25), channel_id=1, source_target_pairs={{0,20},{8,28},{4,16},{12,24},{16,4},{24,12},{20,0},{28,8},{1,21},{... | collective-permute-start | bytes 12296 | tf_op jit(solution)/shard_map/ppermute | solution.py:502
  13.3 0.6 %collective-permute-start.6 = (f32[8,128]{1,0:T(8,128)S(1)}, f32[8,128]{1,0:T(8,128)S(1)}, u32[]{:S(2)}, u32[]{:S(2)}) collective-permute-start(f32[8,128]{1,0:T(8,128)S(1)} %get-tuple-element.26), channel_id=1, source_target_pairs={{4,24},{8,20},{20,8},{24,4},{5,25},{9,21},{21,9},{25,5},{6,26},{10... | collective-permute-start | bytes 12296 | tf_op jit(solution)/shard_map/ppermute | solution.py:502
  14.0 0.7 %collective-permute-done.5.refs_5_ = f32[8,128]{1,0:T(8,128)S(1)} collective-permute-done((f32[8,128]{1,0:T(8,128)S(1)}, f32[8,128]{1,0:T(8,128)S(1)}, u32[]{:S(2)}, u32[]{:S(2)}) %collective-permute-start.5) | collective-permute-done | bytes 4128 | tf_op jit(solution)/shard_map/ppermute | solution.py:502
  14.6 0.0 collective-permute-done.6.refs_6_
  14.6 0.0 collective-permute-done.3.refs_3_
  14.6 0.0 collective-permute-done.4.refs_4_
  14.7 0.0 collective-permute-done.2.refs_2_
  14.7 0.0 copy-done.1
  14.7 1.0 %shard_map.18 = (f32[3,16,40,128]{3,2,1,0:T(8,128)S(1)}, f32[3,7,16,256]{3,2,1,0:T(8,128)S(1)}, f32[6,16,256]{2,1,0:T(8,128)S(1)}) custom-call(f32[8,16,256]{2,1,0:T(8,128)S(1)} %copy-done.1, f32[2,16,16,128]{3,2,1,0:T(8,128)S(1)} %get-tuple-element.21.refs_1_, f32[96,256]{1,0:T(8,128)S(1)} %collective-permute-done.2.refs_2_, ...), custom_call_target="tpu_custom_call" | custom-call | tf_op jit(solution)/shard_map/pallas_call | solution.py:520
  15.7 4.7 %collective-permute-start.7 = (f32[6,16,256]{2,1,0:T(8,128)S(1)}, f32[6,16,256]{2,1,0:T(8,128)S(1)}, u32[]{:S(2)}, u32[]{:S(2)}) collective-permute-start(f32[6,16,256]{2,1,0:T(8,128)S(1)} %get-tuple-element.32.refs_0_.refs_5_), channel_id=1, source_target_pairs={{0,1},{1,0},{2,3},{3,2},{4,5},{5,4},{6,7},{7,6},{8,9},{9,8},{10,11... | collective-permute-start | bytes 294920 | tf_op jit(solution)/shard_map/ppermute | solution.py:487
  20.4 1.4 %shard_map.19 = (f32[3,15,8,256]{3,2,1,0:T(8,128)S(1)}, f32[3,15,2,8,128]{4,3,2,1,0:T(8,128)S(1)}, f32[4,3,8,128]{3,2,1,0:T(8,128)S(1)}, f32[2,8,256]{2,1,0:T(8,128)S(1)}, f32[8,128]{1,0:T(8,128)S(1)}) custom-call(f32[8,16,256]{2,1,0:T(8,128)S(1)} %copy-done.1, f32[3,16,40,128]{3,2,1,0:T(8,128)S(1)} %get-tuple-element.28.refs_1_), custom_call_target="tpu_custom_call" | custom-call | tf_op jit(solution)/shard_map/pallas_call | solution.py:520
  21.8 4.1 %collective-permute-start.8 = (f32[8,128]{1,0:T(8,128)S(1)}, f32[8,128]{1,0:T(8,128)S(1)}, u32[]{:S(2)}, u32[]{:S(2)}) collective-permute-start(f32[8,128]{1,0:T(8,128)S(1)} %get-tuple-element.33.refs_2_.refs_10_), channel_id=1, source_target_pairs={{0,4},{4,0},{8,12},{12,8},{1,5},{5,1},{9,13},{13,9},{2,6},{6,2},{1... | collective-permute-start | bytes 12296 | tf_op jit(solution)/shard_map/ppermute | solution.py:487
  25.9 0.8 %collective-permute-done.8.refs_3_.refs_11_ = f32[8,128]{1,0:T(8,128)S(1)} collective-permute-done((f32[8,128]{1,0:T(8,128)S(1)}, f32[8,128]{1,0:T(8,128)S(1)}, u32[]{:S(2)}, u32[]{:S(2)}) %collective-permute-start.8) | collective-permute-done | bytes 4128 | tf_op jit(solution)/shard_map/ppermute | solution.py:487
  26.8 0.0 collective-permute-done.7.refs_1_.refs_6_
  26.8 1.5 %collective-permute-start.9 = (f32[2,16,256]{2,1,0:T(8,128)S(1)}, f32[2,16,256]{2,1,0:T(8,128)S(1)}, u32[]{:S(2)}, u32[]{:S(2)}) collective-permute-start(f32[2,16,256]{2,1,0:T(8,128)S(1)} %get-tuple-element.34), channel_id=1, source_target_pairs={{0,2},{1,3},{2,0},{3,1},{4,6},{5,7},{6,4},{7,5},{8,10},{9,11},{10,... | collective-permute-start | bytes 98312 | tf_op jit(solution)/shard_map/ppermute | solution.py:487
  28.4 0.5 %collective-permute-start.10 = (f32[2,8,256]{2,1,0:T(8,128)S(1)}, f32[2,8,256]{2,1,0:T(8,128)S(1)}, u32[]{:S(2)}, u32[]{:S(2)}) collective-permute-start(f32[2,8,256]{2,1,0:T(8,128)S(1)} %get-tuple-element.35.refs_8_), channel_id=1, source_target_pairs={{0,16},{16,0},{1,17},{17,1},{2,18},{18,2},{3,19},{19,3},{4,20},{20... | collective-permute-start | bytes 49160 | tf_op jit(solution)/shard_map/ppermute | solution.py:487
  28.9 2.8 %collective-permute-start.11 = (f32[8,128]{1,0:T(8,128)S(1)}, f32[8,128]{1,0:T(8,128)S(1)}, u32[]{:S(2)}, u32[]{:S(2)}) collective-permute-start(f32[8,128]{1,0:T(8,128)S(1)} %get-tuple-element.36), channel_id=1, source_target_pairs={{0,8},{4,12},{8,0},{12,4},{1,9},{5,13},{9,1},{13,5},{2,10},{6,14},... | collective-permute-start | bytes 12296 | tf_op jit(solution)/shard_map/ppermute | solution.py:487
  31.7 0.5 %collective-permute-done.10.refs_9_ = f32[2,8,256]{2,1,0:T(8,128)S(1)} collective-permute-done((f32[2,8,256]{2,1,0:T(8,128)S(1)}, f32[2,8,256]{2,1,0:T(8,128)S(1)}, u32[]{:S(2)}, u32[]{:S(2)}) %collective-permute-start.10) | collective-permute-done | bytes 16416 | tf_op jit(solution)/shard_map/ppermute | solution.py:487
  32.2 1.1 %collective-permute-done.11.refs_12_ = f32[8,128]{1,0:T(8,128)S(1)} collective-permute-done((f32[8,128]{1,0:T(8,128)S(1)}, f32[8,128]{1,0:T(8,128)S(1)}, u32[]{:S(2)}, u32[]{:S(2)}) %collective-permute-start.11) | collective-permute-done | bytes 4128 | tf_op jit(solution)/shard_map/ppermute | solution.py:487
  33.3 0.0 collective-permute-done.9.refs_7_
  33.3 1.0 %shard_map.21 = f32[8,16,256]{2,1,0:T(8,128)} custom-call(f32[8,16,256]{2,1,0:T(8,128)S(1)} %copy-done.1, f32[3,7,16,256]{3,2,1,0:T(8,128)S(1)} %get-tuple-element.27.refs_1_, f32[3,15,8,256]{3,2,1,0:T(8,128)S(1)} %get-tuple-element.29.refs_2_, f32[3,15,2,8,128]{4,3,2,1,0:T(8,128)S(1)} %get-tuple-element.30.refs_3_, ...), custom_call_target="tpu_custom_call" | custom-call | tf_op jit(solution)/shard_map/pallas_call | solution.py:520
  (1 shorter events, 0.0 us)
Async XLA Ops:
  0.0 6.8 %collective-permute-start = (f32[8,16,256]{2,1,0:T(8,128)}, f32[8,16,256]{2,1,0:T(8,128)S(1)}, u32[]{:S(2)}, u32[]{:S(2)}) collective-permute-start(f32[8,16,256]{2,1,0:T(8,128)} %refs_0_.7), channel_id=1, source_target_pairs={{0,1},{2,3},{1,0},{3,2},{4,5},{6,7},{5,4},{7,6},{8,9},{10,11},{9,8... | collective-permute-start | bytes 393224 | tf_op jit(solution)/shard_map/ppermute | solution.py:496
  3.1 3.7 %collective-permute-start.1 = (f32[8,16,256]{2,1,0:T(8,128)}, f32[8,16,256]{2,1,0:T(8,128)S(1)}, u32[]{:S(2)}, u32[]{:S(2)}) collective-permute-start(f32[8,16,256]{2,1,0:T(8,128)} %refs_0_.7), channel_id=1, source_target_pairs={{1,2},{2,1},{5,6},{6,5},{9,10},{10,9},{13,14},{14,13},{17,18},{18,... | collective-permute-start | bytes 393224 | tf_op jit(solution)/shard_map/ppermute | solution.py:496
  6.8 0.9 %copy-start = (f32[8,16,256]{2,1,0:T(8,128)S(1)}, f32[8,16,256]{2,1,0:T(8,128)}, u32[]{:S(2)}) copy-start(f32[8,16,256]{2,1,0:T(8,128)} %refs_0_.7) | copy-start | bytes 393220
  7.7 7.0 %copy-start.1 = (f32[8,16,256]{2,1,0:T(8,128)S(1)}, f32[8,16,256]{2,1,0:T(8,128)}, u32[]{:S(2)}) copy-start(f32[8,16,256]{2,1,0:T(8,128)} %refs_0_.7) | copy-start | bytes 393220
  7.8 6.8 %collective-permute-start.2 = (f32[96,256]{1,0:T(8,128)S(1)}, f32[96,256]{1,0:T(8,128)S(1)}, u32[]{:S(2)}, u32[]{:S(2)}) collective-permute-start(f32[96,256]{1,0:T(8,128)S(1)} %get-tuple-element.22), channel_id=1, source_target_pairs={{0,16},{16,0},{1,17},{17,1},{2,18},{18,2},{3,19},{19,3},{4,20},{20... | collective-permute-start | bytes 294920 | tf_op jit(solution)/shard_map/ppermute | solution.py:496
  9.6 5.1 %collective-permute-start.3 = (f32[8,256]{1,0:T(8,128)S(1)}, f32[8,256]{1,0:T(8,128)S(1)}, u32[]{:S(2)}, u32[]{:S(2)}) collective-permute-start(f32[8,256]{1,0:T(8,128)S(1)} %get-tuple-element.23), channel_id=1, source_target_pairs={{0,4},{8,12},{4,0},{12,8},{1,5},{9,13},{5,1},{13,9},{2,6},{10,14},... | collective-permute-start | bytes 24584 | tf_op jit(solution)/shard_map/ppermute | solution.py:496
  9.6 5.1 %collective-permute-start.4 = (f32[8,256]{1,0:T(8,128)S(1)}, f32[8,256]{1,0:T(8,128)S(1)}, u32[]{:S(2)}, u32[]{:S(2)}) collective-permute-start(f32[8,256]{1,0:T(8,128)S(1)} %get-tuple-element.24), channel_id=1, source_target_pairs={{4,8},{8,4},{5,9},{9,5},{6,10},{10,6},{7,11},{11,7},{20,24},{24,20... | collective-permute-start | bytes 24584 | tf_op jit(solution)/shard_map/ppermute | solution.py:496
  10.2 4.4 %collective-permute-start.5 = (f32[8,128]{1,0:T(8,128)S(1)}, f32[8,128]{1,0:T(8,128)S(1)}, u32[]{:S(2)}, u32[]{:S(2)}) collective-permute-start(f32[8,128]{1,0:T(8,128)S(1)} %get-tuple-element.25), channel_id=1, source_target_pairs={{0,20},{8,28},{4,16},{12,24},{16,4},{24,12},{20,0},{28,8},{1,21},{... | collective-permute-start | bytes 12296 | tf_op jit(solution)/shard_map/ppermute | solution.py:502
  13.3 1.3 %collective-permute-start.6 = (f32[8,128]{1,0:T(8,128)S(1)}, f32[8,128]{1,0:T(8,128)S(1)}, u32[]{:S(2)}, u32[]{:S(2)}) collective-permute-start(f32[8,128]{1,0:T(8,128)S(1)} %get-tuple-element.26), channel_id=1, source_target_pairs={{4,24},{8,20},{20,8},{24,4},{5,25},{9,21},{21,9},{25,5},{6,26},{10... | collective-permute-start | bytes 12296 | tf_op jit(solution)/shard_map/ppermute | solution.py:502
  15.7 11.0 %collective-permute-start.7 = (f32[6,16,256]{2,1,0:T(8,128)S(1)}, f32[6,16,256]{2,1,0:T(8,128)S(1)}, u32[]{:S(2)}, u32[]{:S(2)}) collective-permute-start(f32[6,16,256]{2,1,0:T(8,128)S(1)} %get-tuple-element.32.refs_0_.refs_5_), channel_id=1, source_target_pairs={{0,1},{1,0},{2,3},{3,2},{4,5},{5,4},{6,7},{7,6},{8,9},{9,8},{10,11... | collective-permute-start | bytes 294920 | tf_op jit(solution)/shard_map/ppermute | solution.py:487
  21.8 5.0 %collective-permute-start.8 = (f32[8,128]{1,0:T(8,128)S(1)}, f32[8,128]{1,0:T(8,128)S(1)}, u32[]{:S(2)}, u32[]{:S(2)}) collective-permute-start(f32[8,128]{1,0:T(8,128)S(1)} %get-tuple-element.33.refs_2_.refs_10_), channel_id=1, source_target_pairs={{0,4},{4,0},{8,12},{12,8},{1,5},{5,1},{9,13},{13,9},{2,6},{6,2},{1... | collective-permute-start | bytes 12296 | tf_op jit(solution)/shard_map/ppermute | solution.py:487
  26.8 6.5 %collective-permute-start.9 = (f32[2,16,256]{2,1,0:T(8,128)S(1)}, f32[2,16,256]{2,1,0:T(8,128)S(1)}, u32[]{:S(2)}, u32[]{:S(2)}) collective-permute-start(f32[2,16,256]{2,1,0:T(8,128)S(1)} %get-tuple-element.34), channel_id=1, source_target_pairs={{0,2},{1,3},{2,0},{3,1},{4,6},{5,7},{6,4},{7,5},{8,10},{9,11},{10,... | collective-permute-start | bytes 98312 | tf_op jit(solution)/shard_map/ppermute | solution.py:487
  28.4 3.8 %collective-permute-start.10 = (f32[2,8,256]{2,1,0:T(8,128)S(1)}, f32[2,8,256]{2,1,0:T(8,128)S(1)}, u32[]{:S(2)}, u32[]{:S(2)}) collective-permute-start(f32[2,8,256]{2,1,0:T(8,128)S(1)} %get-tuple-element.35.refs_8_), channel_id=1, source_target_pairs={{0,16},{16,0},{1,17},{17,1},{2,18},{18,2},{3,19},{19,3},{4,20},{20... | collective-permute-start | bytes 49160 | tf_op jit(solution)/shard_map/ppermute | solution.py:487
  28.9 4.4 %collective-permute-start.11 = (f32[8,128]{1,0:T(8,128)S(1)}, f32[8,128]{1,0:T(8,128)S(1)}, u32[]{:S(2)}, u32[]{:S(2)}) collective-permute-start(f32[8,128]{1,0:T(8,128)S(1)} %get-tuple-element.36), channel_id=1, source_target_pairs={{0,8},{4,12},{8,0},{12,4},{1,9},{5,13},{9,1},{13,5},{2,10},{6,14},... | collective-permute-start | bytes 12296 | tf_op jit(solution)/shard_map/ppermute | solution.py:487

commit v5 on v4

--- a/solution.py
+++ b/solution.py
@@ -1,4 +1,5 @@
 import functools
+import itertools
 
 import jax
 import jax.numpy as jnp
@@ -6,6 +7,7 @@
 from jax.experimental import pallas as pl
 from jax.experimental.pallas import tpu as pltpu
 from jax.sharding import PartitionSpec as P
+
 
 kernel_taps = (0.41111229, 0.8007374, 1.0, 0.8007374, 0.41111229)
 time_step = 3000.0
@@ -62,7 +64,7 @@
 
 
 def last_message(upper, seg):
-    a0, an, g00, g0n, gnn, c = seg
+    a0, an, g00, _, gnn, c = seg
     return (jnp.where(upper, a0, an), jnp.where(upper, g00, c / (1.0 + c * gnn)))
 
 
@@ -137,34 +139,43 @@
         window.pop(0)
 
 
-def neighbours(position, refs, load):
+def neighbours(position, count, refs, load):
     odd = position % 2 == 1
     first = load(refs[0])
-    second = load(refs[1]) if len(refs) > 1 else jnp.zeros_like(first)
+    if len(refs) > 1:
+        end = (position == 0) | (position == count - 1)
+        second = jnp.where(end, 0.0, load(refs[1]))
+    else:
+        second = jnp.zeros_like(first)
     return jnp.where(odd, first, second), jnp.where(odd, second, first)
 
 
-def z_kernel(dims, pairs, *refs):
+def open_kernel(dims, volume, kept, *sends):
+    nz = dims[0]
+    odd = lax.axis_index("gz") % 2 == 1
+    for z in range(nz):
+        kept[z] = volume[z]
+    for z in range(halo):
+        low, high = volume[z], volume[nz - halo + z]
+        sends[0][z] = jnp.where(odd, low, high)
+        if len(sends) > 1:
+            sends[1][z] = jnp.where(odd, high, low)
+
+
+def z_kernel(dims, counts, pairs, *refs):
     nz, nx, ny = dims
     nt, nb = ny // lanes, nz + 8
     v, zr = refs[0], refs[1:1 + pairs[0]]
     out, *sends = refs[1 + pairs[0]:]
     x_sends, y_sends = sends[:pairs[1]], sends[pairs[1]:pairs[1] + pairs[2]]
     corner_sends = sends[pairs[1] + pairs[2]:]
-    odd_z = lax.axis_index("gz") % 2 == 1
+    at_z = lax.axis_index("gz")
     odd_x = lax.axis_index("gx") % 2 == 1
     odd_y = lax.axis_index("gy") % 2 == 1
     for t in range(nt):
         cols = cut(t)
-        below, above = {}, {}
-        for z in range(halo):
-            first_top, first_low = zr[0][nz - halo + z, :, cols], zr[0][z, :, cols]
-            if len(zr) > 1:
-                second_top, second_low = zr[1][nz - halo + z, :, cols], zr[1][z, :, cols]
-            else:
-                second_top = second_low = jnp.zeros_like(first_low)
-            below[z] = jnp.where(odd_z, first_top, second_top)
-            above[z] = jnp.where(odd_z, second_low, first_low)
+        below = [neighbours(at_z, counts[0], zr, lambda ref: ref[z, :, cols])[0] for z in range(halo)]
+        above = [neighbours(at_z, counts[0], zr, lambda ref: ref[z, :, cols])[1] for z in range(halo)]
 
         def load(z):
             if z < halo:
@@ -252,13 +263,13 @@
     gap = jnp.zeros((lanes - 2 * edge, lanes), jnp.float32)
 
     def halo_tile(received, cols):
-        low, high = neighbours(at_y, received, lambda ref: ref[:, cols])
+        low, high = neighbours(at_y, counts[2], received, lambda ref: ref[:, cols])
         return jnp.concatenate([high, gap, low], axis=0).T
 
     def sides(t, load, sources):
         for i in range(nb):
             rows = slice(i * halo, (i + 1) * halo)
-            low, high = neighbours(at_x, sources, lambda source: load(source, rows))
+            low, high = neighbours(at_x, counts[1], sources, lambda source: load(source, rows))
             wide[t, i, edge - halo:edge, :] = low
             wide[t, i, edge + nx:edge + nx + halo, :] = high
 
@@ -405,7 +416,7 @@
     return tuple(ref[i] for i in range(count))
 
 
-def merge_kernel(level, counts, depths, axes, *refs):
+def merge_kernel(level, depths, axes, *refs):
     refs = list(refs)
     groups = [[refs.pop(0) for _ in range(level + 2)] for _ in axes]
     for axis, group, out in zip(axes, groups, refs):
@@ -482,24 +493,39 @@
             out[z, :, cols] = v[z, :, cols] + total * (1.0 / 3.0)
 
 
+def partners(n, start):
+    return [i ^ 1 if start == 0 else ((i - 1) ^ 1) + 1 if 0 < i < n - 1 else n - 1 - i for i in range(n)]
+
+
+def permute(value, axes, move):
+    sizes = [lax.axis_size(axis) for axis in axes]
+    moves = []
+    for source in itertools.product(*[range(size) for size in sizes]):
+        index = lambda place: functools.reduce(lambda so_far, pair: so_far * pair[1] + pair[0], zip(place, sizes), 0)
+        moves.append((index(source), index(move(*source))))
+    return lax.ppermute(value, axes if len(axes) > 1 else axes[0], moves)
+
+
 def swap_bit(value, axis, level):
-    n = lax.axis_size(axis)
-    return lax.ppermute(value, axis, [(i, i ^ (2**level)) for i in range(n)])
-
-
-def pairs_of(n, start):
-    lows = range(start, n - 1, 2)
-    return [(i, i + 1) for i in lows] + [(i + 1, i) for i in lows]
+    return permute(value, (axis,), lambda i: (i ^ (2**level),))
 
 
 def swap_pair(value, axis, start):
-    return lax.ppermute(value, axis, pairs_of(lax.axis_size(axis), start))
+    partner = partners(lax.axis_size(axis), start)
+    return permute(value, (axis,), lambda i: (partner[i],))
+
+
+def swap_z(value, start):
+    n = lax.axis_size("gz")
+    partner = partners(n, start)
+    if start == 0:
+        return swap_pair(value, "gz", 0)
+    return permute(value, ("gy", "gz"), lambda y, z: (y, partner[z]) if 0 < z < n - 1 else (y ^ 1, z))
 
 
 def swap_corner(value, x_start, y_start):
-    nx, ny = lax.axis_size("gx"), lax.axis_size("gy")
-    moves = [(a * ny + c, b * ny + d) for a, b in pairs_of(nx, x_start) for c, d in pairs_of(ny, y_start)]
-    return lax.ppermute(value, ("gx", "gy"), moves)
+    of_x, of_y = partners(lax.axis_size("gx"), x_start), partners(lax.axis_size("gy"), y_start)
+    return permute(value, ("gx", "gy"), lambda x, y: (of_x[x], of_y[y]))
 
 
 def body(volume):
@@ -523,10 +549,12 @@
             compiler_params=pltpu.CompilerParams(vmem_limit_bytes=16 * 2**20),
         )(*args)
 
-    z_received = [swap_pair(volume, "gz", e) for e in range(pairs[0])]
+    volume, *z_sends = call(
+        functools.partial(open_kernel, dims), [f32(*dims)] + [f32(halo, nx, ny)] * pairs[0], [], volume)
+    z_received = [swap_z(value, e) for e, value in enumerate(z_sends)]
     ex, ey = range(pairs[1]), range(pairs[2])
     blurred_z, *sends = call(
-        functools.partial(z_kernel, dims, pairs),
+        functools.partial(z_kernel, dims, counts, pairs),
         [f32(nt, nb, nx, lanes)] + [f32(nb * halo, ny) for e in ex] + [f32(edge, nb * nx) for f in ey]
         + [f32(edge, lanes) for e in ex for f in ey], [], volume, *z_received)
     x_received = [swap_pair(sends[e], "gx", e) for e in ex]
@@ -560,7 +588,7 @@
             for axis in axes:
                 count = 2 if depths[axis] == level + 2 else 6
                 shapes.append(f32(8, lanes) if axis == 2 else f32(count, *((nx, ny) if axis == 0 else (nz, ny))))
-            sent = call(functools.partial(merge_kernel, level, counts, depths, axes), shapes, [],
+            sent = call(functools.partial(merge_kernel, level, depths, axes), shapes, [],
                         *[ref for axis in axes for ref in groups[axis]])
             for axis, value in zip(axes, sent):
                 message[axis] = value

time: 34.4 us -> 31.4 us (0.913)
  starting transfers between devices: 23.5 us -> 16.6 us
  waiting for transfers between devices: 6.13 us -> 10 us
    ppermute x12, starting transfers between devices: 23.5 us -> 16.6 us  [permute(): return lax.ppermute(value, axes if len(axes) > 1 else axes[0], moves)]
    ppermute x12, waiting for transfers between devices: 6.13 us -> 10 us  [permute(): return lax.ppermute(value, axes if len(axes) > 1 else axes[0], moves)]
    pallas_call x5 -> x6, Pallas kernels: 3.62 us -> 3.74 us  [call(): pl.pallas_call(kernel, out_shape=out_shape, in_specs=[VMEM] * len(args),...]
    unnamed x4 -> x2, local copies, waits for them, and re-layouts: 0.91 us -> 0.9 us
  transfers between devices with their start and end apart: 12 -> 12, of which waited for: 5 -> 7; matrix products, arithmetic and copies ran while one was open for 0% -> 0% of each run, Pallas kernels for 4% -> 5%
where the time goes in v5:
time: 31.4 us; the launch traced here: 31.3 us
  starting transfers between devices  16.6 us (53%)
  waiting for transfers between devices  10 us (32%)
  Pallas kernels  3.74 us (12%)
  local copies, waits for them, and re-layouts  0.9 us (3%)
    ppermute x12, starting transfers between devices, permute(): return lax.ppermute(value, axes if len(axes) > 1 else axes[0], moves)  16.6 us
    ppermute x12, waiting for transfers between devices, permute(): return lax.ppermute(value, axes if len(axes) > 1 else axes[0], moves)  10 us
    pallas_call x6, Pallas kernels, call(): pl.pallas_call(kernel, out_shape=out_shape, in_specs=[VMEM] * len(args),...  3.74 us
    unnamed x2, local copies, waits for them, and re-layouts  0.9 us
  transfers between devices with their start and end apart: 12, of which 7 were waited for; matrix products, arithmetic and copies ran while one was open for 0% of the time, Pallas kernels for 5%

profile of v5, /device:TPU:0, one launch (start us, length us, event | category | flops | bytes accessed | tf_op | source)
XLA Modules:
  0.0 31.3 jit_solution(18110972928908965717)
XLA Ops:
  0.0 0.0 copy-start
  0.0 0.9 %copy-done = f32[8,16,256]{2,1,0:T(8,128)S(1)} copy-done((f32[8,16,256]{2,1,0:T(8,128)S(1)}, f32[8,16,256]{2,1,0:T(8,128)}, u32[]{:S(2)}) %copy-start) | copy-done | bytes 131096
  0.9 3.1 %collective-permute-start = (f32[6,16,256]{2,1,0:T(8,128)S(1)}, f32[6,16,256]{2,1,0:T(8,128)S(1)}, u32[]{:S(2)}, u32[]{:S(2)}) collective-permute-start(f32[6,16,256]{2,1,0:T(8,128)S(1)} %get-tuple-element.25), channel_id=1, source_target_pairs={{0,1},{1,0},{2,3},{3,2},{4,5},{5,4},{6,7},{7,6},{8,9},{9,8},{10,11... | collective-permute-start | bytes 294920 | tf_op jit(solution)/shard_map/ppermute | solution.py:506
  4.1 0.0 collective-permute-start.1
  4.1 2.8 %collective-permute-done.refs_1_ = f32[6,16,256]{2,1,0:T(8,128)S(1)} collective-permute-done((f32[6,16,256]{2,1,0:T(8,128)S(1)}, f32[6,16,256]{2,1,0:T(8,128)S(1)}, u32[]{:S(2)}, u32[]{:S(2)}) %collective-permute-start) | collective-permute-done | bytes 98336 | tf_op jit(solution)/shard_map/ppermute | solution.py:506
  6.8 0.0 collective-permute-done.1.refs_2_
  6.9 0.2 shard_map.18
  7.0 1.8 %collective-permute-start.2 = (f32[96,256]{1,0:T(8,128)S(1)}, f32[96,256]{1,0:T(8,128)S(1)}, u32[]{:S(2)}, u32[]{:S(2)}) collective-permute-start(f32[96,256]{1,0:T(8,128)S(1)} %get-tuple-element.28), channel_id=1, source_target_pairs={{0,16},{16,0},{1,17},{17,1},{2,18},{18,2},{3,19},{19,3},{4,20},{20... | collective-permute-start | bytes 294920 | tf_op jit(solution)/shard_map/ppermute | solution.py:506
  8.8 0.0 collective-permute-start.3
  8.9 1.6 %collective-permute-start.4 = (f32[8,256]{1,0:T(8,128)S(1)}, f32[8,256]{1,0:T(8,128)S(1)}, u32[]{:S(2)}, u32[]{:S(2)}) collective-permute-start(f32[8,256]{1,0:T(8,128)S(1)} %get-tuple-element.30), channel_id=1, source_target_pairs={{0,12},{4,8},{8,4},{12,0},{1,13},{5,9},{9,5},{13,1},{2,14},{6,10},... | collective-permute-start | bytes 24584 | tf_op jit(solution)/shard_map/ppermute | solution.py:506
  10.5 0.1 collective-permute-start.5
  10.6 1.5 %collective-permute-start.6 = (f32[8,128]{1,0:T(8,128)S(1)}, f32[8,128]{1,0:T(8,128)S(1)}, u32[]{:S(2)}, u32[]{:S(2)}) collective-permute-start(f32[8,128]{1,0:T(8,128)S(1)} %get-tuple-element.32), channel_id=1, source_target_pairs={{0,28},{4,24},{8,20},{12,16},{16,12},{20,8},{24,4},{28,0},{1,29},{... | collective-permute-start | bytes 12296 | tf_op jit(solution)/shard_map/ppermute | solution.py:506
  12.2 1.3 %collective-permute-done.5.refs_5_ = f32[8,128]{1,0:T(8,128)S(1)} collective-permute-done((f32[8,128]{1,0:T(8,128)S(1)}, f32[8,128]{1,0:T(8,128)S(1)}, u32[]{:S(2)}, u32[]{:S(2)}) %collective-permute-start.5) | collective-permute-done | bytes 4128 | tf_op jit(solution)/shard_map/ppermute | solution.py:506
  13.5 1.0 %collective-permute-done.6.refs_6_ = f32[8,128]{1,0:T(8,128)S(1)} collective-permute-done((f32[8,128]{1,0:T(8,128)S(1)}, f32[8,128]{1,0:T(8,128)S(1)}, u32[]{:S(2)}, u32[]{:S(2)}) %collective-permute-start.6) | collective-permute-done | bytes 4128 | tf_op jit(solution)/shard_map/ppermute | solution.py:506
  14.6 0.0 collective-permute-done.3.refs_3_
  14.6 0.0 collective-permute-done.4.refs_4_
  14.6 0.0 collective-permute-done.2.refs_2_
  14.6 1.1 %shard_map.19 = (f32[3,16,40,128]{3,2,1,0:T(8,128)S(1)}, f32[3,7,16,256]{3,2,1,0:T(8,128)S(1)}, f32[6,16,256]{2,1,0:T(8,128)S(1)}) custom-call(f32[8,16,256]{2,1,0:T(8,128)S(1)} %get-tuple-element.24.refs_0_, f32[2,16,16,128]{3,2,1,0:T(8,128)S(1)} %get-tuple-element.27.refs_1_, f32[96,256]{1,0:T(8,128)S(1)} %collective-permute-done.2.refs_2_, ...), custom_call_target="tpu_custom_call" | custom-call | tf_op jit(solution)/shard_map/pallas_call | solution.py:546
  15.7 2.8 %collective-permute-start.7 = (f32[6,16,256]{2,1,0:T(8,128)S(1)}, f32[6,16,256]{2,1,0:T(8,128)S(1)}, u32[]{:S(2)}, u32[]{:S(2)}) collective-permute-start(f32[6,16,256]{2,1,0:T(8,128)S(1)} %get-tuple-element.38.refs_0_.refs_5_), channel_id=1, source_target_pairs={{0,1},{1,0},{2,3},{3,2},{4,5},{5,4},{6,7},{7,6},{8,9},{9,8},{10,11... | collective-permute-start | bytes 294920 | tf_op jit(solution)/shard_map/ppermute | solution.py:506
  18.4 1.4 %shard_map.20 = (f32[3,15,8,256]{3,2,1,0:T(8,128)S(1)}, f32[3,15,2,8,128]{4,3,2,1,0:T(8,128)S(1)}, f32[4,3,8,128]{3,2,1,0:T(8,128)S(1)}, f32[2,8,256]{2,1,0:T(8,128)S(1)}, f32[8,128]{1,0:T(8,128)S(1)}) custom-call(f32[8,16,256]{2,1,0:T(8,128)S(1)} %get-tuple-element.24.refs_0_, f32[3,16,40,128]{3,2,1,0:T(8,128)S(1)} %get-tuple-element.34.refs_1_), custom_call_target="tpu_custom_call" | custom-call | tf_op jit(solution)/shard_map/pallas_call | solution.py:546
  19.9 0.3 collective-permute-start.8
  20.2 0.9 %collective-permute-done.8.refs_3_.refs_11_ = f32[8,128]{1,0:T(8,128)S(1)} collective-permute-done((f32[8,128]{1,0:T(8,128)S(1)}, f32[8,128]{1,0:T(8,128)S(1)}, u32[]{:S(2)}, u32[]{:S(2)}) %collective-permute-start.8) | collective-permute-done | bytes 4128 | tf_op jit(solution)/shard_map/ppermute | solution.py:506
  21.1 0.8 %collective-permute-done.7.refs_1_.refs_6_ = f32[6,16,256]{2,1,0:T(8,128)S(1)} collective-permute-done((f32[6,16,256]{2,1,0:T(8,128)S(1)}, f32[6,16,256]{2,1,0:T(8,128)S(1)}, u32[]{:S(2)}, u32[]{:S(2)}) %collective-permute-start.7) | collective-permute-done | bytes 98336 | tf_op jit(solution)/shard_map/ppermute | solution.py:506
  22.0 3.3 %collective-permute-start.9 = (f32[2,16,256]{2,1,0:T(8,128)S(1)}, f32[2,16,256]{2,1,0:T(8,128)S(1)}, u32[]{:S(2)}, u32[]{:S(2)}) collective-permute-start(f32[2,16,256]{2,1,0:T(8,128)S(1)} %get-tuple-element.40), channel_id=1, source_target_pairs={{0,2},{1,3},{2,0},{3,1},{4,6},{5,7},{6,4},{7,5},{8,10},{9,11},{10,... | collective-permute-start | bytes 98312 | tf_op jit(solution)/shard_map/ppermute | solution.py:506
  25.2 1.5 %collective-permute-start.10 = (f32[2,8,256]{2,1,0:T(8,128)S(1)}, f32[2,8,256]{2,1,0:T(8,128)S(1)}, u32[]{:S(2)}, u32[]{:S(2)}) collective-permute-start(f32[2,8,256]{2,1,0:T(8,128)S(1)} %get-tuple-element.41.refs_8_), channel_id=1, source_target_pairs={{0,16},{16,0},{1,17},{17,1},{2,18},{18,2},{3,19},{19,3},{4,20},{20... | collective-permute-start | bytes 49160 | tf_op jit(solution)/shard_map/ppermute | solution.py:506
  26.7 0.5 %collective-permute-start.11 = (f32[8,128]{1,0:T(8,128)S(1)}, f32[8,128]{1,0:T(8,128)S(1)}, u32[]{:S(2)}, u32[]{:S(2)}) collective-permute-start(f32[8,128]{1,0:T(8,128)S(1)} %get-tuple-element.42), channel_id=1, source_target_pairs={{0,8},{4,12},{8,0},{12,4},{1,9},{5,13},{9,1},{13,5},{2,10},{6,14},... | collective-permute-start | bytes 12296 | tf_op jit(solution)/shard_map/ppermute | solution.py:506
  27.2 1.7 %collective-permute-done.10.refs_9_ = f32[2,8,256]{2,1,0:T(8,128)S(1)} collective-permute-done((f32[2,8,256]{2,1,0:T(8,128)S(1)}, f32[2,8,256]{2,1,0:T(8,128)S(1)}, u32[]{:S(2)}, u32[]{:S(2)}) %collective-permute-start.10) | collective-permute-done | bytes 16416 | tf_op jit(solution)/shard_map/ppermute | solution.py:506
  29.0 1.4 %collective-permute-done.11.refs_12_ = f32[8,128]{1,0:T(8,128)S(1)} collective-permute-done((f32[8,128]{1,0:T(8,128)S(1)}, f32[8,128]{1,0:T(8,128)S(1)}, u32[]{:S(2)}, u32[]{:S(2)}) %collective-permute-start.11) | collective-permute-done | bytes 4128 | tf_op jit(solution)/shard_map/ppermute | solution.py:506
  30.3 0.0 collective-permute-done.9.refs_7_
  30.3 1.0 %shard_map.22 = f32[8,16,256]{2,1,0:T(8,128)} custom-call(f32[8,16,256]{2,1,0:T(8,128)S(1)} %get-tuple-element.24.refs_0_, f32[3,7,16,256]{3,2,1,0:T(8,128)S(1)} %get-tuple-element.33.refs_1_, f32[3,15,8,256]{3,2,1,0:T(8,128)S(1)} %get-tuple-element.35.refs_2_, f32[3,15,2,8,128]{4,3,2,1,0:T(8,128)S(1)} %get-tuple-element.36.refs_3_, ...), custom_call_target="tpu_custom_call" | custom-call | tf_op jit(solution)/shard_map/pallas_call | solution.py:546
  (2 shorter events, 0.1 us)
Async XLA Ops:
  0.0 0.9 %copy-start = (f32[8,16,256]{2,1,0:T(8,128)S(1)}, f32[8,16,256]{2,1,0:T(8,128)}, u32[]{:S(2)}) copy-start(f32[8,16,256]{2,1,0:T(8,128)} %volume.1) | copy-start | bytes 393220
  0.9 5.9 %collective-permute-start = (f32[6,16,256]{2,1,0:T(8,128)S(1)}, f32[6,16,256]{2,1,0:T(8,128)S(1)}, u32[]{:S(2)}, u32[]{:S(2)}) collective-permute-start(f32[6,16,256]{2,1,0:T(8,128)S(1)} %get-tuple-element.25), channel_id=1, source_target_pairs={{0,1},{1,0},{2,3},{3,2},{4,5},{5,4},{6,7},{7,6},{8,9},{9,8},{10,11... | collective-permute-start | bytes 294920 | tf_op jit(solution)/shard_map/ppermute | solution.py:506
  4.1 2.8 %collective-permute-start.1 = (f32[6,16,256]{2,1,0:T(8,128)S(1)}, f32[6,16,256]{2,1,0:T(8,128)S(1)}, u32[]{:S(2)}, u32[]{:S(2)}) collective-permute-start(f32[6,16,256]{2,1,0:T(8,128)S(1)} %get-tuple-element.26), channel_id=1, source_target_pairs={{0,4},{1,2},{2,1},{3,7},{4,0},{5,6},{6,5},{7,3},{8,12},{9,10},{10,... | collective-permute-start | bytes 294920 | tf_op jit(solution)/shard_map/ppermute | solution.py:506
  7.0 7.5 %collective-permute-start.2 = (f32[96,256]{1,0:T(8,128)S(1)}, f32[96,256]{1,0:T(8,128)S(1)}, u32[]{:S(2)}, u32[]{:S(2)}) collective-permute-start(f32[96,256]{1,0:T(8,128)S(1)} %get-tuple-element.28), channel_id=1, source_target_pairs={{0,16},{16,0},{1,17},{17,1},{2,18},{18,2},{3,19},{19,3},{4,20},{20... | collective-permute-start | bytes 294920 | tf_op jit(solution)/shard_map/ppermute | solution.py:506
  8.8 5.7 %collective-permute-start.3 = (f32[8,256]{1,0:T(8,128)S(1)}, f32[8,256]{1,0:T(8,128)S(1)}, u32[]{:S(2)}, u32[]{:S(2)}) collective-permute-start(f32[8,256]{1,0:T(8,128)S(1)} %get-tuple-element.29), channel_id=1, source_target_pairs={{0,4},{4,0},{8,12},{12,8},{1,5},{5,1},{9,13},{13,9},{2,6},{6,2},{1... | collective-permute-start | bytes 24584 | tf_op jit(solution)/shard_map/ppermute | solution.py:506
  8.9 5.7 %collective-permute-start.4 = (f32[8,256]{1,0:T(8,128)S(1)}, f32[8,256]{1,0:T(8,128)S(1)}, u32[]{:S(2)}, u32[]{:S(2)}) collective-permute-start(f32[8,256]{1,0:T(8,128)S(1)} %get-tuple-element.30), channel_id=1, source_target_pairs={{0,12},{4,8},{8,4},{12,0},{1,13},{5,9},{9,5},{13,1},{2,14},{6,10},... | collective-permute-start | bytes 24584 | tf_op jit(solution)/shard_map/ppermute | solution.py:506
  10.5 3.0 %collective-permute-start.5 = (f32[8,128]{1,0:T(8,128)S(1)}, f32[8,128]{1,0:T(8,128)S(1)}, u32[]{:S(2)}, u32[]{:S(2)}) collective-permute-start(f32[8,128]{1,0:T(8,128)S(1)} %get-tuple-element.31), channel_id=1, source_target_pairs={{0,20},{4,16},{8,28},{12,24},{16,4},{20,0},{24,12},{28,8},{1,21},{... | collective-permute-start | bytes 12296 | tf_op jit(solution)/shard_map/ppermute | solution.py:506
  10.6 3.9 %collective-permute-start.6 = (f32[8,128]{1,0:T(8,128)S(1)}, f32[8,128]{1,0:T(8,128)S(1)}, u32[]{:S(2)}, u32[]{:S(2)}) collective-permute-start(f32[8,128]{1,0:T(8,128)S(1)} %get-tuple-element.32), channel_id=1, source_target_pairs={{0,28},{4,24},{8,20},{12,16},{16,12},{20,8},{24,4},{28,0},{1,29},{... | collective-permute-start | bytes 12296 | tf_op jit(solution)/shard_map/ppermute | solution.py:506
  15.7 6.2 %collective-permute-start.7 = (f32[6,16,256]{2,1,0:T(8,128)S(1)}, f32[6,16,256]{2,1,0:T(8,128)S(1)}, u32[]{:S(2)}, u32[]{:S(2)}) collective-permute-start(f32[6,16,256]{2,1,0:T(8,128)S(1)} %get-tuple-element.38.refs_0_.refs_5_), channel_id=1, source_target_pairs={{0,1},{1,0},{2,3},{3,2},{4,5},{5,4},{6,7},{7,6},{8,9},{9,8},{10,11... | collective-permute-start | bytes 294920 | tf_op jit(solution)/shard_map/ppermute | solution.py:506
  19.9 1.2 %collective-permute-start.8 = (f32[8,128]{1,0:T(8,128)S(1)}, f32[8,128]{1,0:T(8,128)S(1)}, u32[]{:S(2)}, u32[]{:S(2)}) collective-permute-start(f32[8,128]{1,0:T(8,128)S(1)} %get-tuple-element.39.refs_2_.refs_10_), channel_id=1, source_target_pairs={{0,4},{4,0},{8,12},{12,8},{1,5},{5,1},{9,13},{13,9},{2,6},{6,2},{1... | collective-permute-start | bytes 12296 | tf_op jit(solution)/shard_map/ppermute | solution.py:506
  22.0 8.4 %collective-permute-start.9 = (f32[2,16,256]{2,1,0:T(8,128)S(1)}, f32[2,16,256]{2,1,0:T(8,128)S(1)}, u32[]{:S(2)}, u32[]{:S(2)}) collective-permute-start(f32[2,16,256]{2,1,0:T(8,128)S(1)} %get-tuple-element.40), channel_id=1, source_target_pairs={{0,2},{1,3},{2,0},{3,1},{4,6},{5,7},{6,4},{7,5},{8,10},{9,11},{10,... | collective-permute-start | bytes 98312 | tf_op jit(solution)/shard_map/ppermute | solution.py:506
  25.2 3.7 %collective-permute-start.10 = (f32[2,8,256]{2,1,0:T(8,128)S(1)}, f32[2,8,256]{2,1,0:T(8,128)S(1)}, u32[]{:S(2)}, u32[]{:S(2)}) collective-permute-start(f32[2,8,256]{2,1,0:T(8,128)S(1)} %get-tuple-element.41.refs_8_), channel_id=1, source_target_pairs={{0,16},{16,0},{1,17},{17,1},{2,18},{18,2},{3,19},{19,3},{4,20},{20... | collective-permute-start | bytes 49160 | tf_op jit(solution)/shard_map/ppermute | solution.py:506
  26.7 3.6 %collective-permute-start.11 = (f32[8,128]{1,0:T(8,128)S(1)}, f32[8,128]{1,0:T(8,128)S(1)}, u32[]{:S(2)}, u32[]{:S(2)}) collective-permute-start(f32[8,128]{1,0:T(8,128)S(1)} %get-tuple-element.42), channel_id=1, source_target_pairs={{0,8},{4,12},{8,0},{12,4},{1,9},{5,13},{9,1},{13,5},{2,10},{6,14},... | collective-permute-start | bytes 12296 | tf_op jit(solution)/shard_map/ppermute | solution.py:506

commit v6 on v5

--- a/solution.py
+++ b/solution.py
@@ -47,13 +47,13 @@
 
 
 def merge(low, high):
-    a0, an, g00, g0n, gnn, c = low
-    b0, bn, h00, h0n, hnn, e = high
-    w = c / (1.0 + c * (gnn + h00))
+    a0, an, g00, g0n, y = low
+    b0, bn, h00, h0n, e = high
+    w = y / (1.0 + y * h00)
     flux = w * (b0 - an)
     by_left = w * g0n
     by_right = w * h0n
-    joined = (a0 + g0n * flux, bn - h0n * flux, g00 - g0n * by_left, by_left * h0n, hnn - h0n * by_right, e)
+    joined = (a0 + g0n * flux, bn - h0n * flux, g00 - g0n * by_left, by_left * h0n, e / (1.0 - e * (h0n * by_right)))
     return joined, (flux, by_left, by_right)
 
 
@@ -64,8 +64,8 @@
 
 
 def last_message(upper, seg):
-    a0, an, g00, _, gnn, c = seg
-    return (jnp.where(upper, a0, an), jnp.where(upper, g00, c / (1.0 + c * gnn)))
+    a0, an, g00, _, y = seg
+    return jnp.where(upper, a0, an), jnp.where(upper, g00, y)
 
 
 def bit_of(position, level):
@@ -114,7 +114,8 @@
         g00 = g00 - g0n * hw
         g0n = hw
         gnn = 1.0 - w
-    return a0, an, g00, g0n, gnn, c(count - 1)
+    face = c(count - 1)
+    return a0, an, g00, g0n, face / (1.0 + face * gnn)
 
 
 def substitute(factors, count, left, right, emit):
@@ -125,6 +126,16 @@
         emit(i + 1, above - flux)
         above = flux
     emit(0, above + left)
+
+
+def responses(factors, count, emit):
+    base, by_left, by_right = 0.0, 0.0, 1.0
+    for i in reversed(range(count - 1)):
+        w, d, h = factors(i)
+        flux = w * (d + base), w * (by_left - h), w * by_right
+        emit(i + 1, base - flux[0], by_left - flux[1], by_right - flux[2])
+        base, by_left, by_right = flux
+    emit(0, base, by_left + 1.0, by_right)
 
 
 def cut(t):
@@ -192,21 +203,32 @@
 
         z_blur(load, store, nb, taps())
 
-    def strips(first_tile, last_tile, targets):
-        first = first_tile.T[:edge, :]
-        last = last_tile.T[lanes - edge:, :]
-        for f, target in enumerate(targets):
-            ref, cols = target
-            ref[:, cols] = jnp.where(odd_y, last, first) if f else jnp.where(odd_y, first, last)
-
     per = lanes // nx
     for chunk in range(nb // per):
         tiles = [out[t, chunk * per:(chunk + 1) * per].reshape(lanes, lanes) for t in (0, nt - 1)]
-        strips(*tiles, [(ref, cut(chunk)) for ref in y_sends])
+        for f, ref in enumerate(y_sends):
+            ref[:, cut(chunk)] = strip(odd_y, f, *tiles)
     pad = jnp.zeros((lanes - nb * halo, lanes), jnp.float32)
-    for e, ref in enumerate(x_sends):
+    for ref, corner in zip(x_sends, corner_sends):
+        corner[...] = strip(odd_y, 1, *[jnp.concatenate([ref[:, cut(t)], pad], axis=0) for t in (0, nt - 1)])
+
+
+def strip(odd_y, f, first_tile, last_tile):
+    first, last = first_tile.T[:edge, :], last_tile.T[lanes - edge:, :]
+    return jnp.where(odd_y, last, first) if f else jnp.where(odd_y, first, last)
+
+
+def pack_kernel(dims, *refs):
+    nz, nx, ny = dims
+    nt, nb = ny // lanes, nz + 8
+    own, xr, out = refs[0], refs[1:-1], refs[-1]
+    odd_y = lax.axis_index("gy") % 2 == 1
+    out[:, :nb * nx] = own[...]
+    pad = jnp.zeros((lanes - nb * halo, lanes), jnp.float32)
+    for e, ref in enumerate(xr):
         tiles = [jnp.concatenate([ref[:, cut(t)], pad], axis=0) for t in (0, nt - 1)]
-        strips(*tiles, [(corner, slice(None)) for corner in corner_sends[e * pairs[2]:(e + 1) * pairs[2]]])
+        begin = nb * nx + e * lanes
+        out[:, begin:begin + lanes] = strip(odd_y, 0, *tiles)
 
 
 def grid_masks(dims, counts):
@@ -254,7 +276,7 @@
     v, zb = refs.pop(0), refs.pop(0)
     xr = [refs.pop(0) for _ in range(pairs[1])]
     yr = [refs.pop(0) for _ in range(pairs[2])]
-    corners = [[refs.pop(0) for _ in range(pairs[2])] for _ in range(pairs[1])]
+    far = [refs.pop(0) for _ in range(pairs[1] if pairs[2] > 1 else 0)]
     bb, fz, send_z, wide, t1, cz = refs
     at_z, at_x, at_y = lax.axis_index("gz"), lax.axis_index("gx"), lax.axis_index("gy")
     nb, rows_b = nz + 8, nx + 8
@@ -277,7 +299,11 @@
         sides(t, lambda ref, rows: ref[rows, cut(t)], xr)
         for i in range(nb):
             wide[t, i, edge:edge + nx, :] = zb[t, i]
-    sides(nt, lambda tile, rows: tile[rows, :], [halo_tile(group, slice(None)) for group in corners])
+    corners = []
+    for e in range(pairs[1]):
+        begin = nb * nx + e * lanes
+        corners.append(halo_tile([yr[0].at[:, begin:begin + lanes]] + far[e:e + 1], slice(None)))
+    sides(nt, lambda tile, rows: tile[rows, :], corners)
     per = lanes // nx
     for chunk in range(nb // per):
         turned = halo_tile(yr, cut(chunk))
@@ -421,7 +447,7 @@
     groups = [[refs.pop(0) for _ in range(level + 2)] for _ in axes]
     for axis, group, out in zip(axes, groups, refs):
         position = lax.axis_index(("gz", "gx", "gy")[axis])
-        own, *received = [summary(ref, axis, 6) for ref in group]
+        own, *received = [summary(ref, axis, 5) for ref in group]
         seg, _ = climb(position, own, received)
         if depths[axis] == level + 2:
             seg = last_message(bit_of(position, level + 1), seg)
@@ -432,65 +458,98 @@
                 out[i] = value
 
 
+def fluxes_of(axis, depths, group):
+    position = lax.axis_index(("gz", "gx", "gy")[axis])
+    if depths[axis] == 1:
+        upper = bit_of(position, 0)
+        mine, final = [summary(ref, axis, 2) for ref in group]
+        (low_a, low_y), (high_a, high_g) = pick(upper, mine, final)
+        flux = low_y * (high_a - low_a) / (1.0 + low_y * high_g)
+        return jnp.where(upper, -flux, 0.0), jnp.where(upper, 0.0, flux)
+    own, *received = [summary(ref, axis, 5) for ref in group[:-1]]
+    return end_fluxes(position, own, received, summary(group[-1], axis, 2))
+
+
+def solve_x(dims, factors, fluxes, target):
+    nz, nx, ny = dims
+
+    def emit(i, value):
+        for t in range(ny // lanes):
+            target[t, pl.ds(i, nz, stride=nx), :] = value[:, cut(t)]
+
+    substitute(lambda i: (factors[0, i], factors[1, i], factors[2, i]), nx, *fluxes, emit)
+
+
+def prepare_kernel(dims, depths, *refs):
+    nz, nx, ny = dims
+    refs = list(refs)
+    v, fz, fx, fy, cy = [refs.pop(0) for _ in range(5)]
+    group = [refs.pop(0) for _ in range(2 if depths[1] == 1 else 0)]
+    base, by_z, by_y, sx = refs
+    third = 1.0 / 3.0
+    if group:
+        solve_x(dims, fx, fluxes_of(1, depths, group), sx)
+
+    sub = lax.broadcasted_iota(jnp.int32, (8, lanes), 0)
+    zero = jnp.zeros((8, lanes), jnp.float32)
+    left, right = (zero, zero + 1.0, zero), (zero, zero, zero + 1.0)
+
+    def crossing(level):
+        const, by_left, by_right = [cy[level, i] for i in range(3)]
+        terms = [by_right * r - by_left * l for l, r in zip(left, right)]
+        return [terms[0] + const] + terms[1:]
+
+    for level in (2, 1, 0):
+        stride = 2**level
+        flux = crossing(level + 1)
+        lower = sub % (2 * stride) == 0
+        left, right = ([jnp.where(lower, l, -pltpu.roll(f, stride, axis=0)) for l, f in zip(left, flux)],
+                       [jnp.where(lower, f, pltpu.roll(r, stride, axis=0)) for r, f in zip(right, flux)])
+    flux = crossing(0)
+    steps = ny // 16
+    for half, (a, b) in enumerate(((left, flux), ([-f for f in flux], right))):
+        a, b = [m * third for m in a], [m * third for m in b]
+
+        def emit(i, own, by_left, by_right, half=half, a=a, b=b):
+            at = pl.ds(half * steps + i, 8, stride=2 * steps)
+            for m in range(3):
+                value = by_left * a[m] + by_right * b[m]
+                by_y[m, at, :] = value + own * third if m == 0 else value
+
+        responses(lambda i, half=half: (fy[0, i, half], fy[1, i, half], fy[2, i, half]), steps, emit)
+
+    def emit_z(i, own, by_left, by_right):
+        total = own
+        if group:
+            total = total + jnp.concatenate([sx[t, i * nx:(i + 1) * nx, :] for t in range(ny // lanes)], axis=1)
+        base[i] = v[i] + total * third
+        by_z[0, i] = jnp.broadcast_to(by_left * third, (nx, ny))
+        by_z[1, i] = jnp.broadcast_to(by_right * third, (nx, ny))
+
+    responses(lambda i: (fz[0, i], fz[1, i], fz[2, i]), nz, emit_z)
+
+
 def last_kernel(dims, depths, *refs):
     nz, nx, ny = dims
     nt = ny // lanes
     refs = list(refs)
-    v, fz, fx, fy, cy = [refs.pop(0) for _ in range(5)]
-    groups = [[refs.pop(0) for _ in range(depths[axis] + 1)] for axis in range(3)]
-    out, acc, st, sx = refs
-    fluxes = []
-    for axis, group in enumerate(groups):
-        position = lax.axis_index(("gz", "gx", "gy")[axis])
-        if depths[axis] == 1:
-            upper = bit_of(position, 0)
-            mine, final = [summary(ref, axis, 2) for ref in group]
-            (low_a, low_y), (high_a, high_g) = pick(upper, mine, final)
-            flux = low_y * (high_a - low_a) / (1.0 + low_y * high_g)
-            fluxes.append((jnp.where(upper, -flux, 0.0), jnp.where(upper, 0.0, flux)))
-        else:
-            own, *received = [summary(ref, axis, 6) for ref in group[:-1]]
-            fluxes.append(end_fluxes(position, own, received, summary(group[-1], axis, 2)))
-
-    left, right = fluxes[2]
-    left = jnp.broadcast_to(left, (8, lanes))
-    right = jnp.broadcast_to(right, (8, lanes))
-    sub = lax.broadcasted_iota(jnp.int32, (8, lanes), 0)
-    for level in (2, 1, 0):
-        stride = 2**level
-        const, by_left, by_right = [cy[level + 1, i] for i in range(3)]
-        flux = const + by_right * right - by_left * left
-        lower = sub % (2 * stride) == 0
-        left, right = (jnp.where(lower, left, -pltpu.roll(flux, stride, axis=0)),
-                       jnp.where(lower, flux, pltpu.roll(right, stride, axis=0)))
-    flux = cy[0, 0] + cy[0, 2] * right - cy[0, 1] * left
-    steps = ny // 16
-    for half, (a, b) in enumerate(((left, flux), (-flux, right))):
-        def factors(i, half=half):
-            return fy[0, i, half], fy[1, i, half], fy[2, i, half]
-
-        def emit(i, value, half=half):
-            st[pl.ds(half * steps + i, 8, stride=2 * steps), :] = value
-
-        substitute(factors, steps, a, b, emit)
-
-    def emit_x(i, value):
+    base, by_z, by_y, fx = [refs.pop(0) for _ in range(4)]
+    groups = {axis: [refs.pop(0) for _ in range(depths[axis] + 1)] for axis in range(3) if axis != 1 or depths[1] > 1}
+    out, st, sx = refs
+    left, right = fluxes_of(2, depths, groups[2])
+    for t in range(nt):
+        st[t] = (by_y[0, cut(t), :] + by_y[1, cut(t), :] * left + by_y[2, cut(t), :] * right).T
+    if 1 in groups:
+        solve_x(dims, fx, fluxes_of(1, depths, groups[1]), sx)
+    left, right = fluxes_of(0, depths, groups[0])
+    for z in range(nz):
+        total = base[z] + by_z[0, z] * left + by_z[1, z] * right
+        rows = slice(z * nx, (z + 1) * nx)
         for t in range(nt):
-            sx[t, pl.ds(i, nz, stride=nx), :] = value[:, t * lanes:(t + 1) * lanes]
-
-    substitute(lambda i: (fx[0, i], fx[1, i], fx[2, i]), nx, *fluxes[1], emit_x)
-
-    def emit_z(i, value):
-        acc[i] = value
-
-    substitute(lambda i: (fz[0, i], fz[1, i], fz[2, i]), nz, *fluxes[0], emit_z)
-    for t in range(nt):
-        cols = slice(t * lanes, (t + 1) * lanes)
-        turned = st[cols, :].T
-        for z in range(nz):
-            rows = slice(z * nx, (z + 1) * nx)
-            total = acc[z, :, cols] + sx[t, rows, :] + turned[rows, :]
-            out[z, :, cols] = v[z, :, cols] + total * (1.0 / 3.0)
+            value = total[:, cut(t)] + st[t, rows, :]
+            if 1 in groups:
+                value = value + sx[t, rows, :] * (1.0 / 3.0)
+            out[z, :, cut(t)] = value
 
 
 def partners(n, start):
@@ -553,16 +612,21 @@
         functools.partial(open_kernel, dims), [f32(*dims)] + [f32(halo, nx, ny)] * pairs[0], [], volume)
     z_received = [swap_z(value, e) for e, value in enumerate(z_sends)]
     ex, ey = range(pairs[1]), range(pairs[2])
+    far = ex if pairs[2] > 1 else []
     blurred_z, *sends = call(
         functools.partial(z_kernel, dims, counts, pairs),
         [f32(nt, nb, nx, lanes)] + [f32(nb * halo, ny) for e in ex] + [f32(edge, nb * nx) for f in ey]
-        + [f32(edge, lanes) for e in ex for f in ey], [], volume, *z_received)
+        + [f32(edge, lanes) for e in far], [], volume, *z_received)
     x_received = [swap_pair(sends[e], "gx", e) for e in ex]
-    y_received = [swap_pair(sends[pairs[1] + f], "gy", f) for f in reversed(ey)][::-1]
-    corners = [swap_corner(sends[pairs[1] + pairs[2] + e * pairs[2] + f], e, f) for e in ex for f in ey]
+    y_sends = sends[pairs[1]:pairs[1] + pairs[2]]
+    corners = [swap_corner(sends[pairs[1] + pairs[2] + e], e, 1) for e in far]
+    y_received = [swap_pair(value, "gy", 1) for value in y_sends[1:]]
+    y_sends[0], = call(functools.partial(pack_kernel, dims), [f32(edge, nb * nx + pairs[1] * lanes)], [],
+                       y_sends[0], *x_received)
+    y_received.insert(0, swap_pair(y_sends[0], "gy", 0))
 
     steps = ny // 16
-    send_shape = lambda d: 6 if d > 1 else 2
+    send_shape = lambda d: 5 if d > 1 else 2
     bb, fz, send_z = call(
         functools.partial(main_kernel, dims, counts, pairs),
         [f32(nt + 1, nb, rows_b + 2 * edge, lanes), f32(3, nz - 1, nx, ny), f32(send_shape(depths[0]), nx, ny)],
@@ -586,16 +650,20 @@
         if axes:
             shapes = []
             for axis in axes:
-                count = 2 if depths[axis] == level + 2 else 6
+                count = 2 if depths[axis] == level + 2 else 5
                 shapes.append(f32(8, lanes) if axis == 2 else f32(count, *((nx, ny) if axis == 0 else (nz, ny))))
             sent = call(functools.partial(merge_kernel, level, depths, axes), shapes, [],
                         *[ref for axis in axes for ref in groups[axis]])
             for axis, value in zip(axes, sent):
                 message[axis] = value
+    x_group = groups[1] if depths[1] == 1 else []
+    base, by_z, by_y = call(
+        functools.partial(prepare_kernel, dims, depths), [f32(*dims), f32(2, *dims), f32(3, ny, lanes)],
+        [scratch(nt, lanes, lanes)], volume, fz, fx, fy, cy, *x_group)
+    rest = groups[0] + ([] if x_group else groups[1]) + groups[2]
     return call(
         functools.partial(last_kernel, dims, depths), [f32(*dims)],
-        [scratch(*dims), scratch(ny, lanes), scratch(nt, lanes, lanes)],
-        volume, fz, fx, fy, cy, *groups[0], *groups[1], *groups[2])[0]
+        [scratch(nt, lanes, lanes), scratch(nt, lanes, lanes)], base, by_z, by_y, fx, *rest)[0]
 
 
 def solution(mesh):

time: 31.4 us -> 33.6 us (1.070)
  waiting for transfers between devices: 10 us -> 12.3 us
  starting transfers between devices: 16.6 us -> 16.1 us
  Pallas kernels: 3.74 us -> 4.12 us
    ppermute x12 -> x11, waiting for transfers between devices: 10 us -> 12.3 us  [permute(): return lax.ppermute(value, axes if len(axes) > 1 else axes[0], moves)]
    ppermute x12 -> x11, starting transfers between devices: 16.6 us -> 16.1 us  [permute(): return lax.ppermute(value, axes if len(axes) > 1 else axes[0], moves)]
    pallas_call x6 -> x8, Pallas kernels: 3.74 us -> 4.12 us  [call(): pl.pallas_call(kernel, out_shape=out_shape, in_specs=[VMEM] * len(args),...]
  transfers between devices with their start and end apart: 12 -> 11, of which waited for: 7 -> 6; matrix products, arithmetic and copies ran while one was open for 0% -> 0% of each run, Pallas kernels for 5% -> 6%
where the time goes in v6:
time: 33.6 us; the launch traced here: 33.5 us
  starting transfers between devices  16.1 us (48%)
  waiting for transfers between devices  12.3 us (37%)
  Pallas kernels  4.12 us (12%)
  local copies, waits for them, and re-layouts  0.9 us (3%)
    ppermute x11, starting transfers between devices, permute(): return lax.ppermute(value, axes if len(axes) > 1 else axes[0], moves)  16.1 us
    ppermute x11, waiting for transfers between devices, permute(): return lax.ppermute(value, axes if len(axes) > 1 else axes[0], moves)  12.3 us
    pallas_call x8, Pallas kernels, call(): pl.pallas_call(kernel, out_shape=out_shape, in_specs=[VMEM] * len(args),...  4.12 us
    unnamed x2, local copies, waits for them, and re-layouts  0.9 us
  transfers between devices with their start and end apart: 11, of which 6 were waited for; matrix products, arithmetic and copies ran while one was open for 0% of the time, Pallas kernels for 6%

profile of v6, /device:TPU:0, one launch (start us, length us, event | category | flops | bytes accessed | tf_op | source)
XLA Modules:
  0.0 33.5 jit_solution(8101973267393861449)
XLA Ops:
  0.0 0.0 copy-start
  0.0 0.9 %copy-done = f32[8,16,256]{2,1,0:T(8,128)S(1)} copy-done((f32[8,16,256]{2,1,0:T(8,128)S(1)}, f32[8,16,256]{2,1,0:T(8,128)}, u32[]{:S(2)}) %copy-start) | copy-done | bytes 131096
  0.9 3.1 %collective-permute-start = (f32[6,16,256]{2,1,0:T(8,128)S(1)}, f32[6,16,256]{2,1,0:T(8,128)S(1)}, u32[]{:S(2)}, u32[]{:S(2)}) collective-permute-start(f32[6,16,256]{2,1,0:T(8,128)S(1)} %get-tuple-element.27), channel_id=1, source_target_pairs={{0,1},{1,0},{2,3},{3,2},{4,5},{5,4},{6,7},{7,6},{8,9},{9,8},{10,11... | collective-permute-start | bytes 294920 | tf_op jit(solution)/shard_map/ppermute | solution.py:565
  4.1 0.0 collective-permute-start.1
  4.1 2.8 %collective-permute-done.refs_1_ = f32[6,16,256]{2,1,0:T(8,128)S(1)} collective-permute-done((f32[6,16,256]{2,1,0:T(8,128)S(1)}, f32[6,16,256]{2,1,0:T(8,128)S(1)}, u32[]{:S(2)}, u32[]{:S(2)}) %collective-permute-start) | collective-permute-done | bytes 98336 | tf_op jit(solution)/shard_map/ppermute | solution.py:565
  6.8 0.0 collective-permute-done.1.refs_2_
  6.9 0.2 shard_map.18
  7.0 1.8 %collective-permute-start.2 = (f32[96,256]{1,0:T(8,128)S(1)}, f32[96,256]{1,0:T(8,128)S(1)}, u32[]{:S(2)}, u32[]{:S(2)}) collective-permute-start(f32[96,256]{1,0:T(8,128)S(1)} %get-tuple-element.30), channel_id=1, source_target_pairs={{0,16},{16,0},{1,17},{17,1},{2,18},{18,2},{3,19},{19,3},{4,20},{20... | collective-permute-start | bytes 294920 | tf_op jit(solution)/shard_map/ppermute | solution.py:565
  8.8 2.9 %collective-permute-done.2.refs_1_.refs_2_ = f32[96,256]{1,0:T(8,128)S(1)} collective-permute-done((f32[96,256]{1,0:T(8,128)S(1)}, f32[96,256]{1,0:T(8,128)S(1)}, u32[]{:S(2)}, u32[]{:S(2)}) %collective-permute-start.2) | collective-permute-done | bytes 98336 | tf_op jit(solution)/shard_map/ppermute | solution.py:565
  11.7 0.1 shard_map.19
  11.8 0.1 collective-permute-start.3
  11.9 1.9 %collective-permute-start.4 = (f32[8,256]{1,0:T(8,128)S(1)}, f32[8,256]{1,0:T(8,128)S(1)}, u32[]{:S(2)}, u32[]{:S(2)}) collective-permute-start(f32[8,256]{1,0:T(8,128)S(1)} %get-tuple-element.32), channel_id=1, source_target_pairs={{0,12},{4,8},{8,4},{12,0},{1,13},{5,9},{9,5},{13,1},{2,14},{6,10},... | collective-permute-start | bytes 24584 | tf_op jit(solution)/shard_map/ppermute | solution.py:565
  13.7 1.1 %collective-permute-start.5 = (f32[8,128]{1,0:T(8,128)S(1)}, f32[8,128]{1,0:T(8,128)S(1)}, u32[]{:S(2)}, u32[]{:S(2)}) collective-permute-start(f32[8,128]{1,0:T(8,128)S(1)} %get-tuple-element.33), channel_id=1, source_target_pairs={{0,28},{4,24},{8,20},{12,16},{16,12},{20,8},{24,4},{28,0},{1,29},{... | collective-permute-start | bytes 12296 | tf_op jit(solution)/shard_map/ppermute | solution.py:565
  14.9 2.8 %collective-permute-done.5.refs_5_ = f32[8,128]{1,0:T(8,128)S(1)} collective-permute-done((f32[8,128]{1,0:T(8,128)S(1)}, f32[8,128]{1,0:T(8,128)S(1)}, u32[]{:S(2)}, u32[]{:S(2)}) %collective-permute-start.5) | collective-permute-done | bytes 4128 | tf_op jit(solution)/shard_map/ppermute | solution.py:565
  17.7 0.0 collective-permute-done.4.refs_4_
  17.7 0.0 collective-permute-done.3.refs_3_
  17.7 1.1 %shard_map.20 = (f32[3,16,40,128]{3,2,1,0:T(8,128)S(1)}, f32[3,7,16,256]{3,2,1,0:T(8,128)S(1)}, f32[5,16,256]{2,1,0:T(8,128)S(1)}) custom-call(f32[8,16,256]{2,1,0:T(8,128)S(1)} %get-tuple-element.26.refs_0_, f32[2,16,16,128]{3,2,1,0:T(8,128)S(1)} %get-tuple-element.29.refs_1_, f32[96,256]{1,0:T(8,128)S(1)} %collective-permute-done.2.refs_1_.refs_2_, ...), custom_call_target="tpu_custom_call" | custom-call | tf_op jit(solution)/shard_map/pallas_call | solution.py:605
  18.8 2.8 %collective-permute-start.7 = (f32[5,16,256]{2,1,0:T(8,128)S(1)}, f32[5,16,256]{2,1,0:T(8,128)S(1)}, u32[]{:S(2)}, u32[]{:S(2)}) collective-permute-start(f32[5,16,256]{2,1,0:T(8,128)S(1)} %get-tuple-element.43.refs_0_.refs_4_), channel_id=1, source_target_pairs={{0,1},{1,0},{2,3},{3,2},{4,5},{5,4},{6,7},{7,6},{8,9},{9,8},{10,11... | collective-permute-start | bytes 245768 | tf_op jit(solution)/shard_map/ppermute | solution.py:565
  21.5 1.4 %shard_map.21 = (f32[3,15,8,256]{3,2,1,0:T(8,128)S(1)}, f32[3,15,2,8,128]{4,3,2,1,0:T(8,128)S(1)}, f32[4,3,8,128]{3,2,1,0:T(8,128)S(1)}, f32[2,8,256]{2,1,0:T(8,128)S(1)}, f32[8,128]{1,0:T(8,128)S(1)}) custom-call(f32[8,16,256]{2,1,0:T(8,128)S(1)} %get-tuple-element.26.refs_0_, f32[3,16,40,128]{3,2,1,0:T(8,128)S(1)} %get-tuple-element.35.refs_1_), custom_call_target="tpu_custom_call" | custom-call | tf_op jit(solution)/shard_map/pallas_call | solution.py:605
  23.0 0.1 collective-permute-start.8
  23.1 1.2 %collective-permute-done.8.refs_3_.refs_8_ = f32[8,128]{1,0:T(8,128)S(1)} collective-permute-done((f32[8,128]{1,0:T(8,128)S(1)}, f32[8,128]{1,0:T(8,128)S(1)}, u32[]{:S(2)}, u32[]{:S(2)}) %collective-permute-start.8) | collective-permute-done | bytes 4128 | tf_op jit(solution)/shard_map/ppermute | solution.py:565
  24.2 0.0 collective-permute-done.7.refs_1_.refs_5_
  24.3 3.3 %collective-permute-start.9 = (f32[2,16,256]{2,1,0:T(8,128)S(1)}, f32[2,16,256]{2,1,0:T(8,128)S(1)}, u32[]{:S(2)}, u32[]{:S(2)}) collective-permute-start(f32[2,16,256]{2,1,0:T(8,128)S(1)} %get-tuple-element.45), channel_id=1, source_target_pairs={{0,2},{1,3},{2,0},{3,1},{4,6},{5,7},{6,4},{7,5},{8,10},{9,11},{10,... | collective-permute-start | bytes 98312 | tf_op jit(solution)/shard_map/ppermute | solution.py:565
  27.6 1.5 %collective-permute-start.6 = (f32[2,8,256]{2,1,0:T(8,128)S(1)}, f32[2,8,256]{2,1,0:T(8,128)S(1)}, u32[]{:S(2)}, u32[]{:S(2)}) collective-permute-start(f32[2,8,256]{2,1,0:T(8,128)S(1)} %get-tuple-element.39.refs_5_), channel_id=1, source_target_pairs={{0,16},{16,0},{1,17},{17,1},{2,18},{18,2},{3,19},{19,3},{4,20},{20... | collective-permute-start | bytes 49160 | tf_op jit(solution)/shard_map/ppermute | solution.py:565
  29.1 0.5 %collective-permute-start.10 = (f32[8,128]{1,0:T(8,128)S(1)}, f32[8,128]{1,0:T(8,128)S(1)}, u32[]{:S(2)}, u32[]{:S(2)}) collective-permute-start(f32[8,128]{1,0:T(8,128)S(1)} %get-tuple-element.46), channel_id=1, source_target_pairs={{0,8},{4,12},{8,0},{12,4},{1,9},{5,13},{9,1},{13,5},{2,10},{6,14},... | collective-permute-start | bytes 12296 | tf_op jit(solution)/shard_map/ppermute | solution.py:565
  29.6 1.7 %collective-permute-done.6.refs_6_ = f32[2,8,256]{2,1,0:T(8,128)S(1)} collective-permute-done((f32[2,8,256]{2,1,0:T(8,128)S(1)}, f32[2,8,256]{2,1,0:T(8,128)S(1)}, u32[]{:S(2)}, u32[]{:S(2)}) %collective-permute-start.6) | collective-permute-done | bytes 16416 | tf_op jit(solution)/shard_map/ppermute | solution.py:565
  31.3 0.5 %shard_map.22 = (f32[8,16,256]{2,1,0:T(8,128)S(1)}, f32[2,8,16,256]{3,2,1,0:T(8,128)S(1)}, f32[3,256,128]{2,1,0:T(8,128)S(1)}) custom-call(f32[8,16,256]{2,1,0:T(8,128)S(1)} %get-tuple-element.26.refs_0_, f32[3,7,16,256]{3,2,1,0:T(8,128)S(1)} %get-tuple-element.34.refs_1_, f32[3,15,8,256]{3,2,1,0:T(8,128)S(1)} %get-tuple-element.36.refs_2_.refs_3_, ...), custom_call_target="tpu_custom_call" | custom-call | tf_op jit(solution)/shard_map/pallas_call | solution.py:605
  31.8 0.9 %collective-permute-done.10.refs_9_ = f32[8,128]{1,0:T(8,128)S(1)} collective-permute-done((f32[8,128]{1,0:T(8,128)S(1)}, f32[8,128]{1,0:T(8,128)S(1)}, u32[]{:S(2)}, u32[]{:S(2)}) %collective-permute-start.10) | collective-permute-done | bytes 4128 | tf_op jit(solution)/shard_map/ppermute | solution.py:565
  32.7 0.0 collective-permute-done.9.refs_6_
  32.7 0.8 %shard_map.24 = f32[8,16,256]{2,1,0:T(8,128)} custom-call(f32[8,16,256]{2,1,0:T(8,128)S(1)} %get-tuple-element.40.refs_0_, f32[2,8,16,256]{3,2,1,0:T(8,128)S(1)} %get-tuple-element.41.refs_1_, f32[3,256,128]{2,1,0:T(8,128)S(1)} %get-tuple-element.42.refs_2_, f32[3,15,8,256]{3,2,1,0:T(8,128)S(1)} %get-tuple-element.36.refs_2_.refs_3_, ...), custom_call_target="tpu_custom_call" | custom-call | tf_op jit(solution)/shard_map/pallas_call | solution.py:605
  (2 shorter events, 0.1 us)
Async XLA Ops:
  0.0 0.9 %copy-start = (f32[8,16,256]{2,1,0:T(8,128)S(1)}, f32[8,16,256]{2,1,0:T(8,128)}, u32[]{:S(2)}) copy-start(f32[8,16,256]{2,1,0:T(8,128)} %volume.1) | copy-start | bytes 393220
  0.9 5.9 %collective-permute-start = (f32[6,16,256]{2,1,0:T(8,128)S(1)}, f32[6,16,256]{2,1,0:T(8,128)S(1)}, u32[]{:S(2)}, u32[]{:S(2)}) collective-permute-start(f32[6,16,256]{2,1,0:T(8,128)S(1)} %get-tuple-element.27), channel_id=1, source_target_pairs={{0,1},{1,0},{2,3},{3,2},{4,5},{5,4},{6,7},{7,6},{8,9},{9,8},{10,11... | collective-permute-start | bytes 294920 | tf_op jit(solution)/shard_map/ppermute | solution.py:565
  4.1 2.8 %collective-permute-start.1 = (f32[6,16,256]{2,1,0:T(8,128)S(1)}, f32[6,16,256]{2,1,0:T(8,128)S(1)}, u32[]{:S(2)}, u32[]{:S(2)}) collective-permute-start(f32[6,16,256]{2,1,0:T(8,128)S(1)} %get-tuple-element.28), channel_id=1, source_target_pairs={{0,4},{1,2},{2,1},{3,7},{4,0},{5,6},{6,5},{7,3},{8,12},{9,10},{10,... | collective-permute-start | bytes 294920 | tf_op jit(solution)/shard_map/ppermute | solution.py:565
  7.0 4.7 %collective-permute-start.2 = (f32[96,256]{1,0:T(8,128)S(1)}, f32[96,256]{1,0:T(8,128)S(1)}, u32[]{:S(2)}, u32[]{:S(2)}) collective-permute-start(f32[96,256]{1,0:T(8,128)S(1)} %get-tuple-element.30), channel_id=1, source_target_pairs={{0,16},{16,0},{1,17},{17,1},{2,18},{18,2},{3,19},{19,3},{4,20},{20... | collective-permute-start | bytes 294920 | tf_op jit(solution)/shard_map/ppermute | solution.py:565
  11.8 5.9 %collective-permute-start.3 = (f32[8,384]{1,0:T(8,128)S(1)}, f32[8,384]{1,0:T(8,128)S(1)}, u32[]{:S(2)}, u32[]{:S(2)}) collective-permute-start(f32[8,384]{1,0:T(8,128)S(1)} %shard_map.19), channel_id=1, source_target_pairs={{0,4},{4,0},{8,12},{12,8},{1,5},{5,1},{9,13},{13,9},{2,6},{6,2},{1... | collective-permute-start | bytes 36872 | tf_op jit(solution)/shard_map/ppermute | solution.py:565
  11.9 5.8 %collective-permute-start.4 = (f32[8,256]{1,0:T(8,128)S(1)}, f32[8,256]{1,0:T(8,128)S(1)}, u32[]{:S(2)}, u32[]{:S(2)}) collective-permute-start(f32[8,256]{1,0:T(8,128)S(1)} %get-tuple-element.32), channel_id=1, source_target_pairs={{0,12},{4,8},{8,4},{12,0},{1,13},{5,9},{9,5},{13,1},{2,14},{6,10},... | collective-permute-start | bytes 24584 | tf_op jit(solution)/shard_map/ppermute | solution.py:565
  13.7 3.9 %collective-permute-start.5 = (f32[8,128]{1,0:T(8,128)S(1)}, f32[8,128]{1,0:T(8,128)S(1)}, u32[]{:S(2)}, u32[]{:S(2)}) collective-permute-start(f32[8,128]{1,0:T(8,128)S(1)} %get-tuple-element.33), channel_id=1, source_target_pairs={{0,28},{4,24},{8,20},{12,16},{16,12},{20,8},{24,4},{28,0},{1,29},{... | collective-permute-start | bytes 12296 | tf_op jit(solution)/shard_map/ppermute | solution.py:565
  18.8 5.5 %collective-permute-start.7 = (f32[5,16,256]{2,1,0:T(8,128)S(1)}, f32[5,16,256]{2,1,0:T(8,128)S(1)}, u32[]{:S(2)}, u32[]{:S(2)}) collective-permute-start(f32[5,16,256]{2,1,0:T(8,128)S(1)} %get-tuple-element.43.refs_0_.refs_4_), channel_id=1, source_target_pairs={{0,1},{1,0},{2,3},{3,2},{4,5},{5,4},{6,7},{7,6},{8,9},{9,8},{10,11... | collective-permute-start | bytes 245768 | tf_op jit(solution)/shard_map/ppermute | solution.py:565
  23.0 1.2 %collective-permute-start.8 = (f32[8,128]{1,0:T(8,128)S(1)}, f32[8,128]{1,0:T(8,128)S(1)}, u32[]{:S(2)}, u32[]{:S(2)}) collective-permute-start(f32[8,128]{1,0:T(8,128)S(1)} %get-tuple-element.44.refs_2_.refs_7_), channel_id=1, source_target_pairs={{0,4},{4,0},{8,12},{12,8},{1,5},{5,1},{9,13},{13,9},{2,6},{6,2},{1... | collective-permute-start | bytes 12296 | tf_op jit(solution)/shard_map/ppermute | solution.py:565
  24.3 8.4 %collective-permute-start.9 = (f32[2,16,256]{2,1,0:T(8,128)S(1)}, f32[2,16,256]{2,1,0:T(8,128)S(1)}, u32[]{:S(2)}, u32[]{:S(2)}) collective-permute-start(f32[2,16,256]{2,1,0:T(8,128)S(1)} %get-tuple-element.45), channel_id=1, source_target_pairs={{0,2},{1,3},{2,0},{3,1},{4,6},{5,7},{6,4},{7,5},{8,10},{9,11},{10,... | collective-permute-start | bytes 98312 | tf_op jit(solution)/shard_map/ppermute | solution.py:565
  27.6 3.7 %collective-permute-start.6 = (f32[2,8,256]{2,1,0:T(8,128)S(1)}, f32[2,8,256]{2,1,0:T(8,128)S(1)}, u32[]{:S(2)}, u32[]{:S(2)}) collective-permute-start(f32[2,8,256]{2,1,0:T(8,128)S(1)} %get-tuple-element.39.refs_5_), channel_id=1, source_target_pairs={{0,16},{16,0},{1,17},{17,1},{2,18},{18,2},{3,19},{19,3},{4,20},{20... | collective-permute-start | bytes 49160 | tf_op jit(solution)/shard_map/ppermute | solution.py:565
  29.1 3.6 %collective-permute-start.10 = (f32[8,128]{1,0:T(8,128)S(1)}, f32[8,128]{1,0:T(8,128)S(1)}, u32[]{:S(2)}, u32[]{:S(2)}) collective-permute-start(f32[8,128]{1,0:T(8,128)S(1)} %get-tuple-element.46), channel_id=1, source_target_pairs={{0,8},{4,12},{8,0},{12,4},{1,9},{5,13},{9,1},{13,5},{2,10},{6,14},... | collective-permute-start | bytes 12296 | tf_op jit(solution)/shard_map/ppermute | solution.py:565

commit v7 on v6

--- a/solution.py
+++ b/solution.py
@@ -268,6 +268,17 @@
     return [1.0 / (1.0 + value) for value in lane_blur(k, along_x, wanted)]
 
 
+def finish_rows(t1, every, rows_b, first, nz, count, wanted):
+    k = taps()
+    windows = [[t1[t, pl.ds(first + 2 + o, nz, stride=rows_b), :] for o in range(4)] for t in every]
+    for x in range(count):
+        for t in every:
+            windows[t].append(t1[t, pl.ds(first + 6 + x, nz, stride=rows_b), :])
+        yield x, [1.0 / (1.0 + value) for value in lane_blur(k, [five(k, *window) for window in windows], wanted)]
+        for window in windows:
+            window.pop(0)
+
+
 def main_kernel(dims, counts, pairs, *refs):
     nz, nx, ny = dims
     nt = ny // lanes
@@ -349,36 +360,38 @@
     nz, nx, ny = dims
     nt = ny // lanes
     own, every = tuple(range(nt)), tuple(range(nt + 1))
-    v, bb, fx, fy, cy_out, send_x, send_y, t1, dxs, vs, cxs, cys, ct, vt = refs
+    v, bb, fx, fy, cy_out, send_x, send_y, t1, t2, vs, vx, cxs, cys, ct, vt = refs
     at_x, at_y = lax.axis_index("gx"), lax.axis_index("gy")
     rows_b = nx + 8
     masks, z_mask = grid_masks(dims, counts)
     kt = taps(0.25 / (contrast * contrast))
-    blank = jnp.zeros((edge, lanes), jnp.float32)
-    for t in every:
-        for z in range(nz):
-            t1[t, z, rows_b:, :] = blank
 
     def square_x(t, z):
         slope = bb[t, z + 4, edge + 1:edge + 1 + rows_b, :] - bb[t, z + 4, edge - 1:edge - 1 + rows_b, :]
         return z_mask(z, slope * slope * masks[t])
 
-    tensor(t1, every, rows_b, square_x, nz)
-    for z in range(nz):
-        here = finish(t1, every, z, rows_b, own)
-        for t in own:
-            dxs[t, z * rows_b:(z + 1) * rows_b, :] = here[t]
+    for t in every:
+        window = [square_x(t, z) for z in range(-2, 2)]
+        for i in range(nz):
+            window.append(square_x(t, i + 2))
+            t1[t, i * rows_b:(i + 1) * rows_b, :] = five(kt, *window)
+            window.pop(0)
+    for t in own:
+        for z in range(nz):
             vs[t, z * nx:(z + 1) * nx, :] = v[z, :, cut(t)]
-    for t in own:
-        here = dxs[t, pl.ds(0, nz, stride=rows_b), :]
         for x in range(nx):
-            following = dxs[t, pl.ds(x + 1, nz, stride=rows_b), :]
+            value = vs[t, pl.ds(x, nz, stride=nx), :]
+            vx[t, x * nz:(x + 1) * nz, :] = value
+            cxs[1, x, :, cut(t)] = value
+    before = None
+    for x, here in finish_rows(t1, every, rows_b, 0, nz, nx + 1, own):
+        if before is not None:
             scale = 0.5 * stiffness
-            if x == nx - 1:
+            if x == nx:
                 scale = jnp.where(at_x < counts[1] - 1, scale, 0.0)
-            cxs[0, x, :, cut(t)] = (here + following) * scale
-            cxs[1, x, :, cut(t)] = vs[t, pl.ds(x, nz, stride=nx), :]
-            here = following
+            for t in own:
+                cxs[0, x - 1, :, cut(t)] = (before[t] + here[t]) * scale
+        before = here
 
     def keep_x(i, w, d, h):
         fx[0, i], fx[1, i], fx[2, i] = w, d, h
@@ -400,16 +413,15 @@
     for z in range(nz):
         window.append(square_y_layer(z + 2))
         for t in every:
-            t1[t, z, 0:rows_b, :] = five(kt, *[layer[t] for layer in window])
+            t2[t, z * rows_b:(z + 1) * rows_b, :] = five(kt, *[tiles[t] for tiles in window])
         window.pop(0)
-    for z in range(nz):
-        here = finish(t1, every, z, nx, every)
+    for x, here in finish_rows(t2, every, rows_b, 0, nz, nx, every):
         following = lane_shift(here, 1, own)
         for t in own:
-            cys[t, z * nx:(z + 1) * nx, :] = (here[t] + following[t]) * (0.5 * stiffness)
+            cys[t, x * nz:(x + 1) * nz, :] = (here[t] + following[t]) * (0.5 * stiffness)
     for t in own:
-        ct[t * lanes:(t + 1) * lanes, :] = cys[t].T
-        vt[t * lanes:(t + 1) * lanes, :] = vs[t].T
+        ct[cut(t), :] = cys[t].T
+        vt[cut(t), :] = vx[t].T
     closing = jnp.where(at_y < counts[2] - 1, 1.0, 0.0)
     ct[ny - 1:ny, :] = ct[ny - 1:ny, :] * closing
 
@@ -546,7 +558,7 @@
         total = base[z] + by_z[0, z] * left + by_z[1, z] * right
         rows = slice(z * nx, (z + 1) * nx)
         for t in range(nt):
-            value = total[:, cut(t)] + st[t, rows, :]
+            value = total[:, cut(t)] + st[t, pl.ds(z, nx, stride=nz), :]
             if 1 in groups:
                 value = value + sx[t, rows, :] * (1.0 / 3.0)
             out[z, :, cut(t)] = value
@@ -636,8 +648,8 @@
         functools.partial(side_kernel, dims, counts),
         [f32(3, nx - 1, nz, ny), f32(3, steps - 1, 2, 8, lanes), f32(4, 3, 8, lanes),
          f32(send_shape(depths[1]), nz, ny), f32(8, lanes)],
-        [scratch(nt + 1, nz, rows_b + 8, lanes), scratch(nt, nz * rows_b, lanes), scratch(nt, lanes, lanes),
-         scratch(2, nx, nz, ny), scratch(nt, lanes, lanes), scratch(ny, lanes), scratch(ny, lanes)],
+        [scratch(nt + 1, nz * rows_b, lanes)] * 2 + [scratch(nt, lanes, lanes)] * 2
+        + [scratch(2, nx, nz, ny), scratch(nt, lanes, lanes), scratch(ny, lanes), scratch(ny, lanes)],
         volume, bb)
 
     groups = [[send_z], [send_x], [send_y]]

time: 33.6 us -> 33.6 us (level)
  transfers between devices with their start and end apart: 11 -> 11, of which waited for: 6 -> 7; matrix products, arithmetic and copies ran while one was open for 0% -> 0% of each run, Pallas kernels for 6% -> 5%
where the time goes in v7:
time: 33.6 us; the launch traced here: 33.5 us
  starting transfers between devices  16.1 us (48%)
  waiting for transfers between devices  12.5 us (37%)
  Pallas kernels  3.96 us (12%)
  local copies, waits for them, and re-layouts  0.9 us (3%)
    ppermute x11, starting transfers between devices, permute(): return lax.ppermute(value, axes if len(axes) > 1 else axes[0], moves)  16.1 us
    ppermute x11, waiting for transfers between devices, permute(): return lax.ppermute(value, axes if len(axes) > 1 else axes[0], moves)  12.5 us
    pallas_call x8, Pallas kernels, call(): pl.pallas_call(kernel, out_shape=out_shape, in_specs=[VMEM] * len(args),...  3.96 us
    unnamed x2, local copies, waits for them, and re-layouts  0.9 us
  transfers between devices with their start and end apart: 11, of which 7 were waited for; matrix products, arithmetic and copies ran while one was open for 0% of the time, Pallas kernels for 5%

profile of v7, /device:TPU:0, one launch (start us, length us, event | category | flops | bytes accessed | tf_op | source)
XLA Modules:
  0.0 33.5 jit_solution(788570912573981126)
XLA Ops:
  0.0 0.0 copy-start
  0.0 0.9 %copy-done = f32[8,16,256]{2,1,0:T(8,128)S(1)} copy-done((f32[8,16,256]{2,1,0:T(8,128)S(1)}, f32[8,16,256]{2,1,0:T(8,128)}, u32[]{:S(2)}) %copy-start) | copy-done | bytes 131096
  0.9 3.1 %collective-permute-start = (f32[6,16,256]{2,1,0:T(8,128)S(1)}, f32[6,16,256]{2,1,0:T(8,128)S(1)}, u32[]{:S(2)}, u32[]{:S(2)}) collective-permute-start(f32[6,16,256]{2,1,0:T(8,128)S(1)} %get-tuple-element.27), channel_id=1, source_target_pairs={{0,1},{1,0},{2,3},{3,2},{4,5},{5,4},{6,7},{7,6},{8,9},{9,8},{10,11... | collective-permute-start | bytes 294920 | tf_op jit(solution)/shard_map/ppermute | solution.py:577
  4.1 0.0 collective-permute-start.1
  4.1 2.8 %collective-permute-done.refs_1_ = f32[6,16,256]{2,1,0:T(8,128)S(1)} collective-permute-done((f32[6,16,256]{2,1,0:T(8,128)S(1)}, f32[6,16,256]{2,1,0:T(8,128)S(1)}, u32[]{:S(2)}, u32[]{:S(2)}) %collective-permute-start) | collective-permute-done | bytes 98336 | tf_op jit(solution)/shard_map/ppermute | solution.py:577
  6.8 0.0 collective-permute-done.1.refs_2_
  6.9 0.2 shard_map.18
  7.0 1.8 %collective-permute-start.2 = (f32[96,256]{1,0:T(8,128)S(1)}, f32[96,256]{1,0:T(8,128)S(1)}, u32[]{:S(2)}, u32[]{:S(2)}) collective-permute-start(f32[96,256]{1,0:T(8,128)S(1)} %get-tuple-element.30), channel_id=1, source_target_pairs={{0,16},{16,0},{1,17},{17,1},{2,18},{18,2},{3,19},{19,3},{4,20},{20... | collective-permute-start | bytes 294920 | tf_op jit(solution)/shard_map/ppermute | solution.py:577
  8.8 2.9 %collective-permute-done.2.refs_1_.refs_2_ = f32[96,256]{1,0:T(8,128)S(1)} collective-permute-done((f32[96,256]{1,0:T(8,128)S(1)}, f32[96,256]{1,0:T(8,128)S(1)}, u32[]{:S(2)}, u32[]{:S(2)}) %collective-permute-start.2) | collective-permute-done | bytes 98336 | tf_op jit(solution)/shard_map/ppermute | solution.py:577
  11.7 0.1 shard_map.19
  11.8 0.1 collective-permute-start.3
  11.9 1.9 %collective-permute-start.4 = (f32[8,256]{1,0:T(8,128)S(1)}, f32[8,256]{1,0:T(8,128)S(1)}, u32[]{:S(2)}, u32[]{:S(2)}) collective-permute-start(f32[8,256]{1,0:T(8,128)S(1)} %get-tuple-element.32), channel_id=1, source_target_pairs={{0,12},{4,8},{8,4},{12,0},{1,13},{5,9},{9,5},{13,1},{2,14},{6,10},... | collective-permute-start | bytes 24584 | tf_op jit(solution)/shard_map/ppermute | solution.py:577
  13.7 1.1 %collective-permute-start.5 = (f32[8,128]{1,0:T(8,128)S(1)}, f32[8,128]{1,0:T(8,128)S(1)}, u32[]{:S(2)}, u32[]{:S(2)}) collective-permute-start(f32[8,128]{1,0:T(8,128)S(1)} %get-tuple-element.33), channel_id=1, source_target_pairs={{0,28},{4,24},{8,20},{12,16},{16,12},{20,8},{24,4},{28,0},{1,29},{... | collective-permute-start | bytes 12296 | tf_op jit(solution)/shard_map/ppermute | solution.py:577
  14.9 2.8 %collective-permute-done.5.refs_5_ = f32[8,128]{1,0:T(8,128)S(1)} collective-permute-done((f32[8,128]{1,0:T(8,128)S(1)}, f32[8,128]{1,0:T(8,128)S(1)}, u32[]{:S(2)}, u32[]{:S(2)}) %collective-permute-start.5) | collective-permute-done | bytes 4128 | tf_op jit(solution)/shard_map/ppermute | solution.py:577
  17.7 0.0 collective-permute-done.4.refs_4_
  17.7 0.0 collective-permute-done.3.refs_3_
  17.7 1.1 %shard_map.20 = (f32[3,16,40,128]{3,2,1,0:T(8,128)S(1)}, f32[3,7,16,256]{3,2,1,0:T(8,128)S(1)}, f32[5,16,256]{2,1,0:T(8,128)S(1)}) custom-call(f32[8,16,256]{2,1,0:T(8,128)S(1)} %get-tuple-element.26.refs_0_, f32[2,16,16,128]{3,2,1,0:T(8,128)S(1)} %get-tuple-element.29.refs_1_, f32[96,256]{1,0:T(8,128)S(1)} %collective-permute-done.2.refs_1_.refs_2_, ...), custom_call_target="tpu_custom_call" | custom-call | tf_op jit(solution)/shard_map/pallas_call | solution.py:617
  18.8 2.8 %collective-permute-start.7 = (f32[5,16,256]{2,1,0:T(8,128)S(1)}, f32[5,16,256]{2,1,0:T(8,128)S(1)}, u32[]{:S(2)}, u32[]{:S(2)}) collective-permute-start(f32[5,16,256]{2,1,0:T(8,128)S(1)} %get-tuple-element.43.refs_0_.refs_4_), channel_id=1, source_target_pairs={{0,1},{1,0},{2,3},{3,2},{4,5},{5,4},{6,7},{7,6},{8,9},{9,8},{10,11... | collective-permute-start | bytes 245768 | tf_op jit(solution)/shard_map/ppermute | solution.py:577
  21.5 1.3 %shard_map.21 = (f32[3,15,8,256]{3,2,1,0:T(8,128)S(1)}, f32[3,15,2,8,128]{4,3,2,1,0:T(8,128)S(1)}, f32[4,3,8,128]{3,2,1,0:T(8,128)S(1)}, f32[2,8,256]{2,1,0:T(8,128)S(1)}, f32[8,128]{1,0:T(8,128)S(1)}) custom-call(f32[8,16,256]{2,1,0:T(8,128)S(1)} %get-tuple-element.26.refs_0_, f32[3,16,40,128]{3,2,1,0:T(8,128)S(1)} %get-tuple-element.35.refs_1_), custom_call_target="tpu_custom_call" | custom-call | tf_op jit(solution)/shard_map/pallas_call | solution.py:617
  22.8 0.1 collective-permute-start.8
  22.9 1.2 %collective-permute-done.8.refs_3_.refs_8_ = f32[8,128]{1,0:T(8,128)S(1)} collective-permute-done((f32[8,128]{1,0:T(8,128)S(1)}, f32[8,128]{1,0:T(8,128)S(1)}, u32[]{:S(2)}, u32[]{:S(2)}) %collective-permute-start.8) | collective-permute-done | bytes 4128 | tf_op jit(solution)/shard_map/ppermute | solution.py:577
  24.0 0.2 collective-permute-done.7.refs_1_.refs_5_
  24.3 3.3 %collective-permute-start.9 = (f32[2,16,256]{2,1,0:T(8,128)S(1)}, f32[2,16,256]{2,1,0:T(8,128)S(1)}, u32[]{:S(2)}, u32[]{:S(2)}) collective-permute-start(f32[2,16,256]{2,1,0:T(8,128)S(1)} %get-tuple-element.45), channel_id=1, source_target_pairs={{0,2},{1,3},{2,0},{3,1},{4,6},{5,7},{6,4},{7,5},{8,10},{9,11},{10,... | collective-permute-start | bytes 98312 | tf_op jit(solution)/shard_map/ppermute | solution.py:577
  27.6 1.5 %collective-permute-start.6 = (f32[2,8,256]{2,1,0:T(8,128)S(1)}, f32[2,8,256]{2,1,0:T(8,128)S(1)}, u32[]{:S(2)}, u32[]{:S(2)}) collective-permute-start(f32[2,8,256]{2,1,0:T(8,128)S(1)} %get-tuple-element.39.refs_5_), channel_id=1, source_target_pairs={{0,16},{16,0},{1,17},{17,1},{2,18},{18,2},{3,19},{19,3},{4,20},{20... | collective-permute-start | bytes 49160 | tf_op jit(solution)/shard_map/ppermute | solution.py:577
  29.1 0.5 %collective-permute-start.10 = (f32[8,128]{1,0:T(8,128)S(1)}, f32[8,128]{1,0:T(8,128)S(1)}, u32[]{:S(2)}, u32[]{:S(2)}) collective-permute-start(f32[8,128]{1,0:T(8,128)S(1)} %get-tuple-element.46), channel_id=1, source_target_pairs={{0,8},{4,12},{8,0},{12,4},{1,9},{5,13},{9,1},{13,5},{2,10},{6,14},... | collective-permute-start | bytes 12296 | tf_op jit(solution)/shard_map/ppermute | solution.py:577
  29.6 1.7 %collective-permute-done.6.refs_6_ = f32[2,8,256]{2,1,0:T(8,128)S(1)} collective-permute-done((f32[2,8,256]{2,1,0:T(8,128)S(1)}, f32[2,8,256]{2,1,0:T(8,128)S(1)}, u32[]{:S(2)}, u32[]{:S(2)}) %collective-permute-start.6) | collective-permute-done | bytes 16416 | tf_op jit(solution)/shard_map/ppermute | solution.py:577
  31.3 0.5 %shard_map.22 = (f32[8,16,256]{2,1,0:T(8,128)S(1)}, f32[2,8,16,256]{3,2,1,0:T(8,128)S(1)}, f32[3,256,128]{2,1,0:T(8,128)S(1)}) custom-call(f32[8,16,256]{2,1,0:T(8,128)S(1)} %get-tuple-element.26.refs_0_, f32[3,7,16,256]{3,2,1,0:T(8,128)S(1)} %get-tuple-element.34.refs_1_, f32[3,15,8,256]{3,2,1,0:T(8,128)S(1)} %get-tuple-element.36.refs_2_.refs_3_, ...), custom_call_target="tpu_custom_call" | custom-call | tf_op jit(solution)/shard_map/pallas_call | solution.py:617
  31.8 0.9 %collective-permute-done.10.refs_9_ = f32[8,128]{1,0:T(8,128)S(1)} collective-permute-done((f32[8,128]{1,0:T(8,128)S(1)}, f32[8,128]{1,0:T(8,128)S(1)}, u32[]{:S(2)}, u32[]{:S(2)}) %collective-permute-start.10) | collective-permute-done | bytes 4128 | tf_op jit(solution)/shard_map/ppermute | solution.py:577
  32.7 0.0 collective-permute-done.9.refs_6_
  32.7 0.8 %shard_map.24 = f32[8,16,256]{2,1,0:T(8,128)} custom-call(f32[8,16,256]{2,1,0:T(8,128)S(1)} %get-tuple-element.40.refs_0_, f32[2,8,16,256]{3,2,1,0:T(8,128)S(1)} %get-tuple-element.41.refs_1_, f32[3,256,128]{2,1,0:T(8,128)S(1)} %get-tuple-element.42.refs_2_, f32[3,15,8,256]{3,2,1,0:T(8,128)S(1)} %get-tuple-element.36.refs_2_.refs_3_, ...), custom_call_target="tpu_custom_call" | custom-call | tf_op jit(solution)/shard_map/pallas_call | solution.py:617
  (2 shorter events, 0.1 us)
Async XLA Ops:
  0.0 0.9 %copy-start = (f32[8,16,256]{2,1,0:T(8,128)S(1)}, f32[8,16,256]{2,1,0:T(8,128)}, u32[]{:S(2)}) copy-start(f32[8,16,256]{2,1,0:T(8,128)} %volume.1) | copy-start | bytes 393220
  0.9 5.9 %collective-permute-start = (f32[6,16,256]{2,1,0:T(8,128)S(1)}, f32[6,16,256]{2,1,0:T(8,128)S(1)}, u32[]{:S(2)}, u32[]{:S(2)}) collective-permute-start(f32[6,16,256]{2,1,0:T(8,128)S(1)} %get-tuple-element.27), channel_id=1, source_target_pairs={{0,1},{1,0},{2,3},{3,2},{4,5},{5,4},{6,7},{7,6},{8,9},{9,8},{10,11... | collective-permute-start | bytes 294920 | tf_op jit(solution)/shard_map/ppermute | solution.py:577
  4.1 2.8 %collective-permute-start.1 = (f32[6,16,256]{2,1,0:T(8,128)S(1)}, f32[6,16,256]{2,1,0:T(8,128)S(1)}, u32[]{:S(2)}, u32[]{:S(2)}) collective-permute-start(f32[6,16,256]{2,1,0:T(8,128)S(1)} %get-tuple-element.28), channel_id=1, source_target_pairs={{0,4},{1,2},{2,1},{3,7},{4,0},{5,6},{6,5},{7,3},{8,12},{9,10},{10,... | collective-permute-start | bytes 294920 | tf_op jit(solution)/shard_map/ppermute | solution.py:577
  7.0 4.7 %collective-permute-start.2 = (f32[96,256]{1,0:T(8,128)S(1)}, f32[96,256]{1,0:T(8,128)S(1)}, u32[]{:S(2)}, u32[]{:S(2)}) collective-permute-start(f32[96,256]{1,0:T(8,128)S(1)} %get-tuple-element.30), channel_id=1, source_target_pairs={{0,16},{16,0},{1,17},{17,1},{2,18},{18,2},{3,19},{19,3},{4,20},{20... | collective-permute-start | bytes 294920 | tf_op jit(solution)/shard_map/ppermute | solution.py:577
  11.8 5.9 %collective-permute-start.3 = (f32[8,384]{1,0:T(8,128)S(1)}, f32[8,384]{1,0:T(8,128)S(1)}, u32[]{:S(2)}, u32[]{:S(2)}) collective-permute-start(f32[8,384]{1,0:T(8,128)S(1)} %shard_map.19), channel_id=1, source_target_pairs={{0,4},{4,0},{8,12},{12,8},{1,5},{5,1},{9,13},{13,9},{2,6},{6,2},{1... | collective-permute-start | bytes 36872 | tf_op jit(solution)/shard_map/ppermute | solution.py:577
  11.9 5.8 %collective-permute-start.4 = (f32[8,256]{1,0:T(8,128)S(1)}, f32[8,256]{1,0:T(8,128)S(1)}, u32[]{:S(2)}, u32[]{:S(2)}) collective-permute-start(f32[8,256]{1,0:T(8,128)S(1)} %get-tuple-element.32), channel_id=1, source_target_pairs={{0,12},{4,8},{8,4},{12,0},{1,13},{5,9},{9,5},{13,1},{2,14},{6,10},... | collective-permute-start | bytes 24584 | tf_op jit(solution)/shard_map/ppermute | solution.py:577
  13.7 3.9 %collective-permute-start.5 = (f32[8,128]{1,0:T(8,128)S(1)}, f32[8,128]{1,0:T(8,128)S(1)}, u32[]{:S(2)}, u32[]{:S(2)}) collective-permute-start(f32[8,128]{1,0:T(8,128)S(1)} %get-tuple-element.33), channel_id=1, source_target_pairs={{0,28},{4,24},{8,20},{12,16},{16,12},{20,8},{24,4},{28,0},{1,29},{... | collective-permute-start | bytes 12296 | tf_op jit(solution)/shard_map/ppermute | solution.py:577
  18.8 5.5 %collective-permute-start.7 = (f32[5,16,256]{2,1,0:T(8,128)S(1)}, f32[5,16,256]{2,1,0:T(8,128)S(1)}, u32[]{:S(2)}, u32[]{:S(2)}) collective-permute-start(f32[5,16,256]{2,1,0:T(8,128)S(1)} %get-tuple-element.43.refs_0_.refs_4_), channel_id=1, source_target_pairs={{0,1},{1,0},{2,3},{3,2},{4,5},{5,4},{6,7},{7,6},{8,9},{9,8},{10,11... | collective-permute-start | bytes 245768 | tf_op jit(solution)/shard_map/ppermute | solution.py:577
  22.8 1.2 %collective-permute-start.8 = (f32[8,128]{1,0:T(8,128)S(1)}, f32[8,128]{1,0:T(8,128)S(1)}, u32[]{:S(2)}, u32[]{:S(2)}) collective-permute-start(f32[8,128]{1,0:T(8,128)S(1)} %get-tuple-element.44.refs_2_.refs_7_), channel_id=1, source_target_pairs={{0,4},{4,0},{8,12},{12,8},{1,5},{5,1},{9,13},{13,9},{2,6},{6,2},{1... | collective-permute-start | bytes 12296 | tf_op jit(solution)/shard_map/ppermute | solution.py:577
  24.3 8.4 %collective-permute-start.9 = (f32[2,16,256]{2,1,0:T(8,128)S(1)}, f32[2,16,256]{2,1,0:T(8,128)S(1)}, u32[]{:S(2)}, u32[]{:S(2)}) collective-permute-start(f32[2,16,256]{2,1,0:T(8,128)S(1)} %get-tuple-element.45), channel_id=1, source_target_pairs={{0,2},{1,3},{2,0},{3,1},{4,6},{5,7},{6,4},{7,5},{8,10},{9,11},{10,... | collective-permute-start | bytes 98312 | tf_op jit(solution)/shard_map/ppermute | solution.py:577
  27.6 3.7 %collective-permute-start.6 = (f32[2,8,256]{2,1,0:T(8,128)S(1)}, f32[2,8,256]{2,1,0:T(8,128)S(1)}, u32[]{:S(2)}, u32[]{:S(2)}) collective-permute-start(f32[2,8,256]{2,1,0:T(8,128)S(1)} %get-tuple-element.39.refs_5_), channel_id=1, source_target_pairs={{0,16},{16,0},{1,17},{17,1},{2,18},{18,2},{3,19},{19,3},{4,20},{20... | collective-permute-start | bytes 49160 | tf_op jit(solution)/shard_map/ppermute | solution.py:577
  29.1 3.6 %collective-permute-start.10 = (f32[8,128]{1,0:T(8,128)S(1)}, f32[8,128]{1,0:T(8,128)S(1)}, u32[]{:S(2)}, u32[]{:S(2)}) collective-permute-start(f32[8,128]{1,0:T(8,128)S(1)} %get-tuple-element.46), channel_id=1, source_target_pairs={{0,8},{4,12},{8,0},{12,4},{1,9},{5,13},{9,1},{13,5},{2,10},{6,14},... | collective-permute-start | bytes 12296 | tf_op jit(solution)/shard_map/ppermute | solution.py:577

commit v8 on v7

--- a/solution.py
+++ b/solution.py
@@ -161,16 +161,9 @@
     return jnp.where(odd, first, second), jnp.where(odd, second, first)
 
 
-def open_kernel(dims, volume, kept, *sends):
-    nz = dims[0]
-    odd = lax.axis_index("gz") % 2 == 1
-    for z in range(nz):
+def open_kernel(dims, volume, kept):
+    for z in range(dims[0]):
         kept[z] = volume[z]
-    for z in range(halo):
-        low, high = volume[z], volume[nz - halo + z]
-        sends[0][z] = jnp.where(odd, low, high)
-        if len(sends) > 1:
-            sends[1][z] = jnp.where(odd, high, low)
 
 
 def z_kernel(dims, counts, pairs, *refs):
@@ -185,7 +178,7 @@
     odd_y = lax.axis_index("gy") % 2 == 1
     for t in range(nt):
         cols = cut(t)
-        below = [neighbours(at_z, counts[0], zr, lambda ref: ref[z, :, cols])[0] for z in range(halo)]
+        below = [neighbours(at_z, counts[0], zr, lambda ref: ref[nz - halo + z, :, cols])[0] for z in range(halo)]
         above = [neighbours(at_z, counts[0], zr, lambda ref: ref[z, :, cols])[1] for z in range(halo)]
 
         def load(z):
@@ -582,7 +575,11 @@
 
 
 def swap_pair(value, axis, start):
-    partner = partners(lax.axis_size(axis), start)
+    n = lax.axis_size(axis)
+    partner = partners(n, start)
+    if axis == "gy" and start == 1:
+        move = lambda y, z: (partner[y], z) if 0 < y < n - 1 else (y, z ^ 1)
+        return permute(value, ("gy", "gz"), move)
     return permute(value, (axis,), lambda i: (partner[i],))
 
 
@@ -596,7 +593,7 @@
 
 def swap_corner(value, x_start, y_start):
     of_x, of_y = partners(lax.axis_size("gx"), x_start), partners(lax.axis_size("gy"), y_start)
-    return permute(value, ("gx", "gy"), lambda x, y: (of_x[x], of_y[y]))
+    return permute(value, ("gx", "gy"), lambda x, y: (of_x[x], of_y[y] if 0 < y < len(of_y) - 1 else y))
 
 
 def body(volume):
@@ -620,9 +617,8 @@
             compiler_params=pltpu.CompilerParams(vmem_limit_bytes=16 * 2**20),
         )(*args)
 
-    volume, *z_sends = call(
-        functools.partial(open_kernel, dims), [f32(*dims)] + [f32(halo, nx, ny)] * pairs[0], [], volume)
-    z_received = [swap_z(value, e) for e, value in enumerate(z_sends)]
+    z_received = [swap_z(volume, e) for e in range(pairs[0])]
+    volume, = call(functools.partial(open_kernel, dims), [f32(*dims)], [], volume)
     ex, ey = range(pairs[1]), range(pairs[2])
     far = ex if pairs[2] > 1 else []
     blurred_z, *sends = call(

time: 33.6 us -> 31.7 us (0.943)
  waiting for transfers between devices: 12.5 us -> 10.5 us
    ppermute x11, waiting for transfers between devices: 12.5 us -> 10.5 us  [permute(): return lax.ppermute(value, axes if len(axes) > 1 else axes[0], moves)]
  transfers between devices with their start and end apart: 11 -> 11, of which waited for: 7 -> 7; matrix products, arithmetic and copies ran while one was open for 0% -> 0% of each run, Pallas kernels for 5% -> 6%
where the time goes in v8:
time: 31.7 us; the launch traced here: 31.6 us
  starting transfers between devices  16.1 us (51%)
  waiting for transfers between devices  10.5 us (33%)
  Pallas kernels  3.91 us (12%)
  local copies, waits for them, and re-layouts  0.93 us (3%)
    ppermute x11, starting transfers between devices, permute(): return lax.ppermute(value, axes if len(axes) > 1 else axes[0], moves)  16.1 us
    ppermute x11, waiting for transfers between devices, permute(): return lax.ppermute(value, axes if len(axes) > 1 else axes[0], moves)  10.5 us
    pallas_call x8, Pallas kernels, call(): pl.pallas_call(kernel, out_shape=out_shape, in_specs=[VMEM] * len(args),...  3.91 us
    unnamed x2, local copies, waits for them, and re-layouts  0.93 us
  transfers between devices with their start and end apart: 11, of which 7 were waited for; matrix products, arithmetic and copies ran while one was open for 0% of the time, Pallas kernels for 6%

profile of v8, /device:TPU:0, one launch (start us, length us, event | category | flops | bytes accessed | tf_op | source)
XLA Modules:
  0.0 31.6 jit_solution(603831637550384586)
XLA Ops:
  0.0 3.1 %collective-permute-start = (f32[8,16,256]{2,1,0:T(8,128)}, f32[8,16,256]{2,1,0:T(8,128)S(1)}, u32[]{:S(2)}, u32[]{:S(2)}) collective-permute-start(f32[8,16,256]{2,1,0:T(8,128)} %volume.1), channel_id=1, source_target_pairs={{0,1},{1,0},{2,3},{3,2},{4,5},{5,4},{6,7},{7,6},{8,9},{9,8},{10,11... | collective-permute-start | bytes 393224 | tf_op jit(solution)/shard_map/ppermute | solution.py:570
  3.1 0.0 collective-permute-start.1
  3.1 0.0 copy-start
  3.1 0.9 %copy-done = f32[8,16,256]{2,1,0:T(8,128)S(1)} copy-done((f32[8,16,256]{2,1,0:T(8,128)S(1)}, f32[8,16,256]{2,1,0:T(8,128)}, u32[]{:S(2)}) %copy-start) | copy-done | bytes 131096
  4.0 2.8 %collective-permute-done.refs_1_ = f32[8,16,256]{2,1,0:T(8,128)S(1)} collective-permute-done((f32[8,16,256]{2,1,0:T(8,128)}, f32[8,16,256]{2,1,0:T(8,128)S(1)}, u32[]{:S(2)}, u32[]{:S(2)}) %collective-permute-start) | collective-permute-done | bytes 131104 | tf_op jit(solution)/shard_map/ppermute | solution.py:570
  6.8 0.0 collective-permute-done.1.refs_2_
  6.8 0.2 shard_map.18
  6.9 1.7 %collective-permute-start.2 = (f32[96,256]{1,0:T(8,128)S(1)}, f32[96,256]{1,0:T(8,128)S(1)}, u32[]{:S(2)}, u32[]{:S(2)}) collective-permute-start(f32[96,256]{1,0:T(8,128)S(1)} %get-tuple-element.24), channel_id=1, source_target_pairs={{0,16},{16,0},{1,17},{17,1},{2,18},{18,2},{3,19},{19,3},{4,20},{20... | collective-permute-start | bytes 294920 | tf_op jit(solution)/shard_map/ppermute | solution.py:570
  8.7 3.0 %collective-permute-done.2.refs_1_.refs_2_ = f32[96,256]{1,0:T(8,128)S(1)} collective-permute-done((f32[96,256]{1,0:T(8,128)S(1)}, f32[96,256]{1,0:T(8,128)S(1)}, u32[]{:S(2)}, u32[]{:S(2)}) %collective-permute-start.2) | collective-permute-done | bytes 98336 | tf_op jit(solution)/shard_map/ppermute | solution.py:570
  11.6 0.1 shard_map.19
  11.7 0.1 collective-permute-start.3
  11.8 3.0 %collective-permute-start.4 = (f32[8,256]{1,0:T(8,128)S(1)}, f32[8,256]{1,0:T(8,128)S(1)}, u32[]{:S(2)}, u32[]{:S(2)}) collective-permute-start(f32[8,256]{1,0:T(8,128)S(1)} %get-tuple-element.26), channel_id=1, source_target_pairs={{0,1},{1,0},{2,3},{3,2},{4,8},{5,9},{6,10},{7,11},{8,4},{9,5},{10,... | collective-permute-start | bytes 24584 | tf_op jit(solution)/shard_map/ppermute | solution.py:570
  14.8 1.5 %collective-permute-start.5 = (f32[8,128]{1,0:T(8,128)S(1)}, f32[8,128]{1,0:T(8,128)S(1)}, u32[]{:S(2)}, u32[]{:S(2)}) collective-permute-start(f32[8,128]{1,0:T(8,128)S(1)} %get-tuple-element.27), channel_id=1, source_target_pairs={{0,16},{4,24},{8,20},{12,28},{16,0},{20,8},{24,4},{28,12},{1,17},{... | collective-permute-start | bytes 12296 | tf_op jit(solution)/shard_map/ppermute | solution.py:570
  16.2 2.1 %collective-permute-done.5.refs_5_ = f32[8,128]{1,0:T(8,128)S(1)} collective-permute-done((f32[8,128]{1,0:T(8,128)S(1)}, f32[8,128]{1,0:T(8,128)S(1)}, u32[]{:S(2)}, u32[]{:S(2)}) %collective-permute-start.5) | collective-permute-done | bytes 4128 | tf_op jit(solution)/shard_map/ppermute | solution.py:570
  18.4 0.0 collective-permute-done.4.refs_4_
  18.4 0.0 collective-permute-done.3.refs_3_
  18.4 1.1 %shard_map.20 = (f32[3,16,40,128]{3,2,1,0:T(8,128)S(1)}, f32[3,7,16,256]{3,2,1,0:T(8,128)S(1)}, f32[5,16,256]{2,1,0:T(8,128)S(1)}) custom-call(f32[8,16,256]{2,1,0:T(8,128)S(1)} %shard_map.17.refs_0_, f32[2,16,16,128]{3,2,1,0:T(8,128)S(1)} %get-tuple-element.23.refs_1_, f32[96,256]{1,0:T(8,128)S(1)} %collective-permute-done.2.refs_1_.refs_2_, ...), custom_call_target="tpu_custom_call" | custom-call | tf_op jit(solution)/shard_map/pallas_call | solution.py:614
  19.4 0.1 collective-permute-start.7
  19.6 1.3 %shard_map.21 = (f32[3,15,8,256]{3,2,1,0:T(8,128)S(1)}, f32[3,15,2,8,128]{4,3,2,1,0:T(8,128)S(1)}, f32[4,3,8,128]{3,2,1,0:T(8,128)S(1)}, f32[2,8,256]{2,1,0:T(8,128)S(1)}, f32[8,128]{1,0:T(8,128)S(1)}) custom-call(f32[8,16,256]{2,1,0:T(8,128)S(1)} %shard_map.17.refs_0_, f32[3,16,40,128]{3,2,1,0:T(8,128)S(1)} %get-tuple-element.29.refs_1_), custom_call_target="tpu_custom_call" | custom-call | tf_op jit(solution)/shard_map/pallas_call | solution.py:614
  20.8 1.7 %collective-permute-start.8 = (f32[8,128]{1,0:T(8,128)S(1)}, f32[8,128]{1,0:T(8,128)S(1)}, u32[]{:S(2)}, u32[]{:S(2)}) collective-permute-start(f32[8,128]{1,0:T(8,128)S(1)} %get-tuple-element.38.refs_2_.refs_7_), channel_id=1, source_target_pairs={{0,4},{4,0},{8,12},{12,8},{1,5},{5,1},{9,13},{13,9},{2,6},{6,2},{1... | collective-permute-start | bytes 12296 | tf_op jit(solution)/shard_map/ppermute | solution.py:570
  22.5 0.8 %collective-permute-done.8.refs_3_.refs_8_ = f32[8,128]{1,0:T(8,128)S(1)} collective-permute-done((f32[8,128]{1,0:T(8,128)S(1)}, f32[8,128]{1,0:T(8,128)S(1)}, u32[]{:S(2)}, u32[]{:S(2)}) %collective-permute-start.8) | collective-permute-done | bytes 4128 | tf_op jit(solution)/shard_map/ppermute | solution.py:570
  23.3 0.7 %collective-permute-done.7.refs_1_.refs_5_ = f32[5,16,256]{2,1,0:T(8,128)S(1)} collective-permute-done((f32[5,16,256]{2,1,0:T(8,128)S(1)}, f32[5,16,256]{2,1,0:T(8,128)S(1)}, u32[]{:S(2)}, u32[]{:S(2)}) %collective-permute-start.7) | collective-permute-done | bytes 81952 | tf_op jit(solution)/shard_map/ppermute | solution.py:570
  24.1 1.5 %collective-permute-start.9 = (f32[2,16,256]{2,1,0:T(8,128)S(1)}, f32[2,16,256]{2,1,0:T(8,128)S(1)}, u32[]{:S(2)}, u32[]{:S(2)}) collective-permute-start(f32[2,16,256]{2,1,0:T(8,128)S(1)} %get-tuple-element.39), channel_id=1, source_target_pairs={{0,2},{1,3},{2,0},{3,1},{4,6},{5,7},{6,4},{7,5},{8,10},{9,11},{10,... | collective-permute-start | bytes 98312 | tf_op jit(solution)/shard_map/ppermute | solution.py:570
  25.6 1.5 %collective-permute-start.6 = (f32[2,8,256]{2,1,0:T(8,128)S(1)}, f32[2,8,256]{2,1,0:T(8,128)S(1)}, u32[]{:S(2)}, u32[]{:S(2)}) collective-permute-start(f32[2,8,256]{2,1,0:T(8,128)S(1)} %get-tuple-element.33.refs_5_), channel_id=1, source_target_pairs={{0,16},{16,0},{1,17},{17,1},{2,18},{18,2},{3,19},{19,3},{4,20},{20... | collective-permute-start | bytes 49160 | tf_op jit(solution)/shard_map/ppermute | solution.py:570
  27.1 2.0 %collective-permute-start.10 = (f32[8,128]{1,0:T(8,128)S(1)}, f32[8,128]{1,0:T(8,128)S(1)}, u32[]{:S(2)}, u32[]{:S(2)}) collective-permute-start(f32[8,128]{1,0:T(8,128)S(1)} %get-tuple-element.40), channel_id=1, source_target_pairs={{0,8},{4,12},{8,0},{12,4},{1,9},{5,13},{9,1},{13,5},{2,10},{6,14},... | collective-permute-start | bytes 12296 | tf_op jit(solution)/shard_map/ppermute | solution.py:570
  29.1 0.3 collective-permute-done.6.refs_6_
  29.4 0.5 %shard_map.22 = (f32[8,16,256]{2,1,0:T(8,128)S(1)}, f32[2,8,16,256]{3,2,1,0:T(8,128)S(1)}, f32[3,256,128]{2,1,0:T(8,128)S(1)}) custom-call(f32[8,16,256]{2,1,0:T(8,128)S(1)} %shard_map.17.refs_0_, f32[3,7,16,256]{3,2,1,0:T(8,128)S(1)} %get-tuple-element.28.refs_1_, f32[3,15,8,256]{3,2,1,0:T(8,128)S(1)} %get-tuple-element.30.refs_2_.refs_3_, ...), custom_call_target="tpu_custom_call" | custom-call | tf_op jit(solution)/shard_map/pallas_call | solution.py:614
  29.9 0.9 %collective-permute-done.10.refs_9_ = f32[8,128]{1,0:T(8,128)S(1)} collective-permute-done((f32[8,128]{1,0:T(8,128)S(1)}, f32[8,128]{1,0:T(8,128)S(1)}, u32[]{:S(2)}, u32[]{:S(2)}) %collective-permute-start.10) | collective-permute-done | bytes 4128 | tf_op jit(solution)/shard_map/ppermute | solution.py:570
  30.7 0.0 collective-permute-done.9.refs_6_
  30.7 0.8 %shard_map.24 = f32[8,16,256]{2,1,0:T(8,128)} custom-call(f32[8,16,256]{2,1,0:T(8,128)S(1)} %get-tuple-element.34.refs_0_, f32[2,8,16,256]{3,2,1,0:T(8,128)S(1)} %get-tuple-element.35.refs_1_, f32[3,256,128]{2,1,0:T(8,128)S(1)} %get-tuple-element.36.refs_2_, f32[3,15,8,256]{3,2,1,0:T(8,128)S(1)} %get-tuple-element.30.refs_2_.refs_3_, ...), custom_call_target="tpu_custom_call" | custom-call | tf_op jit(solution)/shard_map/pallas_call | solution.py:614
  (2 shorter events, 0.1 us)
Async XLA Ops:
  0.0 6.8 %collective-permute-start = (f32[8,16,256]{2,1,0:T(8,128)}, f32[8,16,256]{2,1,0:T(8,128)S(1)}, u32[]{:S(2)}, u32[]{:S(2)}) collective-permute-start(f32[8,16,256]{2,1,0:T(8,128)} %volume.1), channel_id=1, source_target_pairs={{0,1},{1,0},{2,3},{3,2},{4,5},{5,4},{6,7},{7,6},{8,9},{9,8},{10,11... | collective-permute-start | bytes 393224 | tf_op jit(solution)/shard_map/ppermute | solution.py:570
  3.1 3.7 %collective-permute-start.1 = (f32[8,16,256]{2,1,0:T(8,128)}, f32[8,16,256]{2,1,0:T(8,128)S(1)}, u32[]{:S(2)}, u32[]{:S(2)}) collective-permute-start(f32[8,16,256]{2,1,0:T(8,128)} %volume.1), channel_id=1, source_target_pairs={{0,4},{1,2},{2,1},{3,7},{4,0},{5,6},{6,5},{7,3},{8,12},{9,10},{10,... | collective-permute-start | bytes 393224 | tf_op jit(solution)/shard_map/ppermute | solution.py:570
  3.1 0.9 %copy-start = (f32[8,16,256]{2,1,0:T(8,128)S(1)}, f32[8,16,256]{2,1,0:T(8,128)}, u32[]{:S(2)}) copy-start(f32[8,16,256]{2,1,0:T(8,128)} %volume.1) | copy-start | bytes 393220
  6.9 4.7 %collective-permute-start.2 = (f32[96,256]{1,0:T(8,128)S(1)}, f32[96,256]{1,0:T(8,128)S(1)}, u32[]{:S(2)}, u32[]{:S(2)}) collective-permute-start(f32[96,256]{1,0:T(8,128)S(1)} %get-tuple-element.24), channel_id=1, source_target_pairs={{0,16},{16,0},{1,17},{17,1},{2,18},{18,2},{3,19},{19,3},{4,20},{20... | collective-permute-start | bytes 294920 | tf_op jit(solution)/shard_map/ppermute | solution.py:570
  11.7 6.7 %collective-permute-start.3 = (f32[8,384]{1,0:T(8,128)S(1)}, f32[8,384]{1,0:T(8,128)S(1)}, u32[]{:S(2)}, u32[]{:S(2)}) collective-permute-start(f32[8,384]{1,0:T(8,128)S(1)} %shard_map.19), channel_id=1, source_target_pairs={{0,4},{4,0},{8,12},{12,8},{1,5},{5,1},{9,13},{13,9},{2,6},{6,2},{1... | collective-permute-start | bytes 36872 | tf_op jit(solution)/shard_map/ppermute | solution.py:570
  11.8 6.6 %collective-permute-start.4 = (f32[8,256]{1,0:T(8,128)S(1)}, f32[8,256]{1,0:T(8,128)S(1)}, u32[]{:S(2)}, u32[]{:S(2)}) collective-permute-start(f32[8,256]{1,0:T(8,128)S(1)} %get-tuple-element.26), channel_id=1, source_target_pairs={{0,1},{1,0},{2,3},{3,2},{4,8},{5,9},{6,10},{7,11},{8,4},{9,5},{10,... | collective-permute-start | bytes 24584 | tf_op jit(solution)/shard_map/ppermute | solution.py:570
  14.8 3.6 %collective-permute-start.5 = (f32[8,128]{1,0:T(8,128)S(1)}, f32[8,128]{1,0:T(8,128)S(1)}, u32[]{:S(2)}, u32[]{:S(2)}) collective-permute-start(f32[8,128]{1,0:T(8,128)S(1)} %get-tuple-element.27), channel_id=1, source_target_pairs={{0,16},{4,24},{8,20},{12,28},{16,0},{20,8},{24,4},{28,12},{1,17},{... | collective-permute-start | bytes 12296 | tf_op jit(solution)/shard_map/ppermute | solution.py:570
  19.4 4.6 %collective-permute-start.7 = (f32[5,16,256]{2,1,0:T(8,128)S(1)}, f32[5,16,256]{2,1,0:T(8,128)S(1)}, u32[]{:S(2)}, u32[]{:S(2)}) collective-permute-start(f32[5,16,256]{2,1,0:T(8,128)S(1)} %get-tuple-element.37.refs_0_.refs_4_), channel_id=1, source_target_pairs={{0,1},{1,0},{2,3},{3,2},{4,5},{5,4},{6,7},{7,6},{8,9},{9,8},{10,11... | collective-permute-start | bytes 245768 | tf_op jit(solution)/shard_map/ppermute | solution.py:570
  20.8 2.5 %collective-permute-start.8 = (f32[8,128]{1,0:T(8,128)S(1)}, f32[8,128]{1,0:T(8,128)S(1)}, u32[]{:S(2)}, u32[]{:S(2)}) collective-permute-start(f32[8,128]{1,0:T(8,128)S(1)} %get-tuple-element.38.refs_2_.refs_7_), channel_id=1, source_target_pairs={{0,4},{4,0},{8,12},{12,8},{1,5},{5,1},{9,13},{13,9},{2,6},{6,2},{1... | collective-permute-start | bytes 12296 | tf_op jit(solution)/shard_map/ppermute | solution.py:570
  24.1 6.6 %collective-permute-start.9 = (f32[2,16,256]{2,1,0:T(8,128)S(1)}, f32[2,16,256]{2,1,0:T(8,128)S(1)}, u32[]{:S(2)}, u32[]{:S(2)}) collective-permute-start(f32[2,16,256]{2,1,0:T(8,128)S(1)} %get-tuple-element.39), channel_id=1, source_target_pairs={{0,2},{1,3},{2,0},{3,1},{4,6},{5,7},{6,4},{7,5},{8,10},{9,11},{10,... | collective-permute-start | bytes 98312 | tf_op jit(solution)/shard_map/ppermute | solution.py:570
  25.6 3.7 %collective-permute-start.6 = (f32[2,8,256]{2,1,0:T(8,128)S(1)}, f32[2,8,256]{2,1,0:T(8,128)S(1)}, u32[]{:S(2)}, u32[]{:S(2)}) collective-permute-start(f32[2,8,256]{2,1,0:T(8,128)S(1)} %get-tuple-element.33.refs_5_), channel_id=1, source_target_pairs={{0,16},{16,0},{1,17},{17,1},{2,18},{18,2},{3,19},{19,3},{4,20},{20... | collective-permute-start | bytes 49160 | tf_op jit(solution)/shard_map/ppermute | solution.py:570
  27.1 3.6 %collective-permute-start.10 = (f32[8,128]{1,0:T(8,128)S(1)}, f32[8,128]{1,0:T(8,128)S(1)}, u32[]{:S(2)}, u32[]{:S(2)}) collective-permute-start(f32[8,128]{1,0:T(8,128)S(1)} %get-tuple-element.40), channel_id=1, source_target_pairs={{0,8},{4,12},{8,0},{12,4},{1,9},{5,13},{9,1},{13,5},{2,10},{6,14},... | collective-permute-start | bytes 12296 | tf_op jit(solution)/shard_map/ppermute | solution.py:570
